TPU v7x, 32 devices: a whole 2x2x4 slice. The times are simulated.
32 devices in a mesh: dom: 2 (over x), tok: 16 (over z, y, core).
Axes of the slice: x: 2, y: 2, z: 4, core: 2. Of those that a mesh axis runs over, the one named last changes fastest.
Arguments:
- tokens: bfloat16 [512, 4096], P(('dom', 'tok')), parts along dimension 0, may hold values from -6 to 6
- rotation_flip: int32 [4096], replicated, may hold values from 0 to 1
- gate_up: bfloat16 [4, 4096, 16384], P('dom', None, 'tok'), parts along dimension 0, may hold values from -0.09375 to 0.09375
- quant_codes: bfloat16 [4, 4096, 16384], P('dom', None, 'tok'), parts along dimension 0, may hold values from -7 to 7
- quant_exps: int32 [4, 32, 16384], P('dom', None, 'tok'), parts along dimension 0, may hold values from -10 to -7
- down_rows: bfloat16 [32768, 4096], P(('dom', 'tok')), parts along dimension 0, may hold values from -0.046875 to 0.046875
Outputs:
- correction: bfloat16 [32768, 4096], P(('dom', 'tok')), parts along dimension 0
There are 2 independent parts, one for each index of `dom`. A program takes and returns all parts, laid end to end along the dimension named above; an argument that names none is the same for every part. Nothing has to cross between parts.
All inputs are finite; a program needn't handle non-finite values.
Results may differ from a plain program's by a relative error of at most 0.012.
Values may be sent and summed in bfloat16 or wider, within the bound.
No kernel may reach another device: no remote copies, remote signals or barrier semaphores. Data moves between devices by JAX's collectives and lax.ppermute only.
A program may use at most 128 MiB of HBM per device.

v0:
```python
import jax
import jax.numpy as jnp
from jax import lax
from jax.sharding import PartitionSpec as P


def hadamard_table(order):
    index = jnp.arange(order, dtype=jnp.int32)
    common = index[:, None] & index[None, :]
    parity = jnp.zeros((order, order), jnp.int32)
    for bit_pos in range(max(order.bit_length() - 1, 1)):
        parity = parity ^ common >> bit_pos & 1
    return (1 - 2 * parity).astype(jnp.float32)


def rotate(inputs, flip):
    width = inputs.shape[-1]
    signed = inputs.astype(jnp.float32) * (1 - 2 * flip).astype(jnp.float32)
    power = width.bit_length() - 1
    outer_len = 2 ** (power // 2)
    inner_len = width // outer_len
    blocks = signed.reshape(-1, outer_len, inner_len)
    mixed = jnp.einsum(
        "ab,nbc,cd->nad",
        hadamard_table(outer_len),
        blocks,
        hadamard_table(inner_len),
        precision=lax.Precision.HIGHEST,
    )
    return (mixed.reshape(-1, width) * (1.0 / width**0.5)).astype(jnp.bfloat16)


def dequant(codes, exps):
    groups = exps.shape[1]
    scales = jnp.exp2(exps.astype(jnp.float32))
    shaped = codes.astype(jnp.float32).reshape(2, groups, codes.shape[1] // groups, codes.shape[2])
    return (shaped * scales[:, :, None, :]).reshape(codes.shape).astype(jnp.bfloat16)


def swiglu(inputs, weights):
    gate = jnp.dot(inputs, weights[0], preferred_element_type=jnp.float32)
    upper = jnp.dot(inputs, weights[1], preferred_element_type=jnp.float32)
    return (jax.nn.silu(gate) * upper).astype(jnp.bfloat16)


def per_device(tokens, rotation_flip, gate_up, quant_codes, quant_exps, down_rows):
    quant_weight = dequant(quant_codes, quant_exps)
    piece = lax.all_gather(tokens, "tok", axis=0, tiled=True)
    hid_full = swiglu(piece, gate_up)
    hid_quant = swiglu(rotate(piece, rotation_flip), quant_weight)
    mismatch = (hid_full.astype(jnp.float32) - hid_quant.astype(jnp.float32)).astype(jnp.bfloat16)
    total_tokens = mismatch.shape[0]
    partial_proj = jnp.dot(mismatch, down_rows, preferred_element_type=jnp.float32)
    projected = lax.psum(partial_proj, "tok").astype(jnp.bfloat16)
    gram = lax.dot_general(
        hid_quant, projected, (((0,), (0,)), ((), ())), preferred_element_type=jnp.float32
    )
    return (gram * (1.0 / total_tokens**0.5)).astype(jnp.bfloat16)


def solution(mesh):
    placed = (
        P(("dom", "tok"), None),
        P(),
        P("dom", None, "tok"),
        P("dom", None, "tok"),
        P("dom", None, "tok"),
        P(("dom", "tok"), None),
    )
    return jax.shard_map(
        per_device, mesh=mesh, in_specs=placed, out_specs=P(("dom", "tok"), None), check_vma=False
    )
```

profile of v0, /device:TPU:1, one launch (start us, length us, event | category | flops | bytes accessed | tf_op | source)
XLA Modules:
  0.0 203.8 jit_solution(15538142856855820026)
XLA Ops:
  6.5 0.0 all-gather.2.cloned.1.call-start
  6.5 0.7 all-gather.2.cloned.1.call-update
  7.3 1.0 multiply_exponential_fusion
  8.3 0.0 copy-start.2
  8.3 14.8 %fusion = bf16[2,4096,1024]{2,1,0:T(8,128)(2,1)} fusion(bf16[2,4096,1024]{2,1,0:T(8,128)(2,1)} %param.9, f32[2,32,1024]{2,1,0:T(8,128)S(1)} %multiply_exponential_fusion), kind=kLoop, calls=%fused_computation.1 | loop fusion | flops 25165824 | bytes 33816576 | tf_op jit(solution)/shard_map/convert_element_type | solution.py:37
  23.1 0.0 copy-done.2
  23.1 30.4 %all-gather.2.cloned.1.call-done = bf16[256,4096]{1,0:T(8,128)(2,1)} async-done(((bf16[16,4096]{1,0:T(8,128)(2,1)}), bf16[256,4096]{1,0:T(8,128)(2,1)}) %all-gather.2.cloned.1.call-update) | async-done | bytes 2097168 | tf_op jit(solution)/shard_map/all_gather | solution.py:48
  53.4 3.3 %copy.8 = bf16[256,4096]{0,1:T(8,128)(2,1)S(1)} copy(bf16[256,4096]{1,0:T(8,128)(2,1)} %all-gather.2.cloned.1.call-done) | data formatting | bytes 4194304 | tf_op jit(solution)/shard_map/all_gather | solution.py:48
  56.7 0.0 copy-start
  56.7 0.7 convert_multiply_fusion
  57.5 6.8 %fusion.11 = f32[256,64,64]{0,2,1:T(8,128)S(1)} fusion(f32[256,64,64]{0,2,1:T(8,128)S(1)} %bitcast.47), kind=kOutput, calls=%fused_computation.15 | convolution fusion | flops 805392384 | bytes 8388608 | tf_op jit(solution)/shard_map/ab,nbc,cd->nad/dot_general | solution.py:23
  64.2 6.0 %multiply_convert_fusion.1 = bf16[256,64,64]{0,2,1:T(8,128)(2,1)S(1)} fusion(f32[256,64,64]{0,2,1:T(8,128)S(1)} %fusion.11), kind=kOutput, calls=%fused_computation.17 | convolution fusion | flops 807489536 | bytes 6291456 | tf_op jit(solution)/shard_map/ab,nbc,cd->nad/dot_general | solution.py:23
  70.3 0.0 copy-done
  70.3 2.4 %fusion.2 = f32[256,1024]{1,0:T(8,128)S(1)} fusion(bf16[256,4096]{0,1:T(8,128)(2,1)S(1)} %bitcast.48, bf16[2,4096,1024]{2,1,0:T(8,128)(2,1)S(1)} %copy-done), kind=kOutput, calls=%fused_computation.6 | convolution fusion | flops 2147483648 | bytes 11534336 | tf_op jit(solution)/shard_map/dot_general | solution.py:41
  72.6 0.0 copy-start.1
  72.6 2.4 %fusion.20 = bf16[256,1024]{1,0:T(8,128)(2,1)S(1)} fusion(bf16[256,4096]{0,1:T(8,128)(2,1)S(1)} %bitcast.49, bf16[2,4096,1024]{2,1,0:T(8,128)(2,1)S(1)} %copy-done, f32[256,1024]{1,0:T(8,128)S(1)} %fusion.2), kind=kOutput, calls=%fused_computation.22 | convolution fusion | flops 2149056512 | bytes 12058624 | tf_op jit(solution)/shard_map/dot_general | solution.py:42
  75.1 0.0 copy-done.1
  75.1 6.7 %fusion.5 = f32[256,1024]{1,0:T(8,128)} fusion(bf16[256,4096]{1,0:T(8,128)(2,1)S(1)} %copy-done.1, bf16[2,4096,1024]{2,1,0:T(8,128)(2,1)} %param.8), kind=kOutput, calls=%fused_computation.9 | convolution fusion | flops 2147483648 | bytes 11534336 | tf_op jit(solution)/shard_map/dot_general | solution.py:41
  81.8 12.7 %fusion.34 = f32[256,4096]{1,0:T(8,128)} fusion(bf16[1024,4096]{1,0:T(8,128)(2,1)} %param.11, bf16[256,4096]{1,0:T(8,128)(2,1)S(1)} %copy-done.1, bf16[2,4096,1024]{2,1,0:T(8,128)(2,1)} %param.8, bf16[256,1024]{1,0:T(8,128)(2,1)S(1)} %fusion.20, f32[256,1024]{1,0:T(8,128)} %fusion.5), kind=kOutput, calls=%fused_computation.27 | convolution fusion | flops 4297588736 | bytes 24641536 | tf_op jit(solution)/shard_map/dot_general | solution.py:53
  94.5 96.6 %all-reduce.1 = bf16[256,4096]{1,0:T(8,128)(2,1)S(1)} all-reduce(f32[256,4096]{1,0:T(8,128)} %fusion.34), channel_id=1, replica_groups=mesh['dom'=2,'tok'=16] {'tok'}, use_global_device_ids=true, to_apply=%region_0.1 | all-reduce | flops 1048576 | bytes 6291456 | tf_op jit(solution)/shard_map/psum | solution.py:54
  191.1 5.8 %multiply_convert_fusion = bf16[1024,4096]{1,0:T(8,128)(2,1)} fusion(bf16[256,1024]{1,0:T(8,128)(2,1)S(1)} %fusion.20, bf16[256,4096]{1,0:T(8,128)(2,1)S(1)} %all-reduce.1), kind=kOutput, calls=%fused_computation.2 | convolution fusion | flops 2155872256 | bytes 11010048 | tf_op jit(solution)/shard_map/dot_general | solution.py:55
  (1 shorter events, 0.0 us)
Async XLA Ops:
  6.5 46.9 %all-gather.2.cloned.1.call-start = ((), (), s32[]{:S(2)}) async-start(), calls=%async_computation | async-start | bytes 2228224 | tf_op jit(solution)/shard_map/all_gather | solution.py:48
  8.3 14.8 %copy-start.2 = (s32[4096]{0:T(1024)S(1)}, s32[4096]{0:T(1024)}, u32[]{:S(2)}) copy-start(s32[4096]{0:T(1024)} %param.7) | copy-start | bytes 49156
  56.7 13.6 %copy-start = (bf16[2,4096,1024]{2,1,0:T(8,128)(2,1)S(1)}, bf16[2,4096,1024]{2,1,0:T(8,128)(2,1)}, u32[]{:S(2)}) copy-start(bf16[2,4096,1024]{2,1,0:T(8,128)(2,1)} %fusion) | copy-start | bytes 50331652
  72.6 2.5 %copy-start.1 = (bf16[256,4096]{1,0:T(8,128)(2,1)S(1)}, bf16[256,4096]{1,0:T(8,128)(2,1)}, u32[]{:S(2)}) copy-start(bf16[256,4096]{1,0:T(8,128)(2,1)} %all-gather.2.cloned.1.call-done) | copy-start | bytes 6291460
Sparse Core Ops, SparseCore 0:
  9.5 43.9 all-gather.1
where the time goes:
time: 204 us
  blocking collectives  96.6 us (47%)
  matrix products  42.8 us (21%)
  waiting for transfers between devices  31.1 us (15%)
  other arithmetic  16.5 us (8%)
  between operations  13.5 us (7%)
  local copies, waits for them, and re-layouts  3.28 us (2%)
    psum x1, blocking collectives, per_device(): projected = lax.psum(partial_proj, 'tok').astype(jnp.bfloat16)  96.6 us
    all_gather x1, waiting for transfers between devices, per_device(): piece = lax.all_gather(tokens, 'tok', axis=0, tiled=True)  30.4 us
    convert_element_type x1, other arithmetic, dequant(): (shaped * scales[:, :, None, :]).reshape(codes.shape).astype(jnp.bfloat16)  14.8 us
    dot_general x2, matrix products, rotate(): jnp.einsum('ab,nbc,cd->nad', hadamard_table(outer_len), blocks, hadamard_...  12.8 us
    dot_general x1, matrix products, per_device(): jnp.dot(mismatch, down_rows, preferred_element_type=jnp.float32)  12.7 us
    dot_general x2, matrix products, swiglu(): gate = jnp.dot(inputs, weights[0], preferred_element_type=jnp.float32)  9.03 us
    dot_general x1, matrix products, per_device(): lax.dot_general(hid_quant, projected, (((0,), (0,)), ((), ())), preferred...  5.79 us
  transfers between devices with their start and end apart: 1, of which 1 were waited for; matrix products, arithmetic and copies ran while one was open for 8% of the time, Pallas kernels for 0%

commit v1 on v0

v1 whole, which is shorter than its diff:
```python
import functools
import math

import jax
import jax.numpy as jnp
from jax import lax
from jax.experimental import pallas as pl
from jax.experimental.pallas import tpu as pltpu
from jax.sharding import PartitionSpec as P


F32 = jnp.float32
BF16 = jnp.bfloat16


def hadamard_table(order):
    index = jnp.arange(order, dtype=jnp.int32)
    common = index[:, None] & index[None, :]
    parity = jnp.zeros((order, order), jnp.int32)
    for bit_pos in range(max(order.bit_length() - 1, 1)):
        parity = parity ^ common >> bit_pos & 1
    return (1 - 2 * parity).astype(F32)


def spec(space):
    return pl.BlockSpec(memory_space=space)


def params(mib):
    return pltpu.CompilerParams(vmem_limit_bytes=mib << 20)


def shaped(dims, dtype):
    return jax.ShapeDtypeStruct(tuple(dims), dtype)


def rotate_rows(x_ref, sign, table, o_ref, step):
    rows, width = x_ref.shape
    inner = table.shape[0]

    @pl.loop(0, rows // step)
    def _(block):
        cut = pl.ds(pl.multiple_of(block * step, step), step)
        parts = [
            jnp.dot(
                x_ref[cut, k : k + inner] * sign[:, k : k + inner], table, preferred_element_type=F32
            )
            for k in range(0, width, inner)
        ]
        span = 1
        while span < len(parts):
            for k in range(len(parts)):
                if not k & span:
                    a, b = parts[k], parts[k + span]
                    parts[k], parts[k + span] = a + b, a - b
            span *= 2
        for k, part in enumerate(parts):
            o_ref[cut, k * inner : (k + 1) * inner] = (part * (1.0 / width**0.5)).astype(BF16)


def swiglu(pieces, input_ref, gate_of, upper_of):
    depth = input_ref.shape[1] // pieces
    gate = upper = 0.0
    for k in range(pieces):
        cut = slice(k * depth, (k + 1) * depth)
        inputs = input_ref[:, cut]
        gate = gate + jnp.dot(inputs, gate_of(k, cut), preferred_element_type=F32)
        upper = upper + jnp.dot(inputs, upper_of(k, cut), preferred_element_type=F32)
    return (gate / (1.0 + jnp.exp(-gate)) * upper).astype(BF16)


def hidden_columns(
    block, width, tok_ref, rot_ref, gu_refs, qc_refs, qe_ref, hq_ref, mm_ref, full_first, arrived
):
    depth = tok_ref.shape[1]
    groups = qe_ref.shape[1]
    pieces = math.gcd(groups, 4)
    cut = pl.ds(pl.multiple_of(block * width, width), width)

    def full_weight(i):
        return lambda k, rows: gu_refs[i][rows, cut]

    def quant_weight(i):
        def piece(k, rows):
            exps = qe_ref[i, k * groups // pieces : (k + 1) * groups // pieces, cut]
            scale = jnp.exp2(exps.astype(F32)).astype(BF16)
            columns = cut if qc_refs[i].shape[1] > width else slice(None)
            codes = qc_refs[i][rows, columns].reshape(groups // pieces, depth // groups, width)
            return (codes * scale[:, None, :]).reshape(depth // pieces, width)

        return piece

    if full_first:
        full = swiglu(pieces, tok_ref, full_weight(0), full_weight(1))
        arrived(block)
    quant = swiglu(pieces, rot_ref, quant_weight(0), quant_weight(1))
    if not full_first:
        arrived(block)
        full = swiglu(pieces, tok_ref, full_weight(0), full_weight(1))
    hq_ref[:, cut] = quant
    mm_ref[:, cut] = (full.astype(F32) - quant.astype(F32)).astype(BF16)


def fetch_kernel(_, source, *refs):
    targets, sem = refs[:-1], refs[-1]
    copies = [
        pltpu.make_async_copy(source.at[k], target, sem.at[k]) for k, target in enumerate(targets)
    ]
    for copy in copies:
        copy.start()
    for copy in copies:
        copy.wait()


def fetch(after, weights):
    count = weights.shape[0]
    return pl.pallas_call(
        fetch_kernel,
        in_specs=[spec(pltpu.VMEM), spec(pltpu.HBM)],
        out_specs=[spec(pltpu.VMEM)] * count,
        out_shape=[pltpu.VMEM(weights.shape[1:], weights.dtype)] * count,
        scratch_shapes=[pltpu.SemaphoreType.DMA((count,))],
        compiler_params=params(1),
        cost_estimate=pl.CostEstimate(
            flops=0, transcendentals=0, bytes_accessed=4 * weights.size
        ),
        name="fetch",
    )(after, pltpu.with_memory_space_constraint(weights, pltpu.HBM))


def project(mm_ref, down_ref, keep_ref, send_ref):
    total = jnp.dot(mm_ref[...], down_ref[...], preferred_element_type=F32)
    own = keep_ref.shape[0]
    keep_ref[...] = total[:own]
    send_ref[...] = total[own:].astype(BF16)


def stack(blocks, o_ref):
    rows = blocks[0].shape[0]
    for k, block in enumerate(blocks):
        o_ref[k * rows : (k + 1) * rows, :] = block[...]


def first_kernel(count, *refs):
    blocks, refs = refs[:count], refs[count:]
    flip_ref, table_ref, *qc_refs, qe_ref, gu_hbm = refs[:6]
    hq_ref, mm_ref, *gu_refs = refs[6:10]
    tok_ref, rot_ref, gu_sem = refs[10:]
    units = hq_ref.shape[1]
    step = min(256, units)

    def full(k, block):
        cut = pl.ds(pl.multiple_of(block * step, step), step)
        return pltpu.make_async_copy(
            gu_hbm.at[k, :, cut], gu_refs[k].at[:, cut], gu_sem.at[k, block]
        )

    def full_arrived(block):
        for k in range(2):
            full(k, block).wait()

    for block in range(units // step):
        for k in range(2):
            full(k, block).start()
    stack(blocks, tok_ref)
    sign = (1 - 2 * flip_ref[...]).astype(F32).astype(BF16)
    rotate_rows(tok_ref, sign, table_ref[...], rot_ref, 64)

    @pl.loop(0, units // step)
    def _(block):
        hidden_columns(
            block, step, tok_ref, rot_ref, gu_refs, qc_refs, qe_ref, hq_ref, mm_ref,
            full_first=False, arrived=full_arrived,
        )


def first_hidden(blocks, flip, table, gate_up, codes, exps):
    rows, depth = len(blocks) * blocks[0].shape[0], blocks[0].shape[1]
    units = codes[0].shape[1]
    return pl.pallas_call(
        functools.partial(first_kernel, len(blocks)),
        in_specs=[spec(pltpu.VMEM)] * (len(blocks) + 5) + [spec(pltpu.HBM)],
        out_specs=[spec(pltpu.VMEM)] * 4,
        out_shape=[
            shaped((rows, units), BF16),
            shaped((rows, units), BF16),
            pltpu.VMEM(gate_up.shape[1:], BF16),
            pltpu.VMEM(gate_up.shape[1:], BF16),
        ],
        scratch_shapes=[
            pltpu.VMEM((rows, depth), BF16),
            pltpu.VMEM((rows, depth), BF16),
            pltpu.SemaphoreType.DMA((2, units // min(256, units))),
        ],
        compiler_params=params(4 + (2 * rows * depth >> 19)),
        cost_estimate=pl.CostEstimate(
            flops=8 * rows * depth * units, transcendentals=0, bytes_accessed=2 * gate_up.size
        ),
        name="first_hidden",
    )(
        *blocks, flip, table, *codes, exps,
        pltpu.with_memory_space_constraint(gate_up, pltpu.HBM),
    )


def next_kernel(count, parts, *refs):
    blocks, mms, refs = refs[:count], refs[count : count + parts], refs[count + parts :]
    flip_ref, table_ref, *gu_refs, qe_ref, qc_hbm, down_hbm = refs[:7]
    hq_ref, keep_ref, send_ref = refs[7:10]
    keeps, sends = refs[10 : 10 + parts], refs[10 + parts : 10 + 2 * parts]
    tok_ref, rot_ref, mm_ref, qc_ref, down_ref, qc_sem, down_sem = refs[10 + 2 * parts :]
    units = hq_ref.shape[1]
    step = min(256, units)
    slots = qc_ref.shape[0]

    def codes(block):
        cut = pl.ds(pl.multiple_of(block * step, step), step)
        slot = lax.rem(block, slots)
        return pltpu.make_async_copy(qc_hbm.at[:, :, cut], qc_ref.at[slot], qc_sem.at[slot])

    rest = pltpu.make_async_copy(down_hbm, down_ref, down_sem)
    for block in range(min(slots, units // step)):
        codes(block).start()
    stack(blocks, tok_ref)
    sign = (1 - 2 * flip_ref[...]).astype(F32).astype(BF16)
    rotate_rows(tok_ref, sign, table_ref[...], rot_ref, 64)

    @pl.loop(0, units // step)
    def _(block):
        slot = lax.rem(block, slots)
        hidden_columns(
            block, step, tok_ref, rot_ref, gu_refs, [qc_ref.at[slot, k] for k in range(2)],
            qe_ref, hq_ref, mm_ref, full_first=True, arrived=lambda k: codes(k).wait(),
        )

        @pl.when(block + slots < units // step)
        def _():
            codes(block + slots).start()

        @pl.when(block == max(units // step - slots - 1, 0))
        def _():
            rest.start()

    rest.wait()
    project(mm_ref, down_ref, keep_ref, send_ref)
    for own_ref, kept, sent in zip(mms, keeps, sends):
        project(own_ref, down_ref, kept, sent)


def next_hidden(cores, blocks, mms, flip, table, gate_up, codes, exps, down):
    rows, depth = len(blocks) * blocks[0].shape[0], blocks[0].shape[1]
    units, width = down.shape
    own = rows // cores
    step = min(256, units)
    parts = 1 + len(mms)
    return pl.pallas_call(
        functools.partial(next_kernel, len(blocks), len(mms)),
        in_specs=[spec(pltpu.VMEM)] * (len(blocks) + len(mms) + 5) + [spec(pltpu.HBM)] * 2,
        out_specs=[spec(pltpu.VMEM)] * (1 + 2 * parts),
        out_shape=[
            shaped((rows, units), BF16),
            shaped((own, width), F32),
            shaped((rows - own, width), BF16),
        ]
        + [shaped((own, width), F32)] * len(mms)
        + [shaped((rows - own, width), BF16)] * len(mms),
        scratch_shapes=[
            pltpu.VMEM((rows, depth), BF16),
            pltpu.VMEM((rows, depth), BF16),
            pltpu.VMEM((rows, units), BF16),
            pltpu.VMEM((2, 2, depth, step), BF16),
            pltpu.VMEM(down.shape, BF16),
            pltpu.SemaphoreType.DMA((2,)),
            pltpu.SemaphoreType.DMA(()),
        ],
        compiler_params=params(2 + (2 * rows * depth + 4 * depth * step + down.size >> 19)),
        cost_estimate=pl.CostEstimate(
            flops=10 * rows * depth * units, transcendentals=0, bytes_accessed=2 * codes.size
        ),
        name="next_hidden",
    )(
        *blocks, *mms, flip, table, *gate_up, exps,
        pltpu.with_memory_space_constraint(codes, pltpu.HBM),
        pltpu.with_memory_space_constraint(down, pltpu.HBM),
    )


def last_kernel(mm_ref, down_ref, keep_ref, send_ref):
    project(mm_ref, down_ref, keep_ref, send_ref)


def last_project(cores, mm, down):
    rows, (units, width) = mm.shape[0], down.shape
    own = rows // cores
    return pl.pallas_call(
        last_kernel,
        in_specs=[spec(pltpu.VMEM)] * 2,
        out_specs=[spec(pltpu.VMEM)] * 2,
        out_shape=[shaped((own, width), F32), shaped((rows - own, width), BF16)],
        compiler_params=params(12),
        name="last_project",
    )(mm, down)


def join_kernel(others, keep_ref, *refs):
    received, outs = refs[:others], refs[others:]
    rows = outs[0].shape[0]
    for k, out in enumerate(outs):
        cut = slice(k * rows, (k + 1) * rows)
        total = keep_ref[cut, :]
        for ref in received:
            total = total + ref[cut, :].astype(F32)
        out[...] = total.astype(BF16)


def join(lines, keep, received):
    rows = keep.shape[0] // lines
    block = shaped((rows, keep.shape[1]), BF16)
    return pl.pallas_call(
        functools.partial(join_kernel, len(received)),
        in_specs=[spec(pltpu.VMEM)] * (1 + len(received)),
        out_specs=[spec(pltpu.VMEM)] * lines,
        out_shape=[block] * lines,
        compiler_params=params(4),
        name="join",
    )(keep, *received)


def add_kernel(cut, whole, keep_ref, *refs):
    received, out = refs[:-1], refs[-1]
    total = keep_ref[cut, :]
    for k, ref in enumerate(received):
        total = total + (ref[cut, :] if k < whole else ref[...]).astype(F32)
    out[...] = total.astype(BF16)


def add(rows, line, keep, received, blocks):
    return pl.pallas_call(
        functools.partial(add_kernel, slice(line * rows, (line + 1) * rows), len(received)),
        in_specs=[spec(pltpu.VMEM)] * (1 + len(received) + len(blocks)),
        out_specs=spec(pltpu.VMEM),
        out_shape=shaped((rows, keep.shape[1]), BF16),
        compiler_params=params(4),
        name="add",
    )(keep, *received, *blocks)


def gram_kernel(scale, parts, *refs):
    hqs, blocks = refs[:parts], refs[parts:-3]
    o_ref, hq_ref, proj_ref = refs[-3:]

    @pl.when(pl.program_id(0) == 0)
    def _():
        stack(hqs, hq_ref)
        stack(blocks, proj_ref)

    step = o_ref.shape[0]
    cut = pl.ds(pl.multiple_of(pl.program_id(0) * step, step), step)
    gram = lax.dot_general(
        hq_ref[:, cut], proj_ref[...], (((0,), (0,)), ((), ())), preferred_element_type=F32
    )
    o_ref[...] = (gram * scale).astype(BF16)


def gram(hqs, blocks):
    rows = len(hqs) * hqs[0].shape[0]
    units, out = hqs[0].shape[1], blocks[0].shape[1]
    step = min(128, units)
    return pl.pallas_call(
        functools.partial(gram_kernel, 1.0 / rows**0.5, len(hqs)),
        grid=(units // step,),
        in_specs=[spec(pltpu.VMEM)] * (len(hqs) + len(blocks)),
        out_specs=pl.BlockSpec((step, out), lambda i: (i, 0)),
        out_shape=shaped((units, out), BF16),
        scratch_shapes=[pltpu.VMEM((rows, units), BF16), pltpu.VMEM((rows, out), BF16)],
        compiler_params=params(16),
        name="gram",
    )(*hqs, *blocks)


def grid_of(mesh):
    devices = mesh.devices.reshape(-1, mesh.shape["tok"])[0]
    spots = [tuple(d.coords) for d in devices]
    cores = sum(spot == spots[0] for spot in spots)
    chips = spots[::cores]
    side = next((k for k in range(1, len(chips)) if chips[k][2] != chips[0][2]), len(chips))
    if len(chips) % side:
        side = 1
    return len(chips) // side, side, cores


def shift(grid, axis, by):
    pairs = []
    for line in range(grid[0]):
        for side in range(grid[1]):
            for core in range(grid[2]):
                spot = [line, side, core]
                source = (spot[0] * grid[1] + spot[1]) * grid[2] + spot[2]
                spot[axis] = (spot[axis] + by) % grid[axis]
                pairs.append((source, (spot[0] * grid[1] + spot[1]) * grid[2] + spot[2]))
    return pairs


def far_first(lines):
    return sorted(range(lines), key=lambda s: -min(s, lines - s))


def gather(grid, block):
    send = lambda value, axis, by: lax.ppermute(value, "tok", shift(grid, axis, by))
    order = far_first(grid[0])[::-1]
    blocks = {}
    for line in order:
        blocks[0, 0, line] = send(block, 0, line) if line else block
    for by in range(grid[1]):
        for line in order:
            if by:
                blocks[by, 0, line] = send(blocks[0, 0, line], 1, by)
            for core in range(1, grid[2]):
                blocks[by, core, line] = send(blocks[by, 0, line], 2, core)
    return blocks, blocks[0, 0, order[1]]


def reduce_to_owner(grid, group, kept, sent):
    send = lambda value, axis, by: lax.ppermute(value, "tok", shift(grid, axis, -by))
    size = kept[0, 0].shape[0]
    rows = size // group
    received = {
        key: [send(sent[key][c * size :][:size], 2, c + 1) for c in range(grid[2] - 1)]
        for key in list(kept)[::-1]
    }
    moved = {line: [] for line in range(grid[0])}
    for by in range(grid[1] - 1, 0, -1):
        blocks = []
        for part in range(grid[0] // group):
            blocks += join(group, kept[by, part], received[by, part])
        for line in far_first(grid[0]):
            moved[line].append(send(blocks[line], 1, by))

    def total(line, arrived):
        key = 0, line // group
        return add(rows, line % group, kept[key], received[key], moved[line] + arrived)

    arrived = [send(total(line, []), 0, line) for line in far_first(grid[0])[:-1]]
    return total(0, arrived)


def solution(mesh):
    grid = grid_of(mesh)
    group = math.gcd(grid[0], 4)
    chunks = [(by, part) for by in range(grid[1]) for part in range(grid[0] // group)]

    def chunk_blocks(blocks, chunk):
        by, part = chunk
        lines = range(part * group, (part + 1) * group)
        return [blocks[by, core, line] for core in range(grid[2]) for line in lines]

    def per_device(tokens, rotation_flip, gate_up, quant_codes, quant_exps, down_rows):
        width = tokens.shape[1]
        held = lambda value: pltpu.with_memory_space_constraint(value, pltpu.VMEM)
        flip = rotation_flip.reshape(1, width)
        table = hadamard_table(min(256, width)).astype(BF16)
        blocks, near = gather(grid, tokens)
        codes = [held(value) for value in fetch(near, quant_codes)]
        hq, mm, *gu = first_hidden(
            chunk_blocks(blocks, chunks[0]), flip, table, gate_up, codes, quant_exps
        )
        gu = [held(value) for value in gu]
        hqs, kept, sent = [hq], {chunks[0]: None}, {}
        for chunk in chunks[1:]:
            hq, kept[chunk], sent[chunk], *rest = next_hidden(
                grid[2],
                chunk_blocks(blocks, chunk),
                [mm] if chunk == chunks[-1] else [],
                flip, table, gu, quant_codes, quant_exps, down_rows,
            )
            hqs.append(hq)
        if len(chunks) == 1:
            rest = last_project(grid[2], mm, down_rows)
        kept[chunks[0]], sent[chunks[0]] = rest
        own = reduce_to_owner(grid, group, kept, sent)
        projected, _ = gather(grid, own)
        return gram(hqs, sum((chunk_blocks(projected, chunk) for chunk in chunks), []))

    placed = (
        P(("dom", "tok"), None),
        P(),
        P("dom", None, "tok"),
        P("dom", None, "tok"),
        P("dom", None, "tok"),
        P(("dom", "tok"), None),
    )
    return jax.shard_map(
        per_device, mesh=mesh, in_specs=placed, out_specs=P(("dom", "tok"), None), check_vma=False
    )
```

time: 204 us -> 99.3 us (0.49)
  blocking collectives: 96.6 us -> 0 us
  matrix products: 42.8 us -> 0 us
  starting transfers between devices: 0.01 us -> 39.8 us
  Pallas kernels: 0 us -> 32.8 us
  other arithmetic: 16.5 us -> 0.24 us
  between operations: 13.5 us -> 0.19 us
  waiting for transfers between devices: 31.1 us -> 25.8 us
  local copies, waits for them, and re-layouts: 3.28 us -> 0.02 us
    psum x1 -> x0, blocking collectives: 96.6 us -> none  [per_device(): projected = lax.psum(partial_proj, 'tok').astype(jnp.bfloat16)]
    dot_general x7 -> x0, matrix products: 42.8 us -> none  [the longest x2 12.8 us: rotate(): jnp.einsum('ab,nbc,cd->nad', hadamard_table(outer_len), blocks, hadamard_...]
    ppermute x0 -> x39, starting transfers between devices: none -> 39.8 us  [the longest x30 34 us: gather(): lax.ppermute(value, 'tok', shift(grid, axis, by))]
    pallas_call x0 -> x9, Pallas kernels: none -> 32.8 us  [the longest x1 12.2 us: next_hidden(): pl.pallas_call(functools.partial(next_kernel, len(blocks), len(mms)), in_...]
    all_gather x1 -> x0, waiting for transfers between devices: 30.4 us -> none  [per_device(): piece = lax.all_gather(tokens, 'tok', axis=0, tiled=True)]
    ppermute x0 -> x39, waiting for transfers between devices: none -> 25.8 us  [the longest x9 16.1 us: reduce_to_owner(): lax.ppermute(value, 'tok', shift(grid, axis, -by))]
    convert_element_type x2 -> x1, other arithmetic: 14.8 us -> 0.24 us  [per_device(): table = hadamard_table(min(256, width)).astype(BF16)]
    all_gather x1 -> x0, local copies, waits for them, and re-layouts: 3.27 us -> none  [per_device(): piece = lax.all_gather(tokens, 'tok', axis=0, tiled=True)]
  transfers between devices with their start and end apart: 1 -> 39, of which waited for: 1 -> 14; matrix products, arithmetic and copies ran while one was open for 8% -> 0% of each run, Pallas kernels for 0% -> 14%
where the time goes in v1:
time: 99.3 us; the launch traced here: 98.8 us
  starting transfers between devices  39.8 us (40%)
  Pallas kernels  32.8 us (33%)
  waiting for transfers between devices  25.8 us (26%)
    ppermute x30, starting transfers between devices, gather(): lax.ppermute(value, 'tok', shift(grid, axis, by))  34 us
    ppermute x9, waiting for transfers between devices, reduce_to_owner(): lax.ppermute(value, 'tok', shift(grid, axis, -by))  16.1 us
    pallas_call x1, Pallas kernels, next_hidden(): pl.pallas_call(functools.partial(next_kernel, len(blocks), len(mms)), in_...  12.2 us
    ppermute x30, waiting for transfers between devices, gather(): lax.ppermute(value, 'tok', shift(grid, axis, by))  9.68 us
    pallas_call x1, Pallas kernels, first_hidden(): pl.pallas_call(functools.partial(first_kernel, len(blocks)), in_specs=[sp...  7.99 us
    pallas_call x1, Pallas kernels, gram(): pl.pallas_call(functools.partial(gram_kernel, 1.0 / rows ** 0.5, len(hqs)...  6.47 us
    ppermute x9, starting transfers between devices, reduce_to_owner(): lax.ppermute(value, 'tok', shift(grid, axis, -by))  5.85 us
    pallas_call x1, Pallas kernels, fetch(): pl.pallas_call(fetch_kernel, in_specs=[spec(pltpu.VMEM), spec(pltpu.HBM)]...  5.83 us
  transfers between devices with their start and end apart: 39, of which 14 were waited for; matrix products, arithmetic and copies ran while one was open for 0% of the time, Pallas kernels for 14%

profile of v1, /device:TPU:1, one launch (start us, length us, event | category | flops | bytes accessed | tf_op | source)
XLA Modules:
  0.0 98.8 jit_solution(5257807483636306815)
XLA Ops:
  0.0 4.1 %collective-permute-start.2 = (bf16[16,4096]{1,0:T(8,128)(2,1)}, bf16[16,4096]{1,0:T(8,128)(2,1)S(1)}, u32[]{:S(2)}, u32[]{:S(2)}) collective-permute-start(bf16[16,4096]{1,0:T(8,128)(2,1)} %refs_0_.1), channel_id=1, source_target_pairs={{0,12},{1,13},{2,14},{3,15},{4,0},{5,1},{6,2},{7,3},{8,4},{9,5},{1... | collective-permute-start | bytes 393224 | tf_op jit(solution)/shard_map/ppermute | solution.py:409
  4.6 1.5 %collective-permute-start.3 = (bf16[16,4096]{1,0:T(8,128)(2,1)}, bf16[16,4096]{1,0:T(8,128)(2,1)S(1)}, u32[]{:S(2)}, u32[]{:S(2)}) collective-permute-start(bf16[16,4096]{1,0:T(8,128)(2,1)} %refs_0_.1), channel_id=1, source_target_pairs={{0,1},{1,0},{2,3},{3,2},{4,5},{5,4},{6,7},{7,6},{8,9},{9,8},{10,11... | collective-permute-start | bytes 393224 | tf_op jit(solution)/shard_map/ppermute | solution.py:409
  6.1 1.2 %collective-permute-start.7 = (bf16[16,4096]{1,0:T(8,128)(2,1)}, bf16[16,4096]{1,0:T(8,128)(2,1)S(1)}, u32[]{:S(2)}, u32[]{:S(2)}) collective-permute-start(bf16[16,4096]{1,0:T(8,128)(2,1)} %refs_0_.1), channel_id=1, source_target_pairs={{0,2},{1,3},{2,0},{3,1},{4,6},{5,7},{6,4},{7,5},{8,10},{9,11},{10,... | collective-permute-start | bytes 393224 | tf_op jit(solution)/shard_map/ppermute | solution.py:409
  7.4 1.9 %collective-permute-start.6 = (bf16[16,4096]{1,0:T(8,128)(2,1)S(1)}, bf16[16,4096]{1,0:T(8,128)(2,1)S(1)}, u32[]{:S(2)}, u32[]{:S(2)}) collective-permute-start(bf16[16,4096]{1,0:T(8,128)(2,1)S(1)} %collective-permute-done.2._.refs_3_), channel_id=1, source_target_pairs={{0,1},{1,0},{2,3},{3,2},{4,5},{5,4},{6,7},{7,6},{8,9},{9,8},{10,11... | collective-permute-start | bytes 393224 | tf_op jit(solution)/shard_map/ppermute | solution.py:409
  9.3 1.0 %collective-permute-done.refs_1_ = bf16[16,4096]{1,0:T(8,128)(2,1)S(1)} collective-permute-done((bf16[16,4096]{1,0:T(8,128)(2,1)}, bf16[16,4096]{1,0:T(8,128)(2,1)S(1)}, u32[]{:S(2)}, u32[]{:S(2)}) %collective-permute-start) | collective-permute-done | bytes 131104 | tf_op jit(solution)/shard_map/ppermute | solution.py:409
  10.3 3.2 %collective-permute-start.4 = (bf16[16,4096]{1,0:T(8,128)(2,1)S(1)}, bf16[16,4096]{1,0:T(8,128)(2,1)S(1)}, u32[]{:S(2)}, u32[]{:S(2)}) collective-permute-start(bf16[16,4096]{1,0:T(8,128)(2,1)S(1)} %collective-permute-done.refs_1_), channel_id=1, source_target_pairs={{0,1},{1,0},{2,3},{3,2},{4,5},{5,4},{6,7},{7,6},{8,9},{9,8},{10,11... | collective-permute-start | bytes 393224 | tf_op jit(solution)/shard_map/ppermute | solution.py:409
  13.5 1.9 %collective-permute-done.1.refs_2_ = bf16[16,4096]{1,0:T(8,128)(2,1)S(1)} collective-permute-done((bf16[16,4096]{1,0:T(8,128)(2,1)}, bf16[16,4096]{1,0:T(8,128)(2,1)S(1)}, u32[]{:S(2)}, u32[]{:S(2)}) %collective-permute-start.1) | collective-permute-done | bytes 131104 | tf_op jit(solution)/shard_map/ppermute | solution.py:409
  15.4 1.2 %collective-permute-start.10 = (bf16[16,4096]{1,0:T(8,128)(2,1)S(1)}, bf16[16,4096]{1,0:T(8,128)(2,1)S(1)}, u32[]{:S(2)}, u32[]{:S(2)}) collective-permute-start(bf16[16,4096]{1,0:T(8,128)(2,1)S(1)} %collective-permute-done.2._.refs_3_), channel_id=1, source_target_pairs={{0,2},{1,3},{2,0},{3,1},{4,6},{5,7},{6,4},{7,5},{8,10},{9,11},{10,... | collective-permute-start | bytes 393224 | tf_op jit(solution)/shard_map/ppermute | solution.py:409
  16.9 1.2 %collective-permute-start.9 = (bf16[16,4096]{1,0:T(8,128)(2,1)S(1)}, bf16[16,4096]{1,0:T(8,128)(2,1)S(1)}, u32[]{:S(2)}, u32[]{:S(2)}) collective-permute-start(bf16[16,4096]{1,0:T(8,128)(2,1)S(1)} %collective-permute-done.1.refs_2_), channel_id=1, source_target_pairs={{0,2},{1,3},{2,0},{3,1},{4,6},{5,7},{6,4},{7,5},{8,10},{9,11},{10,... | collective-permute-start | bytes 393224 | tf_op jit(solution)/shard_map/ppermute | solution.py:409
  18.1 2.2 %collective-permute-start.5 = (bf16[16,4096]{1,0:T(8,128)(2,1)S(1)}, bf16[16,4096]{1,0:T(8,128)(2,1)S(1)}, u32[]{:S(2)}, u32[]{:S(2)}) collective-permute-start(bf16[16,4096]{1,0:T(8,128)(2,1)S(1)} %collective-permute-done.1.refs_2_), channel_id=1, source_target_pairs={{0,1},{1,0},{2,3},{3,2},{4,5},{5,4},{6,7},{7,6},{8,9},{9,8},{10,11... | collective-permute-start | bytes 393224 | tf_op jit(solution)/shard_map/ppermute | solution.py:409
  20.6 5.8 %fetch.1 = (bf16[4096,1024]{1,0:T(8,128)(2,1)S(1)}, bf16[4096,1024]{1,0:T(8,128)(2,1)S(1)}) custom-call(bf16[16,4096]{1,0:T(8,128)(2,1)S(1)} %collective-permute-done.2._.refs_3_, bf16[2,4096,1024]{2,1,0:T(8,128)(2,1)} %refs_14_.1), custom_call_target="tpu_custom_call" | custom-call | bytes 33554432 | tf_op jit(solution)/shard_map/fetch/pallas_call | solution.py:117
  27.6 8.0 %first_hidden.1 = (bf16[128,1024]{1,0:T(8,128)(2,1)S(1)}, bf16[128,1024]{1,0:T(8,128)(2,1)S(1)}, bf16[4096,1024]{1,0:T(8,128)(2,1)S(1)}, bf16[4096,1024]{1,0:T(8,128)(2,1)S(1)}) custom-call(bf16[16,4096]{1,0:T(8,128)(2,1)S(1)} %copy-done.1, bf16[16,4096]{1,0:T(8,128)(2,1)S(1)} %collective-permute-done.refs_1_, ...), custom_call_target="tpu_custom_call" | custom-call | flops 4294967296 | bytes 16777216 | tf_op jit(solution)/shard_map/first_hidden/pallas_call | solution.py:180
  35.6 12.2 %next_hidden.1 = (bf16[128,1024]{1,0:T(8,128)(2,1)S(1)}, f32[64,4096]{1,0:T(8,128)S(1)}, bf16[64,4096]{1,0:T(8,128)(2,1)S(1)}, f32[64,4096]{1,0:T(8,128)S(1)}, bf16[64,4096]{1,0:T(8,128)(2,1)S(1)}) custom-call(bf16[16,4096]{1,0:T(8,128)(2,1)S(1)} %collective-permute-done.7.refs_0_, bf16[16,4096]{1,0:T(8,128)(2,1)S(1)} %collective-permute-done.8.refs_1_, ...), custom_call_target="tpu_custom_call" | custom-call | flops 5368709120 | bytes 16777216 | tf_op jit(solution)/shard_map/next_hidden/pallas_call | solution.py:256
  48.4 1.4 %collective-permute-done.16.refs_0_ = bf16[64,4096]{1,0:T(8,128)(2,1)S(1)} collective-permute-done((bf16[64,4096]{1,0:T(8,128)(2,1)S(1)}, bf16[64,4096]{1,0:T(8,128)(2,1)S(1)}, u32[]{:S(2)}, u32[]{:S(2)}) %collective-permute-start.16) | collective-permute-done | bytes 524320 | tf_op jit(solution)/shard_map/ppermute | solution.py:424
  50.5 0.9 collective-permute-start.20
  52.0 0.9 collective-permute-start.17
  52.9 2.0 %collective-permute-done.22.refs_1_ = bf16[16,4096]{1,0:T(8,128)(2,1)S(1)} collective-permute-done((bf16[16,4096]{1,0:T(8,128)(2,1)S(1)}, bf16[16,4096]{1,0:T(8,128)(2,1)S(1)}, u32[]{:S(2)}, u32[]{:S(2)}) %collective-permute-start.22) | collective-permute-done | bytes 131104 | tf_op jit(solution)/shard_map/ppermute | solution.py:424
  55.0 2.7 %collective-permute-done.20.refs_1_ = bf16[16,4096]{1,0:T(8,128)(2,1)S(1)} collective-permute-done((bf16[16,4096]{1,0:T(8,128)(2,1)S(1)}, bf16[16,4096]{1,0:T(8,128)(2,1)S(1)}, u32[]{:S(2)}, u32[]{:S(2)}) %collective-permute-start.20) | collective-permute-done | bytes 131104 | tf_op jit(solution)/shard_map/ppermute | solution.py:424
  57.7 2.0 %collective-permute-start.21 = (bf16[16,4096]{1,0:T(8,128)(2,1)S(1)}, bf16[16,4096]{1,0:T(8,128)(2,1)S(1)}, u32[]{:S(2)}, u32[]{:S(2)}) collective-permute-start(bf16[16,4096]{1,0:T(8,128)(2,1)S(1)} %add.5), channel_id=1, source_target_pairs={{0,12},{1,13},{2,14},{3,15},{4,0},{5,1},{6,2},{7,3},{8,4},{9,5},{1... | collective-permute-start | bytes 393224 | tf_op jit(solution)/shard_map/ppermute | solution.py:424
  59.7 0.7 collective-permute-done.18.refs_1_
  60.7 2.6 %collective-permute-done.17.refs_1_ = bf16[16,4096]{1,0:T(8,128)(2,1)S(1)} collective-permute-done((bf16[16,4096]{1,0:T(8,128)(2,1)S(1)}, bf16[16,4096]{1,0:T(8,128)(2,1)S(1)}, u32[]{:S(2)}, u32[]{:S(2)}) %collective-permute-start.17) | collective-permute-done | bytes 131104 | tf_op jit(solution)/shard_map/ppermute | solution.py:424
  63.3 0.8 collective-permute-done.21.refs_3_
  64.1 5.9 %collective-permute-done.19.refs_2_ = bf16[16,4096]{1,0:T(8,128)(2,1)S(1)} collective-permute-done((bf16[16,4096]{1,0:T(8,128)(2,1)S(1)}, bf16[16,4096]{1,0:T(8,128)(2,1)S(1)}, u32[]{:S(2)}, u32[]{:S(2)}) %collective-permute-start.19) | collective-permute-done | bytes 131104 | tf_op jit(solution)/shard_map/ppermute | solution.py:424
  70.2 2.8 %collective-permute-start.25 = (bf16[16,4096]{1,0:T(8,128)(2,1)S(1)}, bf16[16,4096]{1,0:T(8,128)(2,1)S(1)}, u32[]{:S(2)}, u32[]{:S(2)}) collective-permute-start(bf16[16,4096]{1,0:T(8,128)(2,1)S(1)} %add.7.refs_2_), channel_id=1, source_target_pairs={{0,8},{1,9},{2,10},{3,11},{4,12},{5,13},{6,14},{7,15},{8,0},{9,1},... | collective-permute-start | bytes 393224 | tf_op jit(solution)/shard_map/ppermute | solution.py:409
  73.9 1.7 %collective-permute-start.27 = (bf16[16,4096]{1,0:T(8,128)(2,1)S(1)}, bf16[16,4096]{1,0:T(8,128)(2,1)S(1)}, u32[]{:S(2)}, u32[]{:S(2)}) collective-permute-start(bf16[16,4096]{1,0:T(8,128)(2,1)S(1)} %add.7.refs_2_), channel_id=1, source_target_pairs={{0,1},{1,0},{2,3},{3,2},{4,5},{5,4},{6,7},{7,6},{8,9},{9,8},{10,11... | collective-permute-start | bytes 393224 | tf_op jit(solution)/shard_map/ppermute | solution.py:409
  75.9 0.8 collective-permute-start.32
  76.8 5.3 %collective-permute-done.25.refs_4_ = bf16[16,4096]{1,0:T(8,128)(2,1)S(1)} collective-permute-done((bf16[16,4096]{1,0:T(8,128)(2,1)S(1)}, bf16[16,4096]{1,0:T(8,128)(2,1)S(1)}, u32[]{:S(2)}, u32[]{:S(2)}) %collective-permute-start.25) | collective-permute-done | bytes 131104 | tf_op jit(solution)/shard_map/ppermute | solution.py:409
  82.1 1.2 %collective-permute-start.33 = (bf16[16,4096]{1,0:T(8,128)(2,1)S(1)}, bf16[16,4096]{1,0:T(8,128)(2,1)S(1)}, u32[]{:S(2)}, u32[]{:S(2)}) collective-permute-start(bf16[16,4096]{1,0:T(8,128)(2,1)S(1)} %collective-permute-done.25.refs_4_), channel_id=1, source_target_pairs={{0,2},{1,3},{2,0},{3,1},{4,6},{5,7},{6,4},{7,5},{8,10},{9,11},{10,... | collective-permute-start | bytes 393224 | tf_op jit(solution)/shard_map/ppermute | solution.py:409
  83.6 2.1 %collective-permute-start.28 = (bf16[16,4096]{1,0:T(8,128)(2,1)S(1)}, bf16[16,4096]{1,0:T(8,128)(2,1)S(1)}, u32[]{:S(2)}, u32[]{:S(2)}) collective-permute-start(bf16[16,4096]{1,0:T(8,128)(2,1)S(1)} %collective-permute-done.24.refs_3_), channel_id=1, source_target_pairs={{0,1},{1,0},{2,3},{3,2},{4,5},{5,4},{6,7},{7,6},{8,9},{9,8},{10,11... | collective-permute-start | bytes 393224 | tf_op jit(solution)/shard_map/ppermute | solution.py:409
  86.2 3.3 %collective-permute-start.35 = (bf16[16,4096]{1,0:T(8,128)(2,1)S(1)}, bf16[16,4096]{1,0:T(8,128)(2,1)S(1)}, u32[]{:S(2)}, u32[]{:S(2)}) collective-permute-start(bf16[16,4096]{1,0:T(8,128)(2,1)S(1)} %collective-permute-done.31.refs_10_), channel_id=1, source_target_pairs={{0,1},{1,0},{2,3},{3,2},{4,5},{5,4},{6,7},{7,6},{8,9},{9,8},{10,11... | collective-permute-start | bytes 393224 | tf_op jit(solution)/shard_map/ppermute | solution.py:409
  89.4 1.4 %collective-permute-start.36 = (bf16[16,4096]{1,0:T(8,128)(2,1)S(1)}, bf16[16,4096]{1,0:T(8,128)(2,1)S(1)}, u32[]{:S(2)}, u32[]{:S(2)}) collective-permute-start(bf16[16,4096]{1,0:T(8,128)(2,1)S(1)} %collective-permute-done.32.refs_11_), channel_id=1, source_target_pairs={{0,1},{1,0},{2,3},{3,2},{4,5},{5,4},{6,7},{7,6},{8,9},{9,8},{10,11... | collective-permute-start | bytes 393224 | tf_op jit(solution)/shard_map/ppermute | solution.py:409
  92.4 6.5 %gram.1 = bf16[1024,4096]{1,0:T(8,128)(2,1)} custom-call(bf16[128,1024]{1,0:T(8,128)(2,1)S(1)} %get-tuple-element.22.refs_0_, bf16[128,1024]{1,0:T(8,128)(2,1)S(1)} %get-tuple-element.26.refs_1_, bf16[16,4096]{1,0:T(8,128)(2,1)S(1)} %add.7.refs_2_, bf16[16,4096]{1,0:T(8,128)(2,1)S(1)} %collective-permute-done.24.refs_3_, ...), custom_call_target="tpu_custom_call" | custom-call | tf_op jit(solution)/shard_map/gram/pallas_call | solution.py:369
  (62 shorter events, 8.0 us)
Async XLA Ops:
  0.0 7.4 %collective-permute-start.2 = (bf16[16,4096]{1,0:T(8,128)(2,1)}, bf16[16,4096]{1,0:T(8,128)(2,1)S(1)}, u32[]{:S(2)}, u32[]{:S(2)}) collective-permute-start(bf16[16,4096]{1,0:T(8,128)(2,1)} %refs_0_.1), channel_id=1, source_target_pairs={{0,12},{1,13},{2,14},{3,15},{4,0},{5,1},{6,2},{7,3},{8,4},{9,5},{1... | collective-permute-start | bytes 393224 | tf_op jit(solution)/shard_map/ppermute | solution.py:409
  4.1 6.2 %collective-permute-start = (bf16[16,4096]{1,0:T(8,128)(2,1)}, bf16[16,4096]{1,0:T(8,128)(2,1)S(1)}, u32[]{:S(2)}, u32[]{:S(2)}) collective-permute-start(bf16[16,4096]{1,0:T(8,128)(2,1)} %refs_0_.1), channel_id=1, source_target_pairs={{0,4},{1,5},{2,6},{3,7},{4,8},{5,9},{6,10},{7,11},{8,12},{9,13},{1... | collective-permute-start | bytes 393224 | tf_op jit(solution)/shard_map/ppermute | solution.py:409
  4.1 11.2 %collective-permute-start.1 = (bf16[16,4096]{1,0:T(8,128)(2,1)}, bf16[16,4096]{1,0:T(8,128)(2,1)S(1)}, u32[]{:S(2)}, u32[]{:S(2)}) collective-permute-start(bf16[16,4096]{1,0:T(8,128)(2,1)} %refs_0_.1), channel_id=1, source_target_pairs={{0,8},{1,9},{2,10},{3,11},{4,12},{5,13},{6,14},{7,15},{8,0},{9,1},... | collective-permute-start | bytes 393224 | tf_op jit(solution)/shard_map/ppermute | solution.py:409
  4.6 12.0 %collective-permute-start.3 = (bf16[16,4096]{1,0:T(8,128)(2,1)}, bf16[16,4096]{1,0:T(8,128)(2,1)S(1)}, u32[]{:S(2)}, u32[]{:S(2)}) collective-permute-start(bf16[16,4096]{1,0:T(8,128)(2,1)} %refs_0_.1), channel_id=1, source_target_pairs={{0,1},{1,0},{2,3},{3,2},{4,5},{5,4},{6,7},{7,6},{8,9},{9,8},{10,11... | collective-permute-start | bytes 393224 | tf_op jit(solution)/shard_map/ppermute | solution.py:409
  6.1 10.8 %collective-permute-start.7 = (bf16[16,4096]{1,0:T(8,128)(2,1)}, bf16[16,4096]{1,0:T(8,128)(2,1)S(1)}, u32[]{:S(2)}, u32[]{:S(2)}) collective-permute-start(bf16[16,4096]{1,0:T(8,128)(2,1)} %refs_0_.1), channel_id=1, source_target_pairs={{0,2},{1,3},{2,0},{3,1},{4,6},{5,7},{6,4},{7,5},{8,10},{9,11},{10,... | collective-permute-start | bytes 393224 | tf_op jit(solution)/shard_map/ppermute | solution.py:409
  7.4 10.8 %collective-permute-start.6 = (bf16[16,4096]{1,0:T(8,128)(2,1)S(1)}, bf16[16,4096]{1,0:T(8,128)(2,1)S(1)}, u32[]{:S(2)}, u32[]{:S(2)}) collective-permute-start(bf16[16,4096]{1,0:T(8,128)(2,1)S(1)} %collective-permute-done.2._.refs_3_), channel_id=1, source_target_pairs={{0,1},{1,0},{2,3},{3,2},{4,5},{5,4},{6,7},{7,6},{8,9},{9,8},{10,11... | collective-permute-start | bytes 393224 | tf_op jit(solution)/shard_map/ppermute | solution.py:409
  10.3 16.1 %collective-permute-start.4 = (bf16[16,4096]{1,0:T(8,128)(2,1)S(1)}, bf16[16,4096]{1,0:T(8,128)(2,1)S(1)}, u32[]{:S(2)}, u32[]{:S(2)}) collective-permute-start(bf16[16,4096]{1,0:T(8,128)(2,1)S(1)} %collective-permute-done.refs_1_), channel_id=1, source_target_pairs={{0,1},{1,0},{2,3},{3,2},{4,5},{5,4},{6,7},{7,6},{8,9},{9,8},{10,11... | collective-permute-start | bytes 393224 | tf_op jit(solution)/shard_map/ppermute | solution.py:409
  15.4 11.2 %collective-permute-start.10 = (bf16[16,4096]{1,0:T(8,128)(2,1)S(1)}, bf16[16,4096]{1,0:T(8,128)(2,1)S(1)}, u32[]{:S(2)}, u32[]{:S(2)}) collective-permute-start(bf16[16,4096]{1,0:T(8,128)(2,1)S(1)} %collective-permute-done.2._.refs_3_), channel_id=1, source_target_pairs={{0,2},{1,3},{2,0},{3,1},{4,6},{5,7},{6,4},{7,5},{8,10},{9,11},{10,... | collective-permute-start | bytes 393224 | tf_op jit(solution)/shard_map/ppermute | solution.py:409
  16.6 10.4 %collective-permute-start.8 = (bf16[16,4096]{1,0:T(8,128)(2,1)S(1)}, bf16[16,4096]{1,0:T(8,128)(2,1)S(1)}, u32[]{:S(2)}, u32[]{:S(2)}) collective-permute-start(bf16[16,4096]{1,0:T(8,128)(2,1)S(1)} %collective-permute-done.refs_1_), channel_id=1, source_target_pairs={{0,2},{1,3},{2,0},{3,1},{4,6},{5,7},{6,4},{7,5},{8,10},{9,11},{10,... | collective-permute-start | bytes 393224 | tf_op jit(solution)/shard_map/ppermute | solution.py:409
  16.9 10.3 %collective-permute-start.9 = (bf16[16,4096]{1,0:T(8,128)(2,1)S(1)}, bf16[16,4096]{1,0:T(8,128)(2,1)S(1)}, u32[]{:S(2)}, u32[]{:S(2)}) collective-permute-start(bf16[16,4096]{1,0:T(8,128)(2,1)S(1)} %collective-permute-done.1.refs_2_), channel_id=1, source_target_pairs={{0,2},{1,3},{2,0},{3,1},{4,6},{5,7},{6,4},{7,5},{8,10},{9,11},{10,... | collective-permute-start | bytes 393224 | tf_op jit(solution)/shard_map/ppermute | solution.py:409
  18.1 9.5 %collective-permute-start.5 = (bf16[16,4096]{1,0:T(8,128)(2,1)S(1)}, bf16[16,4096]{1,0:T(8,128)(2,1)S(1)}, u32[]{:S(2)}, u32[]{:S(2)}) collective-permute-start(bf16[16,4096]{1,0:T(8,128)(2,1)S(1)} %collective-permute-done.1.refs_2_), channel_id=1, source_target_pairs={{0,1},{1,0},{2,3},{3,2},{4,5},{5,4},{6,7},{7,6},{8,9},{9,8},{10,11... | collective-permute-start | bytes 393224 | tf_op jit(solution)/shard_map/ppermute | solution.py:409
  26.5 9.1 %collective-permute-start.11 = (bf16[16,4096]{1,0:T(8,128)(2,1)S(1)}, bf16[16,4096]{1,0:T(8,128)(2,1)S(1)}, u32[]{:S(2)}, u32[]{:S(2)}) collective-permute-start(bf16[16,4096]{1,0:T(8,128)(2,1)S(1)} %collective-permute-done.7.refs_0_), channel_id=1, source_target_pairs={{0,1},{1,0},{2,3},{3,2},{4,5},{5,4},{6,7},{7,6},{8,9},{9,8},{10,11... | collective-permute-start | bytes 393224 | tf_op jit(solution)/shard_map/ppermute | solution.py:409
  26.6 9.0 %collective-permute-start.14 = (bf16[16,4096]{1,0:T(8,128)(2,1)S(1)}, bf16[16,4096]{1,0:T(8,128)(2,1)S(1)}, u32[]{:S(2)}, u32[]{:S(2)}) collective-permute-start(bf16[16,4096]{1,0:T(8,128)(2,1)S(1)} %collective-permute-done.10.refs_3_), channel_id=1, source_target_pairs={{0,1},{1,0},{2,3},{3,2},{4,5},{5,4},{6,7},{7,6},{8,9},{9,8},{10,11... | collective-permute-start | bytes 393224 | tf_op jit(solution)/shard_map/ppermute | solution.py:409
  27.1 8.6 %collective-permute-start.12 = (bf16[16,4096]{1,0:T(8,128)(2,1)S(1)}, bf16[16,4096]{1,0:T(8,128)(2,1)S(1)}, u32[]{:S(2)}, u32[]{:S(2)}) collective-permute-start(bf16[16,4096]{1,0:T(8,128)(2,1)S(1)} %collective-permute-done.8.refs_1_), channel_id=1, source_target_pairs={{0,1},{1,0},{2,3},{3,2},{4,5},{5,4},{6,7},{7,6},{8,9},{9,8},{10,11... | collective-permute-start | bytes 393224 | tf_op jit(solution)/shard_map/ppermute | solution.py:409
  27.1 8.5 %collective-permute-start.13 = (bf16[16,4096]{1,0:T(8,128)(2,1)S(1)}, bf16[16,4096]{1,0:T(8,128)(2,1)S(1)}, u32[]{:S(2)}, u32[]{:S(2)}) collective-permute-start(bf16[16,4096]{1,0:T(8,128)(2,1)S(1)} %collective-permute-done.9.refs_2_), channel_id=1, source_target_pairs={{0,1},{1,0},{2,3},{3,2},{4,5},{5,4},{6,7},{7,6},{8,9},{9,8},{10,11... | collective-permute-start | bytes 393224 | tf_op jit(solution)/shard_map/ppermute | solution.py:409
  50.5 7.1 %collective-permute-start.20 = (bf16[16,4096]{1,0:T(8,128)(2,1)S(1)}, bf16[16,4096]{1,0:T(8,128)(2,1)S(1)}, u32[]{:S(2)}, u32[]{:S(2)}) collective-permute-start(bf16[16,4096]{1,0:T(8,128)(2,1)S(1)} %get-tuple-element.33), channel_id=1, source_target_pairs={{0,2},{1,3},{2,0},{3,1},{4,6},{5,7},{6,4},{7,5},{8,10},{9,11},{10,... | collective-permute-start | bytes 393224 | tf_op jit(solution)/shard_map/ppermute | solution.py:424
  51.4 9.1 %collective-permute-start.18 = (bf16[16,4096]{1,0:T(8,128)(2,1)S(1)}, bf16[16,4096]{1,0:T(8,128)(2,1)S(1)}, u32[]{:S(2)}, u32[]{:S(2)}) collective-permute-start(bf16[16,4096]{1,0:T(8,128)(2,1)S(1)} %get-tuple-element.32), channel_id=1, source_target_pairs={{0,2},{1,3},{2,0},{3,1},{4,6},{5,7},{6,4},{7,5},{8,10},{9,11},{10,... | collective-permute-start | bytes 393224 | tf_op jit(solution)/shard_map/ppermute | solution.py:424
  52.0 11.3 %collective-permute-start.17 = (bf16[16,4096]{1,0:T(8,128)(2,1)S(1)}, bf16[16,4096]{1,0:T(8,128)(2,1)S(1)}, u32[]{:S(2)}, u32[]{:S(2)}) collective-permute-start(bf16[16,4096]{1,0:T(8,128)(2,1)S(1)} %get-tuple-element.31), channel_id=1, source_target_pairs={{0,2},{1,3},{2,0},{3,1},{4,6},{5,7},{6,4},{7,5},{8,10},{9,11},{10,... | collective-permute-start | bytes 393224 | tf_op jit(solution)/shard_map/ppermute | solution.py:424
  54.9 8.4 %collective-permute-start.23 = (bf16[16,4096]{1,0:T(8,128)(2,1)S(1)}, bf16[16,4096]{1,0:T(8,128)(2,1)S(1)}, u32[]{:S(2)}, u32[]{:S(2)}) collective-permute-start(bf16[16,4096]{1,0:T(8,128)(2,1)S(1)} %add.6), channel_id=1, source_target_pairs={{0,4},{1,5},{2,6},{3,7},{4,8},{5,9},{6,10},{7,11},{8,12},{9,13},{1... | collective-permute-start | bytes 393224 | tf_op jit(solution)/shard_map/ppermute | solution.py:424
  57.7 6.4 %collective-permute-start.21 = (bf16[16,4096]{1,0:T(8,128)(2,1)S(1)}, bf16[16,4096]{1,0:T(8,128)(2,1)S(1)}, u32[]{:S(2)}, u32[]{:S(2)}) collective-permute-start(bf16[16,4096]{1,0:T(8,128)(2,1)S(1)} %add.5), channel_id=1, source_target_pairs={{0,12},{1,13},{2,14},{3,15},{4,0},{5,1},{6,2},{7,3},{8,4},{9,5},{1... | collective-permute-start | bytes 393224 | tf_op jit(solution)/shard_map/ppermute | solution.py:424
  60.5 9.5 %collective-permute-start.19 = (bf16[16,4096]{1,0:T(8,128)(2,1)S(1)}, bf16[16,4096]{1,0:T(8,128)(2,1)S(1)}, u32[]{:S(2)}, u32[]{:S(2)}) collective-permute-start(bf16[16,4096]{1,0:T(8,128)(2,1)S(1)} %add.4), channel_id=1, source_target_pairs={{0,8},{1,9},{2,10},{3,11},{4,12},{5,13},{6,14},{7,15},{8,0},{9,1},... | collective-permute-start | bytes 393224 | tf_op jit(solution)/shard_map/ppermute | solution.py:424
  70.1 5.8 %collective-permute-start.24 = (bf16[16,4096]{1,0:T(8,128)(2,1)S(1)}, bf16[16,4096]{1,0:T(8,128)(2,1)S(1)}, u32[]{:S(2)}, u32[]{:S(2)}) collective-permute-start(bf16[16,4096]{1,0:T(8,128)(2,1)S(1)} %add.7.refs_2_), channel_id=1, source_target_pairs={{0,4},{1,5},{2,6},{3,7},{4,8},{5,9},{6,10},{7,11},{8,12},{9,13},{1... | collective-permute-start | bytes 393224 | tf_op jit(solution)/shard_map/ppermute | solution.py:409
  70.2 11.9 %collective-permute-start.25 = (bf16[16,4096]{1,0:T(8,128)(2,1)S(1)}, bf16[16,4096]{1,0:T(8,128)(2,1)S(1)}, u32[]{:S(2)}, u32[]{:S(2)}) collective-permute-start(bf16[16,4096]{1,0:T(8,128)(2,1)S(1)} %add.7.refs_2_), channel_id=1, source_target_pairs={{0,8},{1,9},{2,10},{3,11},{4,12},{5,13},{6,14},{7,15},{8,0},{9,1},... | collective-permute-start | bytes 393224 | tf_op jit(solution)/shard_map/ppermute | solution.py:409
  73.0 10.4 %collective-permute-start.26 = (bf16[16,4096]{1,0:T(8,128)(2,1)S(1)}, bf16[16,4096]{1,0:T(8,128)(2,1)S(1)}, u32[]{:S(2)}, u32[]{:S(2)}) collective-permute-start(bf16[16,4096]{1,0:T(8,128)(2,1)S(1)} %add.7.refs_2_), channel_id=1, source_target_pairs={{0,12},{1,13},{2,14},{3,15},{4,0},{5,1},{6,2},{7,3},{8,4},{9,5},{1... | collective-permute-start | bytes 393224 | tf_op jit(solution)/shard_map/ppermute | solution.py:409
  73.4 10.1 %collective-permute-start.31 = (bf16[16,4096]{1,0:T(8,128)(2,1)S(1)}, bf16[16,4096]{1,0:T(8,128)(2,1)S(1)}, u32[]{:S(2)}, u32[]{:S(2)}) collective-permute-start(bf16[16,4096]{1,0:T(8,128)(2,1)S(1)} %add.7.refs_2_), channel_id=1, source_target_pairs={{0,2},{1,3},{2,0},{3,1},{4,6},{5,7},{6,4},{7,5},{8,10},{9,11},{10,... | collective-permute-start | bytes 393224 | tf_op jit(solution)/shard_map/ppermute | solution.py:409
  73.9 11.8 %collective-permute-start.27 = (bf16[16,4096]{1,0:T(8,128)(2,1)S(1)}, bf16[16,4096]{1,0:T(8,128)(2,1)S(1)}, u32[]{:S(2)}, u32[]{:S(2)}) collective-permute-start(bf16[16,4096]{1,0:T(8,128)(2,1)S(1)} %add.7.refs_2_), channel_id=1, source_target_pairs={{0,1},{1,0},{2,3},{3,2},{4,5},{5,4},{6,7},{7,6},{8,9},{9,8},{10,11... | collective-permute-start | bytes 393224 | tf_op jit(solution)/shard_map/ppermute | solution.py:409
  75.9 9.8 %collective-permute-start.32 = (bf16[16,4096]{1,0:T(8,128)(2,1)S(1)}, bf16[16,4096]{1,0:T(8,128)(2,1)S(1)}, u32[]{:S(2)}, u32[]{:S(2)}) collective-permute-start(bf16[16,4096]{1,0:T(8,128)(2,1)S(1)} %collective-permute-done.24.refs_3_), channel_id=1, source_target_pairs={{0,2},{1,3},{2,0},{3,1},{4,6},{5,7},{6,4},{7,5},{8,10},{9,11},{10,... | collective-permute-start | bytes 393224 | tf_op jit(solution)/shard_map/ppermute | solution.py:409
  83.3 6.1 %collective-permute-start.34 = (bf16[16,4096]{1,0:T(8,128)(2,1)S(1)}, bf16[16,4096]{1,0:T(8,128)(2,1)S(1)}, u32[]{:S(2)}, u32[]{:S(2)}) collective-permute-start(bf16[16,4096]{1,0:T(8,128)(2,1)S(1)} %collective-permute-done.26.refs_5_), channel_id=1, source_target_pairs={{0,2},{1,3},{2,0},{3,1},{4,6},{5,7},{6,4},{7,5},{8,10},{9,11},{10,... | collective-permute-start | bytes 393224 | tf_op jit(solution)/shard_map/ppermute | solution.py:409
  83.6 7.3 %collective-permute-start.28 = (bf16[16,4096]{1,0:T(8,128)(2,1)S(1)}, bf16[16,4096]{1,0:T(8,128)(2,1)S(1)}, u32[]{:S(2)}, u32[]{:S(2)}) collective-permute-start(bf16[16,4096]{1,0:T(8,128)(2,1)S(1)} %collective-permute-done.24.refs_3_), channel_id=1, source_target_pairs={{0,1},{1,0},{2,3},{3,2},{4,5},{5,4},{6,7},{7,6},{8,9},{9,8},{10,11... | collective-permute-start | bytes 393224 | tf_op jit(solution)/shard_map/ppermute | solution.py:409
  85.6 5.2 %collective-permute-start.29 = (bf16[16,4096]{1,0:T(8,128)(2,1)S(1)}, bf16[16,4096]{1,0:T(8,128)(2,1)S(1)}, u32[]{:S(2)}, u32[]{:S(2)}) collective-permute-start(bf16[16,4096]{1,0:T(8,128)(2,1)S(1)} %collective-permute-done.25.refs_4_), channel_id=1, source_target_pairs={{0,1},{1,0},{2,3},{3,2},{4,5},{5,4},{6,7},{7,6},{8,9},{9,8},{10,11... | collective-permute-start | bytes 393224 | tf_op jit(solution)/shard_map/ppermute | solution.py:409
  85.7 5.6 %collective-permute-start.30 = (bf16[16,4096]{1,0:T(8,128)(2,1)S(1)}, bf16[16,4096]{1,0:T(8,128)(2,1)S(1)}, u32[]{:S(2)}, u32[]{:S(2)}) collective-permute-start(bf16[16,4096]{1,0:T(8,128)(2,1)S(1)} %collective-permute-done.26.refs_5_), channel_id=1, source_target_pairs={{0,1},{1,0},{2,3},{3,2},{4,5},{5,4},{6,7},{7,6},{8,9},{9,8},{10,11... | collective-permute-start | bytes 393224 | tf_op jit(solution)/shard_map/ppermute | solution.py:409
  86.2 5.2 %collective-permute-start.35 = (bf16[16,4096]{1,0:T(8,128)(2,1)S(1)}, bf16[16,4096]{1,0:T(8,128)(2,1)S(1)}, u32[]{:S(2)}, u32[]{:S(2)}) collective-permute-start(bf16[16,4096]{1,0:T(8,128)(2,1)S(1)} %collective-permute-done.31.refs_10_), channel_id=1, source_target_pairs={{0,1},{1,0},{2,3},{3,2},{4,5},{5,4},{6,7},{7,6},{8,9},{9,8},{10,11... | collective-permute-start | bytes 393224 | tf_op jit(solution)/shard_map/ppermute | solution.py:409
  (10 other events, 42.1 us)

commit v2 on v1

--- a/solution.py
+++ b/solution.py
@@ -34,28 +34,37 @@
     return jax.ShapeDtypeStruct(tuple(dims), dtype)
 
 
-def rotate_rows(x_ref, sign, table, o_ref, step):
+def stack(blocks, o_ref):
+    rows = blocks[0].shape[0]
+    for k, block in enumerate(blocks):
+        o_ref[k * rows : (k + 1) * rows, :] = block[...]
+
+
+def rotate_rows(blocks, sign, table, x_ref, mixed_ref, o_ref):
+    stack(blocks, x_ref)
     rows, width = x_ref.shape
     inner = table.shape[0]
+    count = width // inner
+    scale = 1.0 / width**0.5
+    signed = jnp.concatenate(
+        [x_ref[:, k : k + inner] * sign[:, k : k + inner] for k in range(0, width, inner)], axis=0
+    )
+    mixed_ref[...] = jnp.dot(signed, table, preferred_element_type=F32)
+    step = 16
 
     @pl.loop(0, rows // step)
     def _(block):
-        cut = pl.ds(pl.multiple_of(block * step, step), step)
-        parts = [
-            jnp.dot(
-                x_ref[cut, k : k + inner] * sign[:, k : k + inner], table, preferred_element_type=F32
-            )
-            for k in range(0, width, inner)
-        ]
+        row = pl.multiple_of(block * step, step)
+        parts = [mixed_ref[pl.ds(k * rows + row, step), :] for k in range(count)]
         span = 1
-        while span < len(parts):
-            for k in range(len(parts)):
+        while span < count:
+            for k in range(count):
                 if not k & span:
                     a, b = parts[k], parts[k + span]
                     parts[k], parts[k + span] = a + b, a - b
             span *= 2
         for k, part in enumerate(parts):
-            o_ref[cut, k * inner : (k + 1) * inner] = (part * (1.0 / width**0.5)).astype(BF16)
+            o_ref[pl.ds(row, step), k * inner : (k + 1) * inner] = (part * scale).astype(BF16)
 
 
 def swiglu(pieces, input_ref, gate_of, upper_of):
@@ -69,12 +78,16 @@
     return (gate / (1.0 + jnp.exp(-gate)) * upper).astype(BF16)
 
 
+def depth_pieces(groups):
+    return math.gcd(groups, 4)
+
+
 def hidden_columns(
-    block, width, tok_ref, rot_ref, gu_refs, qc_refs, qe_ref, hq_ref, mm_ref, full_first, arrived
+    block, width, tok_ref, rot_ref, gu_refs, codes_of, qe_ref, hq_ref, mm_ref, full_first, arrived
 ):
     depth = tok_ref.shape[1]
     groups = qe_ref.shape[1]
-    pieces = math.gcd(groups, 4)
+    pieces = depth_pieces(groups)
     cut = pl.ds(pl.multiple_of(block * width, width), width)
 
     def full_weight(i):
@@ -84,8 +97,7 @@
         def piece(k, rows):
             exps = qe_ref[i, k * groups // pieces : (k + 1) * groups // pieces, cut]
             scale = jnp.exp2(exps.astype(F32)).astype(BF16)
-            columns = cut if qc_refs[i].shape[1] > width else slice(None)
-            codes = qc_refs[i][rows, columns].reshape(groups // pieces, depth // groups, width)
+            codes = codes_of(i, k, rows, cut).reshape(groups // pieces, depth // groups, width)
             return (codes * scale[:, None, :]).reshape(depth // pieces, width)
 
         return piece
@@ -103,8 +115,13 @@
 
 def fetch_kernel(_, source, *refs):
     targets, sem = refs[:-1], refs[-1]
+    rows = targets[0].shape[0]
+    pieces = source.shape[1] // rows
     copies = [
-        pltpu.make_async_copy(source.at[k], target, sem.at[k]) for k, target in enumerate(targets)
+        pltpu.make_async_copy(
+            source.at[k // pieces, pl.ds(k % pieces * rows, rows)], target, sem.at[k]
+        )
+        for k, target in enumerate(targets)
     ]
     for copy in copies:
         copy.start()
@@ -112,13 +129,14 @@
         copy.wait()
 
 
-def fetch(after, weights):
-    count = weights.shape[0]
+def fetch(after, weights, pieces):
+    count = weights.shape[0] * pieces
+    dims = weights.shape[1] // pieces, weights.shape[2]
     return pl.pallas_call(
         fetch_kernel,
         in_specs=[spec(pltpu.VMEM), spec(pltpu.HBM)],
         out_specs=[spec(pltpu.VMEM)] * count,
-        out_shape=[pltpu.VMEM(weights.shape[1:], weights.dtype)] * count,
+        out_shape=[pltpu.VMEM(dims, weights.dtype)] * count,
         scratch_shapes=[pltpu.SemaphoreType.DMA((count,))],
         compiler_params=params(1),
         cost_estimate=pl.CostEstimate(
@@ -135,17 +153,11 @@
     send_ref[...] = total[own:].astype(BF16)
 
 
-def stack(blocks, o_ref):
-    rows = blocks[0].shape[0]
-    for k, block in enumerate(blocks):
-        o_ref[k * rows : (k + 1) * rows, :] = block[...]
-
-
 def first_kernel(count, *refs):
     blocks, refs = refs[:count], refs[count:]
-    flip_ref, table_ref, *qc_refs, qe_ref, gu_hbm = refs[:6]
-    hq_ref, mm_ref, *gu_refs = refs[6:10]
-    tok_ref, rot_ref, gu_sem = refs[10:]
+    flip_ref, table_ref, *qc_refs, qe_ref, gu_hbm = refs[:-8]
+    hq_ref, mm_ref, *gu_refs = refs[-8:-4]
+    tok_ref, rot_ref, mixed_ref, gu_sem = refs[-4:]
     units = hq_ref.shape[1]
     step = min(256, units)
 
@@ -162,15 +174,15 @@
     for block in range(units // step):
         for k in range(2):
             full(k, block).start()
-    stack(blocks, tok_ref)
     sign = (1 - 2 * flip_ref[...]).astype(F32).astype(BF16)
-    rotate_rows(tok_ref, sign, table_ref[...], rot_ref, 64)
+    rotate_rows(blocks, sign, table_ref[...], tok_ref, mixed_ref, rot_ref)
 
     @pl.loop(0, units // step)
     def _(block):
         hidden_columns(
-            block, step, tok_ref, rot_ref, gu_refs, qc_refs, qe_ref, hq_ref, mm_ref,
-            full_first=False, arrived=full_arrived,
+            block, step, tok_ref, rot_ref, gu_refs,
+            lambda i, k, rows, cut: qc_refs[i * len(qc_refs) // 2 + k][:, cut],
+            qe_ref, hq_ref, mm_ref, full_first=False, arrived=full_arrived,
         )
 
 
@@ -179,7 +191,7 @@
     units = codes[0].shape[1]
     return pl.pallas_call(
         functools.partial(first_kernel, len(blocks)),
-        in_specs=[spec(pltpu.VMEM)] * (len(blocks) + 5) + [spec(pltpu.HBM)],
+        in_specs=[spec(pltpu.VMEM)] * (len(blocks) + 3 + len(codes)) + [spec(pltpu.HBM)],
         out_specs=[spec(pltpu.VMEM)] * 4,
         out_shape=[
             shaped((rows, units), BF16),
@@ -190,9 +202,10 @@
         scratch_shapes=[
             pltpu.VMEM((rows, depth), BF16),
             pltpu.VMEM((rows, depth), BF16),
+            pltpu.VMEM((rows * depth // table.shape[0], table.shape[0]), F32),
             pltpu.SemaphoreType.DMA((2, units // min(256, units))),
         ],
-        compiler_params=params(4 + (2 * rows * depth >> 19)),
+        compiler_params=params(2 + (4 * rows * depth >> 19)),
         cost_estimate=pl.CostEstimate(
             flops=8 * rows * depth * units, transcendentals=0, bytes_accessed=2 * gate_up.size
         ),
@@ -203,14 +216,14 @@
     )
 
 
-def next_kernel(count, parts, *refs):
-    blocks, mms, refs = refs[:count], refs[count : count + parts], refs[count + parts :]
-    flip_ref, table_ref, *gu_refs, qe_ref, qc_hbm, down_hbm = refs[:7]
+def next_kernel(count, *refs):
+    blocks, refs = refs[:count], refs[count:]
+    flip_ref, table_ref, *gu_refs, qe_ref, down_ref, qc_hbm = refs[:7]
     hq_ref, keep_ref, send_ref = refs[7:10]
-    keeps, sends = refs[10 : 10 + parts], refs[10 + parts : 10 + 2 * parts]
-    tok_ref, rot_ref, mm_ref, qc_ref, down_ref, qc_sem, down_sem = refs[10 + 2 * parts :]
+    tok_ref, rot_ref, mixed_ref, mm_ref, qc_ref, qc_sem = refs[10:]
     units = hq_ref.shape[1]
     step = min(256, units)
+
     slots = qc_ref.shape[0]
 
     def codes(block):
@@ -218,18 +231,17 @@
         slot = lax.rem(block, slots)
         return pltpu.make_async_copy(qc_hbm.at[:, :, cut], qc_ref.at[slot], qc_sem.at[slot])
 
-    rest = pltpu.make_async_copy(down_hbm, down_ref, down_sem)
-    for block in range(min(slots, units // step)):
+    for block in range(slots):
         codes(block).start()
-    stack(blocks, tok_ref)
     sign = (1 - 2 * flip_ref[...]).astype(F32).astype(BF16)
-    rotate_rows(tok_ref, sign, table_ref[...], rot_ref, 64)
+    rotate_rows(blocks, sign, table_ref[...], tok_ref, mixed_ref, rot_ref)
 
     @pl.loop(0, units // step)
     def _(block):
         slot = lax.rem(block, slots)
         hidden_columns(
-            block, step, tok_ref, rot_ref, gu_refs, [qc_ref.at[slot, k] for k in range(2)],
+            block, step, tok_ref, rot_ref, gu_refs,
+            lambda i, k, rows, cut: qc_ref[slot, i, rows, :],
             qe_ref, hq_ref, mm_ref, full_first=True, arrived=lambda k: codes(k).wait(),
         )
 
@@ -237,51 +249,40 @@
         def _():
             codes(block + slots).start()
 
-        @pl.when(block == max(units // step - slots - 1, 0))
-        def _():
-            rest.start()
-
-    rest.wait()
     project(mm_ref, down_ref, keep_ref, send_ref)
-    for own_ref, kept, sent in zip(mms, keeps, sends):
-        project(own_ref, down_ref, kept, sent)
-
-
-def next_hidden(cores, blocks, mms, flip, table, gate_up, codes, exps, down):
+
+
+def next_hidden(cores, blocks, flip, table, gate_up, codes, exps, down):
     rows, depth = len(blocks) * blocks[0].shape[0], blocks[0].shape[1]
     units, width = down.shape
     own = rows // cores
     step = min(256, units)
-    parts = 1 + len(mms)
-    return pl.pallas_call(
-        functools.partial(next_kernel, len(blocks), len(mms)),
-        in_specs=[spec(pltpu.VMEM)] * (len(blocks) + len(mms) + 5) + [spec(pltpu.HBM)] * 2,
-        out_specs=[spec(pltpu.VMEM)] * (1 + 2 * parts),
+    slots = min(2, units // step)
+    return pl.pallas_call(
+        functools.partial(next_kernel, len(blocks)),
+        in_specs=[spec(pltpu.VMEM)] * (len(blocks) + 6) + [spec(pltpu.HBM)],
+        out_specs=[spec(pltpu.VMEM)] * 3,
         out_shape=[
             shaped((rows, units), BF16),
             shaped((own, width), F32),
             shaped((rows - own, width), BF16),
-        ]
-        + [shaped((own, width), F32)] * len(mms)
-        + [shaped((rows - own, width), BF16)] * len(mms),
+        ],
         scratch_shapes=[
             pltpu.VMEM((rows, depth), BF16),
             pltpu.VMEM((rows, depth), BF16),
+            pltpu.VMEM((rows * depth // table.shape[0], table.shape[0]), F32),
             pltpu.VMEM((rows, units), BF16),
-            pltpu.VMEM((2, 2, depth, step), BF16),
-            pltpu.VMEM(down.shape, BF16),
-            pltpu.SemaphoreType.DMA((2,)),
-            pltpu.SemaphoreType.DMA(()),
+            pltpu.VMEM((slots, 2, depth, step), BF16),
+            pltpu.SemaphoreType.DMA((slots,)),
         ],
-        compiler_params=params(2 + (2 * rows * depth + 4 * depth * step + down.size >> 19)),
+        compiler_params=params(2 + (4 * rows * depth + 2 * slots * depth * step >> 19)),
         cost_estimate=pl.CostEstimate(
             flops=10 * rows * depth * units, transcendentals=0, bytes_accessed=2 * codes.size
         ),
         name="next_hidden",
     )(
-        *blocks, *mms, flip, table, *gate_up, exps,
+        *blocks, flip, table, *gate_up, exps, down,
         pltpu.with_memory_space_constraint(codes, pltpu.HBM),
-        pltpu.with_memory_space_constraint(down, pltpu.HBM),
     )
 
 
@@ -297,7 +298,7 @@
         in_specs=[spec(pltpu.VMEM)] * 2,
         out_specs=[spec(pltpu.VMEM)] * 2,
         out_shape=[shaped((own, width), F32), shaped((rows - own, width), BF16)],
-        compiler_params=params(12),
+        compiler_params=params(4),
         name="last_project",
     )(mm, down)
 
@@ -346,34 +347,40 @@
 
 
 def gram_kernel(scale, parts, *refs):
-    hqs, blocks = refs[:parts], refs[parts:-3]
-    o_ref, hq_ref, proj_ref = refs[-3:]
-
-    @pl.when(pl.program_id(0) == 0)
-    def _():
-        stack(hqs, hq_ref)
-        stack(blocks, proj_ref)
-
-    step = o_ref.shape[0]
-    cut = pl.ds(pl.multiple_of(pl.program_id(0) * step, step), step)
-    gram = lax.dot_general(
-        hq_ref[:, cut], proj_ref[...], (((0,), (0,)), ((), ())), preferred_element_type=F32
-    )
-    o_ref[...] = (gram * scale).astype(BF16)
+    hqs, blocks = refs[:parts], refs[parts:-6]
+    o_hbm, hq_ref, turned_ref, proj_ref, o_ref, sem = refs[-6:]
+    stack(hqs, hq_ref)
+    stack(blocks, proj_ref)
+    turned_ref[...] = hq_ref[...].T
+    units = turned_ref.shape[0]
+    step = min(256, units)
+    copies = []
+    for k in range(units // step):
+        cut = pl.ds(k * step, step)
+        gram = jnp.dot(turned_ref[cut, :], proj_ref[...], preferred_element_type=F32)
+        o_ref[cut, :] = (gram * scale).astype(BF16)
+        copies.append(pltpu.make_async_copy(o_ref.at[cut], o_hbm.at[cut], sem.at[k]))
+        copies[-1].start()
+    for copy in copies:
+        copy.wait()
 
 
 def gram(hqs, blocks):
-    rows = len(hqs) * hqs[0].shape[0]
+    rows = sum(hq.shape[0] for hq in hqs)
     units, out = hqs[0].shape[1], blocks[0].shape[1]
-    step = min(128, units)
     return pl.pallas_call(
         functools.partial(gram_kernel, 1.0 / rows**0.5, len(hqs)),
-        grid=(units // step,),
         in_specs=[spec(pltpu.VMEM)] * (len(hqs) + len(blocks)),
-        out_specs=pl.BlockSpec((step, out), lambda i: (i, 0)),
+        out_specs=spec(pltpu.HBM),
         out_shape=shaped((units, out), BF16),
-        scratch_shapes=[pltpu.VMEM((rows, units), BF16), pltpu.VMEM((rows, out), BF16)],
-        compiler_params=params(16),
+        scratch_shapes=[
+            pltpu.VMEM((rows, units), BF16),
+            pltpu.VMEM((units, rows), BF16),
+            pltpu.VMEM((rows, out), BF16),
+            pltpu.VMEM((units, out), BF16),
+            pltpu.SemaphoreType.DMA((units // min(256, units),)),
+        ],
+        compiler_params=params(24),
         name="gram",
     )(*hqs, *blocks)
 
@@ -460,23 +467,18 @@
         flip = rotation_flip.reshape(1, width)
         table = hadamard_table(min(256, width)).astype(BF16)
         blocks, near = gather(grid, tokens)
-        codes = [held(value) for value in fetch(near, quant_codes)]
+        codes = [held(value) for value in fetch(near, quant_codes, depth_pieces(quant_exps.shape[1]))]
         hq, mm, *gu = first_hidden(
             chunk_blocks(blocks, chunks[0]), flip, table, gate_up, codes, quant_exps
         )
         gu = [held(value) for value in gu]
         hqs, kept, sent = [hq], {chunks[0]: None}, {}
         for chunk in chunks[1:]:
-            hq, kept[chunk], sent[chunk], *rest = next_hidden(
-                grid[2],
-                chunk_blocks(blocks, chunk),
-                [mm] if chunk == chunks[-1] else [],
-                flip, table, gu, quant_codes, quant_exps, down_rows,
+            hq, kept[chunk], sent[chunk] = next_hidden(
+                grid[2], chunk_blocks(blocks, chunk), flip, table, gu, quant_codes, quant_exps, down_rows
             )
             hqs.append(hq)
-        if len(chunks) == 1:
-            rest = last_project(grid[2], mm, down_rows)
-        kept[chunks[0]], sent[chunks[0]] = rest
+        kept[chunks[0]], sent[chunks[0]] = last_project(grid[2], mm, down_rows)
         own = reduce_to_owner(grid, group, kept, sent)
         projected, _ = gather(grid, own)
         return gram(hqs, sum((chunk_blocks(projected, chunk) for chunk in chunks), []))

time: 99.3 us -> 94.9 us (0.956)
  Pallas kernels: 32.8 us -> 29.4 us
  waiting for transfers between devices: 25.8 us -> 24.4 us
    pallas_call x1, Pallas kernels: 6.47 us -> 4.11 us  [gram(): pl.pallas_call(functools.partial(gram_kernel, 1.0 / rows ** 0.5, len(hqs)...]
    pallas_call x1 -> x2, Pallas kernels: 12.2 us -> 10.5 us  [the longest x1 9.26 us: next_hidden(): pl.pallas_call(functools.partial(next_kernel, len(blocks)), in_specs=[spe...]
    ppermute x9, waiting for transfers between devices: 16.1 us -> 14.7 us  [reduce_to_owner(): lax.ppermute(value, 'tok', shift(grid, axis, -by))]
  transfers between devices with their start and end apart: 39 -> 39, of which waited for: 14 -> 14; matrix products, arithmetic and copies ran while one was open for 0% -> 0% of each run, Pallas kernels for 14% -> 17%
where the time goes in v2:
time: 94.9 us; the launch traced here: 94.4 us
  starting transfers between devices  40 us (42%)
  Pallas kernels  29.4 us (31%)
  waiting for transfers between devices  24.4 us (26%)
    ppermute x30, starting transfers between devices, gather(): lax.ppermute(value, 'tok', shift(grid, axis, by))  34 us
    ppermute x9, waiting for transfers between devices, reduce_to_owner(): lax.ppermute(value, 'tok', shift(grid, axis, -by))  14.7 us
    ppermute x30, waiting for transfers between devices, gather(): lax.ppermute(value, 'tok', shift(grid, axis, by))  9.69 us
    pallas_call x1, Pallas kernels, next_hidden(): pl.pallas_call(functools.partial(next_kernel, len(blocks)), in_specs=[spe...  9.26 us
    pallas_call x1, Pallas kernels, first_hidden(): pl.pallas_call(functools.partial(first_kernel, len(blocks)), in_specs=[sp...  8.46 us
    ppermute x9, starting transfers between devices, reduce_to_owner(): lax.ppermute(value, 'tok', shift(grid, axis, -by))  5.98 us
    pallas_call x1, Pallas kernels, fetch(): pl.pallas_call(fetch_kernel, in_specs=[spec(pltpu.VMEM), spec(pltpu.HBM)]...  5.96 us
    pallas_call x1, Pallas kernels, gram(): pl.pallas_call(functools.partial(gram_kernel, 1.0 / rows ** 0.5, len(hqs)...  4.11 us
  transfers between devices with their start and end apart: 39, of which 14 were waited for; matrix products, arithmetic and copies ran while one was open for 0% of the time, Pallas kernels for 17%

profile of v2, /device:TPU:1, one launch (start us, length us, event | category | flops | bytes accessed | tf_op | source)
XLA Modules:
  0.0 94.4 jit_solution(3742968798838428657)
XLA Ops:
  0.0 4.1 %collective-permute-start.2 = (bf16[16,4096]{1,0:T(8,128)(2,1)}, bf16[16,4096]{1,0:T(8,128)(2,1)S(1)}, u32[]{:S(2)}, u32[]{:S(2)}) collective-permute-start(bf16[16,4096]{1,0:T(8,128)(2,1)} %refs_0_.1), channel_id=1, source_target_pairs={{0,12},{1,13},{2,14},{3,15},{4,0},{5,1},{6,2},{7,3},{8,4},{9,5},{1... | collective-permute-start | bytes 393224 | tf_op jit(solution)/shard_map/ppermute | solution.py:416
  4.6 1.5 %collective-permute-start.3 = (bf16[16,4096]{1,0:T(8,128)(2,1)}, bf16[16,4096]{1,0:T(8,128)(2,1)S(1)}, u32[]{:S(2)}, u32[]{:S(2)}) collective-permute-start(bf16[16,4096]{1,0:T(8,128)(2,1)} %refs_0_.1), channel_id=1, source_target_pairs={{0,1},{1,0},{2,3},{3,2},{4,5},{5,4},{6,7},{7,6},{8,9},{9,8},{10,11... | collective-permute-start | bytes 393224 | tf_op jit(solution)/shard_map/ppermute | solution.py:416
  6.1 1.2 %collective-permute-start.7 = (bf16[16,4096]{1,0:T(8,128)(2,1)}, bf16[16,4096]{1,0:T(8,128)(2,1)S(1)}, u32[]{:S(2)}, u32[]{:S(2)}) collective-permute-start(bf16[16,4096]{1,0:T(8,128)(2,1)} %refs_0_.1), channel_id=1, source_target_pairs={{0,2},{1,3},{2,0},{3,1},{4,6},{5,7},{6,4},{7,5},{8,10},{9,11},{10,... | collective-permute-start | bytes 393224 | tf_op jit(solution)/shard_map/ppermute | solution.py:416
  7.4 1.9 %collective-permute-start.6 = (bf16[16,4096]{1,0:T(8,128)(2,1)S(1)}, bf16[16,4096]{1,0:T(8,128)(2,1)S(1)}, u32[]{:S(2)}, u32[]{:S(2)}) collective-permute-start(bf16[16,4096]{1,0:T(8,128)(2,1)S(1)} %collective-permute-done.2._.refs_3_), channel_id=1, source_target_pairs={{0,1},{1,0},{2,3},{3,2},{4,5},{5,4},{6,7},{7,6},{8,9},{9,8},{10,11... | collective-permute-start | bytes 393224 | tf_op jit(solution)/shard_map/ppermute | solution.py:416
  9.3 1.0 %collective-permute-done.refs_1_ = bf16[16,4096]{1,0:T(8,128)(2,1)S(1)} collective-permute-done((bf16[16,4096]{1,0:T(8,128)(2,1)}, bf16[16,4096]{1,0:T(8,128)(2,1)S(1)}, u32[]{:S(2)}, u32[]{:S(2)}) %collective-permute-start) | collective-permute-done | bytes 131104 | tf_op jit(solution)/shard_map/ppermute | solution.py:416
  10.3 3.2 %collective-permute-start.4 = (bf16[16,4096]{1,0:T(8,128)(2,1)S(1)}, bf16[16,4096]{1,0:T(8,128)(2,1)S(1)}, u32[]{:S(2)}, u32[]{:S(2)}) collective-permute-start(bf16[16,4096]{1,0:T(8,128)(2,1)S(1)} %collective-permute-done.refs_1_), channel_id=1, source_target_pairs={{0,1},{1,0},{2,3},{3,2},{4,5},{5,4},{6,7},{7,6},{8,9},{9,8},{10,11... | collective-permute-start | bytes 393224 | tf_op jit(solution)/shard_map/ppermute | solution.py:416
  13.5 1.9 %collective-permute-done.1.refs_2_ = bf16[16,4096]{1,0:T(8,128)(2,1)S(1)} collective-permute-done((bf16[16,4096]{1,0:T(8,128)(2,1)}, bf16[16,4096]{1,0:T(8,128)(2,1)S(1)}, u32[]{:S(2)}, u32[]{:S(2)}) %collective-permute-start.1) | collective-permute-done | bytes 131104 | tf_op jit(solution)/shard_map/ppermute | solution.py:416
  15.4 1.2 %collective-permute-start.10 = (bf16[16,4096]{1,0:T(8,128)(2,1)S(1)}, bf16[16,4096]{1,0:T(8,128)(2,1)S(1)}, u32[]{:S(2)}, u32[]{:S(2)}) collective-permute-start(bf16[16,4096]{1,0:T(8,128)(2,1)S(1)} %collective-permute-done.2._.refs_3_), channel_id=1, source_target_pairs={{0,2},{1,3},{2,0},{3,1},{4,6},{5,7},{6,4},{7,5},{8,10},{9,11},{10,... | collective-permute-start | bytes 393224 | tf_op jit(solution)/shard_map/ppermute | solution.py:416
  16.9 1.2 %collective-permute-start.9 = (bf16[16,4096]{1,0:T(8,128)(2,1)S(1)}, bf16[16,4096]{1,0:T(8,128)(2,1)S(1)}, u32[]{:S(2)}, u32[]{:S(2)}) collective-permute-start(bf16[16,4096]{1,0:T(8,128)(2,1)S(1)} %collective-permute-done.1.refs_2_), channel_id=1, source_target_pairs={{0,2},{1,3},{2,0},{3,1},{4,6},{5,7},{6,4},{7,5},{8,10},{9,11},{10,... | collective-permute-start | bytes 393224 | tf_op jit(solution)/shard_map/ppermute | solution.py:416
  18.1 2.2 %collective-permute-start.5 = (bf16[16,4096]{1,0:T(8,128)(2,1)S(1)}, bf16[16,4096]{1,0:T(8,128)(2,1)S(1)}, u32[]{:S(2)}, u32[]{:S(2)}) collective-permute-start(bf16[16,4096]{1,0:T(8,128)(2,1)S(1)} %collective-permute-done.1.refs_2_), channel_id=1, source_target_pairs={{0,1},{1,0},{2,3},{3,2},{4,5},{5,4},{6,7},{7,6},{8,9},{9,8},{10,11... | collective-permute-start | bytes 393224 | tf_op jit(solution)/shard_map/ppermute | solution.py:416
  20.6 6.0 %fetch.1 = (bf16[1024,1024]{1,0:T(8,128)(2,1)S(1)}, bf16[1024,1024]{1,0:T(8,128)(2,1)S(1)}, bf16[1024,1024]{1,0:T(8,128)(2,1)S(1)}, bf16[1024,1024]{1,0:T(8,128)...) custom-call(bf16[16,4096]{1,0:T(8,128)(2,1)S(1)} %collective-permute, ...), custom_call_target="tpu_custom_call" | custom-call | bytes 33554432 | tf_op jit(solution)/shard_map/fetch/pallas_call | solution.py:135
  27.7 8.5 %first_hidden.1 = (bf16[128,1024]{1,0:T(8,128)(2,1)S(1)}, bf16[128,1024]{1,0:T(8,128)(2,1)S(1)}, bf16[4096,1024]{1,0:T(8,128)(2,1)S(1)}, bf16[4096,1024]{1,0:T(8,128)(2,1)S(1)}) custom-call(bf16[16,4096]{1,0:T(8,128)(2,1)S(1)} %copy-done.1, bf16[16,4096]{1,0:T(8,128)(2,1)S(1)} %collective-permute-done.refs_1_, ...), custom_call_target="tpu_custom_call" | custom-call | flops 4294967296 | bytes 16777216 | tf_op jit(solution)/shard_map/first_hidden/pallas_call | solution.py:192
  36.3 9.3 %next_hidden.1 = (bf16[128,1024]{1,0:T(8,128)(2,1)S(1)}, f32[64,4096]{1,0:T(8,128)S(1)}, bf16[64,4096]{1,0:T(8,128)(2,1)S(1)}) custom-call(bf16[16,4096]{1,0:T(8,128)(2,1)S(1)} %collective-permute-done.7.refs_0_, bf16[16,4096]{1,0:T(8,128)(2,1)S(1)} %collective-permute-done.8.refs_1_, bf16[16,4096]{1,0:T(8,128)(2,1)S(1)} %collective-permute-done.9.refs_2_, ...), custom_call_target="tpu_custom_call" | custom-call | flops 5368709120 | bytes 16777216 | tf_op jit(solution)/shard_map/next_hidden/pallas_call | solution.py:261
  45.7 1.3 %last_project.1 = (f32[64,4096]{1,0:T(8,128)S(1)}, bf16[64,4096]{1,0:T(8,128)(2,1)S(1)}) custom-call(bf16[128,1024]{1,0:T(8,128)(2,1)S(1)} %get-tuple-element.38.mm_ref, bf16[1024,4096]{1,0:T(8,128)(2,1)S(1)} %bitcast.2), custom_call_target="tpu_custom_call" | custom-call | tf_op jit(solution)/shard_map/last_project/pallas_call | solution.py:296
  48.2 1.0 %collective-permute-start.20 = (bf16[16,4096]{1,0:T(8,128)(2,1)S(1)}, bf16[16,4096]{1,0:T(8,128)(2,1)S(1)}, u32[]{:S(2)}, u32[]{:S(2)}) collective-permute-start(bf16[16,4096]{1,0:T(8,128)(2,1)S(1)} %get-tuple-element.45), channel_id=1, source_target_pairs={{0,2},{1,3},{2,0},{3,1},{4,6},{5,7},{6,4},{7,5},{8,10},{9,11},{10,... | collective-permute-start | bytes 393224 | tf_op jit(solution)/shard_map/ppermute | solution.py:431
  49.6 1.0 %collective-permute-start.17 = (bf16[16,4096]{1,0:T(8,128)(2,1)S(1)}, bf16[16,4096]{1,0:T(8,128)(2,1)S(1)}, u32[]{:S(2)}, u32[]{:S(2)}) collective-permute-start(bf16[16,4096]{1,0:T(8,128)(2,1)S(1)} %get-tuple-element.43), channel_id=1, source_target_pairs={{0,2},{1,3},{2,0},{3,1},{4,6},{5,7},{6,4},{7,5},{8,10},{9,11},{10,... | collective-permute-start | bytes 393224 | tf_op jit(solution)/shard_map/ppermute | solution.py:431
  50.6 2.0 %collective-permute-done.22.refs_1_ = bf16[16,4096]{1,0:T(8,128)(2,1)S(1)} collective-permute-done((bf16[16,4096]{1,0:T(8,128)(2,1)S(1)}, bf16[16,4096]{1,0:T(8,128)(2,1)S(1)}, u32[]{:S(2)}, u32[]{:S(2)}) %collective-permute-start.22) | collective-permute-done | bytes 131104 | tf_op jit(solution)/shard_map/ppermute | solution.py:431
  52.7 2.7 %collective-permute-done.20.refs_1_ = bf16[16,4096]{1,0:T(8,128)(2,1)S(1)} collective-permute-done((bf16[16,4096]{1,0:T(8,128)(2,1)S(1)}, bf16[16,4096]{1,0:T(8,128)(2,1)S(1)}, u32[]{:S(2)}, u32[]{:S(2)}) %collective-permute-start.20) | collective-permute-done | bytes 131104 | tf_op jit(solution)/shard_map/ppermute | solution.py:431
  55.4 2.0 %collective-permute-start.21 = (bf16[16,4096]{1,0:T(8,128)(2,1)S(1)}, bf16[16,4096]{1,0:T(8,128)(2,1)S(1)}, u32[]{:S(2)}, u32[]{:S(2)}) collective-permute-start(bf16[16,4096]{1,0:T(8,128)(2,1)S(1)} %add.5), channel_id=1, source_target_pairs={{0,12},{1,13},{2,14},{3,15},{4,0},{5,1},{6,2},{7,3},{8,4},{9,5},{1... | collective-permute-start | bytes 393224 | tf_op jit(solution)/shard_map/ppermute | solution.py:431
  57.5 0.7 collective-permute-done.18.refs_1_
  58.5 2.5 %collective-permute-done.17.refs_1_ = bf16[16,4096]{1,0:T(8,128)(2,1)S(1)} collective-permute-done((bf16[16,4096]{1,0:T(8,128)(2,1)S(1)}, bf16[16,4096]{1,0:T(8,128)(2,1)S(1)}, u32[]{:S(2)}, u32[]{:S(2)}) %collective-permute-start.17) | collective-permute-done | bytes 131104 | tf_op jit(solution)/shard_map/ppermute | solution.py:431
  61.0 0.8 collective-permute-done.21.refs_3_
  61.9 5.9 %collective-permute-done.19.refs_2_ = bf16[16,4096]{1,0:T(8,128)(2,1)S(1)} collective-permute-done((bf16[16,4096]{1,0:T(8,128)(2,1)S(1)}, bf16[16,4096]{1,0:T(8,128)(2,1)S(1)}, u32[]{:S(2)}, u32[]{:S(2)}) %collective-permute-start.19) | collective-permute-done | bytes 131104 | tf_op jit(solution)/shard_map/ppermute | solution.py:431
  67.9 2.8 %collective-permute-start.25 = (bf16[16,4096]{1,0:T(8,128)(2,1)S(1)}, bf16[16,4096]{1,0:T(8,128)(2,1)S(1)}, u32[]{:S(2)}, u32[]{:S(2)}) collective-permute-start(bf16[16,4096]{1,0:T(8,128)(2,1)S(1)} %add.7.refs_2_), channel_id=1, source_target_pairs={{0,8},{1,9},{2,10},{3,11},{4,12},{5,13},{6,14},{7,15},{8,0},{9,1},... | collective-permute-start | bytes 393224 | tf_op jit(solution)/shard_map/ppermute | solution.py:416
  71.5 1.8 %collective-permute-start.27 = (bf16[16,4096]{1,0:T(8,128)(2,1)S(1)}, bf16[16,4096]{1,0:T(8,128)(2,1)S(1)}, u32[]{:S(2)}, u32[]{:S(2)}) collective-permute-start(bf16[16,4096]{1,0:T(8,128)(2,1)S(1)} %add.7.refs_2_), channel_id=1, source_target_pairs={{0,1},{1,0},{2,3},{3,2},{4,5},{5,4},{6,7},{7,6},{8,9},{9,8},{10,11... | collective-permute-start | bytes 393224 | tf_op jit(solution)/shard_map/ppermute | solution.py:416
  73.7 0.9 collective-permute-start.32
  74.6 5.3 %collective-permute-done.25.refs_4_ = bf16[16,4096]{1,0:T(8,128)(2,1)S(1)} collective-permute-done((bf16[16,4096]{1,0:T(8,128)(2,1)S(1)}, bf16[16,4096]{1,0:T(8,128)(2,1)S(1)}, u32[]{:S(2)}, u32[]{:S(2)}) %collective-permute-start.25) | collective-permute-done | bytes 131104 | tf_op jit(solution)/shard_map/ppermute | solution.py:416
  79.9 1.1 %collective-permute-start.33 = (bf16[16,4096]{1,0:T(8,128)(2,1)S(1)}, bf16[16,4096]{1,0:T(8,128)(2,1)S(1)}, u32[]{:S(2)}, u32[]{:S(2)}) collective-permute-start(bf16[16,4096]{1,0:T(8,128)(2,1)S(1)} %collective-permute-done.25.refs_4_), channel_id=1, source_target_pairs={{0,2},{1,3},{2,0},{3,1},{4,6},{5,7},{6,4},{7,5},{8,10},{9,11},{10,... | collective-permute-start | bytes 393224 | tf_op jit(solution)/shard_map/ppermute | solution.py:416
  81.4 2.0 %collective-permute-start.28 = (bf16[16,4096]{1,0:T(8,128)(2,1)S(1)}, bf16[16,4096]{1,0:T(8,128)(2,1)S(1)}, u32[]{:S(2)}, u32[]{:S(2)}) collective-permute-start(bf16[16,4096]{1,0:T(8,128)(2,1)S(1)} %collective-permute-done.24.refs_3_), channel_id=1, source_target_pairs={{0,1},{1,0},{2,3},{3,2},{4,5},{5,4},{6,7},{7,6},{8,9},{9,8},{10,11... | collective-permute-start | bytes 393224 | tf_op jit(solution)/shard_map/ppermute | solution.py:416
  83.9 3.3 %collective-permute-start.35 = (bf16[16,4096]{1,0:T(8,128)(2,1)S(1)}, bf16[16,4096]{1,0:T(8,128)(2,1)S(1)}, u32[]{:S(2)}, u32[]{:S(2)}) collective-permute-start(bf16[16,4096]{1,0:T(8,128)(2,1)S(1)} %collective-permute-done.31.refs_10_), channel_id=1, source_target_pairs={{0,1},{1,0},{2,3},{3,2},{4,5},{5,4},{6,7},{7,6},{8,9},{9,8},{10,11... | collective-permute-start | bytes 393224 | tf_op jit(solution)/shard_map/ppermute | solution.py:416
  87.2 1.4 %collective-permute-start.36 = (bf16[16,4096]{1,0:T(8,128)(2,1)S(1)}, bf16[16,4096]{1,0:T(8,128)(2,1)S(1)}, u32[]{:S(2)}, u32[]{:S(2)}) collective-permute-start(bf16[16,4096]{1,0:T(8,128)(2,1)S(1)} %collective-permute-done.32.refs_11_), channel_id=1, source_target_pairs={{0,1},{1,0},{2,3},{3,2},{4,5},{5,4},{6,7},{7,6},{8,9},{9,8},{10,11... | collective-permute-start | bytes 393224 | tf_op jit(solution)/shard_map/ppermute | solution.py:416
  90.2 4.1 %gram.1 = bf16[1024,4096]{1,0:T(8,128)(2,1)} custom-call(bf16[128,1024]{1,0:T(8,128)(2,1)S(1)} %get-tuple-element.34.refs_0_, bf16[128,1024]{1,0:T(8,128)(2,1)S(1)} %get-tuple-element.37.refs_1_, bf16[16,4096]{1,0:T(8,128)(2,1)S(1)} %add.7.refs_2_, bf16[16,4096]{1,0:T(8,128)(2,1)S(1)} %collective-permute-done.24.refs_3_, ...), custom_call_target="tpu_custom_call" | custom-call | tf_op jit(solution)/shard_map/gram/pallas_call | solution.py:371
  (68 shorter events, 8.0 us)
Async XLA Ops:
  0.0 7.4 %collective-permute-start.2 = (bf16[16,4096]{1,0:T(8,128)(2,1)}, bf16[16,4096]{1,0:T(8,128)(2,1)S(1)}, u32[]{:S(2)}, u32[]{:S(2)}) collective-permute-start(bf16[16,4096]{1,0:T(8,128)(2,1)} %refs_0_.1), channel_id=1, source_target_pairs={{0,12},{1,13},{2,14},{3,15},{4,0},{5,1},{6,2},{7,3},{8,4},{9,5},{1... | collective-permute-start | bytes 393224 | tf_op jit(solution)/shard_map/ppermute | solution.py:416
  4.1 6.2 %collective-permute-start = (bf16[16,4096]{1,0:T(8,128)(2,1)}, bf16[16,4096]{1,0:T(8,128)(2,1)S(1)}, u32[]{:S(2)}, u32[]{:S(2)}) collective-permute-start(bf16[16,4096]{1,0:T(8,128)(2,1)} %refs_0_.1), channel_id=1, source_target_pairs={{0,4},{1,5},{2,6},{3,7},{4,8},{5,9},{6,10},{7,11},{8,12},{9,13},{1... | collective-permute-start | bytes 393224 | tf_op jit(solution)/shard_map/ppermute | solution.py:416
  4.1 11.2 %collective-permute-start.1 = (bf16[16,4096]{1,0:T(8,128)(2,1)}, bf16[16,4096]{1,0:T(8,128)(2,1)S(1)}, u32[]{:S(2)}, u32[]{:S(2)}) collective-permute-start(bf16[16,4096]{1,0:T(8,128)(2,1)} %refs_0_.1), channel_id=1, source_target_pairs={{0,8},{1,9},{2,10},{3,11},{4,12},{5,13},{6,14},{7,15},{8,0},{9,1},... | collective-permute-start | bytes 393224 | tf_op jit(solution)/shard_map/ppermute | solution.py:416
  4.6 12.0 %collective-permute-start.3 = (bf16[16,4096]{1,0:T(8,128)(2,1)}, bf16[16,4096]{1,0:T(8,128)(2,1)S(1)}, u32[]{:S(2)}, u32[]{:S(2)}) collective-permute-start(bf16[16,4096]{1,0:T(8,128)(2,1)} %refs_0_.1), channel_id=1, source_target_pairs={{0,1},{1,0},{2,3},{3,2},{4,5},{5,4},{6,7},{7,6},{8,9},{9,8},{10,11... | collective-permute-start | bytes 393224 | tf_op jit(solution)/shard_map/ppermute | solution.py:416
  6.1 10.8 %collective-permute-start.7 = (bf16[16,4096]{1,0:T(8,128)(2,1)}, bf16[16,4096]{1,0:T(8,128)(2,1)S(1)}, u32[]{:S(2)}, u32[]{:S(2)}) collective-permute-start(bf16[16,4096]{1,0:T(8,128)(2,1)} %refs_0_.1), channel_id=1, source_target_pairs={{0,2},{1,3},{2,0},{3,1},{4,6},{5,7},{6,4},{7,5},{8,10},{9,11},{10,... | collective-permute-start | bytes 393224 | tf_op jit(solution)/shard_map/ppermute | solution.py:416
  7.4 10.8 %collective-permute-start.6 = (bf16[16,4096]{1,0:T(8,128)(2,1)S(1)}, bf16[16,4096]{1,0:T(8,128)(2,1)S(1)}, u32[]{:S(2)}, u32[]{:S(2)}) collective-permute-start(bf16[16,4096]{1,0:T(8,128)(2,1)S(1)} %collective-permute-done.2._.refs_3_), channel_id=1, source_target_pairs={{0,1},{1,0},{2,3},{3,2},{4,5},{5,4},{6,7},{7,6},{8,9},{9,8},{10,11... | collective-permute-start | bytes 393224 | tf_op jit(solution)/shard_map/ppermute | solution.py:416
  10.3 16.3 %collective-permute-start.4 = (bf16[16,4096]{1,0:T(8,128)(2,1)S(1)}, bf16[16,4096]{1,0:T(8,128)(2,1)S(1)}, u32[]{:S(2)}, u32[]{:S(2)}) collective-permute-start(bf16[16,4096]{1,0:T(8,128)(2,1)S(1)} %collective-permute-done.refs_1_), channel_id=1, source_target_pairs={{0,1},{1,0},{2,3},{3,2},{4,5},{5,4},{6,7},{7,6},{8,9},{9,8},{10,11... | collective-permute-start | bytes 393224 | tf_op jit(solution)/shard_map/ppermute | solution.py:416
  15.4 11.3 %collective-permute-start.10 = (bf16[16,4096]{1,0:T(8,128)(2,1)S(1)}, bf16[16,4096]{1,0:T(8,128)(2,1)S(1)}, u32[]{:S(2)}, u32[]{:S(2)}) collective-permute-start(bf16[16,4096]{1,0:T(8,128)(2,1)S(1)} %collective-permute-done.2._.refs_3_), channel_id=1, source_target_pairs={{0,2},{1,3},{2,0},{3,1},{4,6},{5,7},{6,4},{7,5},{8,10},{9,11},{10,... | collective-permute-start | bytes 393224 | tf_op jit(solution)/shard_map/ppermute | solution.py:416
  16.6 10.6 %collective-permute-start.8 = (bf16[16,4096]{1,0:T(8,128)(2,1)S(1)}, bf16[16,4096]{1,0:T(8,128)(2,1)S(1)}, u32[]{:S(2)}, u32[]{:S(2)}) collective-permute-start(bf16[16,4096]{1,0:T(8,128)(2,1)S(1)} %collective-permute-done.refs_1_), channel_id=1, source_target_pairs={{0,2},{1,3},{2,0},{3,1},{4,6},{5,7},{6,4},{7,5},{8,10},{9,11},{10,... | collective-permute-start | bytes 393224 | tf_op jit(solution)/shard_map/ppermute | solution.py:416
  16.9 10.4 %collective-permute-start.9 = (bf16[16,4096]{1,0:T(8,128)(2,1)S(1)}, bf16[16,4096]{1,0:T(8,128)(2,1)S(1)}, u32[]{:S(2)}, u32[]{:S(2)}) collective-permute-start(bf16[16,4096]{1,0:T(8,128)(2,1)S(1)} %collective-permute-done.1.refs_2_), channel_id=1, source_target_pairs={{0,2},{1,3},{2,0},{3,1},{4,6},{5,7},{6,4},{7,5},{8,10},{9,11},{10,... | collective-permute-start | bytes 393224 | tf_op jit(solution)/shard_map/ppermute | solution.py:416
  18.1 9.6 %collective-permute-start.5 = (bf16[16,4096]{1,0:T(8,128)(2,1)S(1)}, bf16[16,4096]{1,0:T(8,128)(2,1)S(1)}, u32[]{:S(2)}, u32[]{:S(2)}) collective-permute-start(bf16[16,4096]{1,0:T(8,128)(2,1)S(1)} %collective-permute-done.1.refs_2_), channel_id=1, source_target_pairs={{0,1},{1,0},{2,3},{3,2},{4,5},{5,4},{6,7},{7,6},{8,9},{9,8},{10,11... | collective-permute-start | bytes 393224 | tf_op jit(solution)/shard_map/ppermute | solution.py:416
  26.6 9.6 %collective-permute-start.11 = (bf16[16,4096]{1,0:T(8,128)(2,1)S(1)}, bf16[16,4096]{1,0:T(8,128)(2,1)S(1)}, u32[]{:S(2)}, u32[]{:S(2)}) collective-permute-start(bf16[16,4096]{1,0:T(8,128)(2,1)S(1)} %collective-permute-done.7.refs_0_), channel_id=1, source_target_pairs={{0,1},{1,0},{2,3},{3,2},{4,5},{5,4},{6,7},{7,6},{8,9},{9,8},{10,11... | collective-permute-start | bytes 393224 | tf_op jit(solution)/shard_map/ppermute | solution.py:416
  26.7 9.5 %collective-permute-start.14 = (bf16[16,4096]{1,0:T(8,128)(2,1)S(1)}, bf16[16,4096]{1,0:T(8,128)(2,1)S(1)}, u32[]{:S(2)}, u32[]{:S(2)}) collective-permute-start(bf16[16,4096]{1,0:T(8,128)(2,1)S(1)} %collective-permute-done.10.refs_3_), channel_id=1, source_target_pairs={{0,1},{1,0},{2,3},{3,2},{4,5},{5,4},{6,7},{7,6},{8,9},{9,8},{10,11... | collective-permute-start | bytes 393224 | tf_op jit(solution)/shard_map/ppermute | solution.py:416
  27.2 9.0 %collective-permute-start.12 = (bf16[16,4096]{1,0:T(8,128)(2,1)S(1)}, bf16[16,4096]{1,0:T(8,128)(2,1)S(1)}, u32[]{:S(2)}, u32[]{:S(2)}) collective-permute-start(bf16[16,4096]{1,0:T(8,128)(2,1)S(1)} %collective-permute-done.8.refs_1_), channel_id=1, source_target_pairs={{0,1},{1,0},{2,3},{3,2},{4,5},{5,4},{6,7},{7,6},{8,9},{9,8},{10,11... | collective-permute-start | bytes 393224 | tf_op jit(solution)/shard_map/ppermute | solution.py:416
  27.3 9.0 %collective-permute-start.13 = (bf16[16,4096]{1,0:T(8,128)(2,1)S(1)}, bf16[16,4096]{1,0:T(8,128)(2,1)S(1)}, u32[]{:S(2)}, u32[]{:S(2)}) collective-permute-start(bf16[16,4096]{1,0:T(8,128)(2,1)S(1)} %collective-permute-done.9.refs_2_), channel_id=1, source_target_pairs={{0,1},{1,0},{2,3},{3,2},{4,5},{5,4},{6,7},{7,6},{8,9},{9,8},{10,11... | collective-permute-start | bytes 393224 | tf_op jit(solution)/shard_map/ppermute | solution.py:416
  48.2 7.2 %collective-permute-start.20 = (bf16[16,4096]{1,0:T(8,128)(2,1)S(1)}, bf16[16,4096]{1,0:T(8,128)(2,1)S(1)}, u32[]{:S(2)}, u32[]{:S(2)}) collective-permute-start(bf16[16,4096]{1,0:T(8,128)(2,1)S(1)} %get-tuple-element.45), channel_id=1, source_target_pairs={{0,2},{1,3},{2,0},{3,1},{4,6},{5,7},{6,4},{7,5},{8,10},{9,11},{10,... | collective-permute-start | bytes 393224 | tf_op jit(solution)/shard_map/ppermute | solution.py:431
  49.1 9.1 %collective-permute-start.18 = (bf16[16,4096]{1,0:T(8,128)(2,1)S(1)}, bf16[16,4096]{1,0:T(8,128)(2,1)S(1)}, u32[]{:S(2)}, u32[]{:S(2)}) collective-permute-start(bf16[16,4096]{1,0:T(8,128)(2,1)S(1)} %get-tuple-element.44), channel_id=1, source_target_pairs={{0,2},{1,3},{2,0},{3,1},{4,6},{5,7},{6,4},{7,5},{8,10},{9,11},{10,... | collective-permute-start | bytes 393224 | tf_op jit(solution)/shard_map/ppermute | solution.py:431
  49.6 11.4 %collective-permute-start.17 = (bf16[16,4096]{1,0:T(8,128)(2,1)S(1)}, bf16[16,4096]{1,0:T(8,128)(2,1)S(1)}, u32[]{:S(2)}, u32[]{:S(2)}) collective-permute-start(bf16[16,4096]{1,0:T(8,128)(2,1)S(1)} %get-tuple-element.43), channel_id=1, source_target_pairs={{0,2},{1,3},{2,0},{3,1},{4,6},{5,7},{6,4},{7,5},{8,10},{9,11},{10,... | collective-permute-start | bytes 393224 | tf_op jit(solution)/shard_map/ppermute | solution.py:431
  52.6 8.4 %collective-permute-start.23 = (bf16[16,4096]{1,0:T(8,128)(2,1)S(1)}, bf16[16,4096]{1,0:T(8,128)(2,1)S(1)}, u32[]{:S(2)}, u32[]{:S(2)}) collective-permute-start(bf16[16,4096]{1,0:T(8,128)(2,1)S(1)} %add.6), channel_id=1, source_target_pairs={{0,4},{1,5},{2,6},{3,7},{4,8},{5,9},{6,10},{7,11},{8,12},{9,13},{1... | collective-permute-start | bytes 393224 | tf_op jit(solution)/shard_map/ppermute | solution.py:431
  55.4 6.4 %collective-permute-start.21 = (bf16[16,4096]{1,0:T(8,128)(2,1)S(1)}, bf16[16,4096]{1,0:T(8,128)(2,1)S(1)}, u32[]{:S(2)}, u32[]{:S(2)}) collective-permute-start(bf16[16,4096]{1,0:T(8,128)(2,1)S(1)} %add.5), channel_id=1, source_target_pairs={{0,12},{1,13},{2,14},{3,15},{4,0},{5,1},{6,2},{7,3},{8,4},{9,5},{1... | collective-permute-start | bytes 393224 | tf_op jit(solution)/shard_map/ppermute | solution.py:431
  58.3 9.5 %collective-permute-start.19 = (bf16[16,4096]{1,0:T(8,128)(2,1)S(1)}, bf16[16,4096]{1,0:T(8,128)(2,1)S(1)}, u32[]{:S(2)}, u32[]{:S(2)}) collective-permute-start(bf16[16,4096]{1,0:T(8,128)(2,1)S(1)} %add.4), channel_id=1, source_target_pairs={{0,8},{1,9},{2,10},{3,11},{4,12},{5,13},{6,14},{7,15},{8,0},{9,1},... | collective-permute-start | bytes 393224 | tf_op jit(solution)/shard_map/ppermute | solution.py:431
  67.9 5.8 %collective-permute-start.24 = (bf16[16,4096]{1,0:T(8,128)(2,1)S(1)}, bf16[16,4096]{1,0:T(8,128)(2,1)S(1)}, u32[]{:S(2)}, u32[]{:S(2)}) collective-permute-start(bf16[16,4096]{1,0:T(8,128)(2,1)S(1)} %add.7.refs_2_), channel_id=1, source_target_pairs={{0,4},{1,5},{2,6},{3,7},{4,8},{5,9},{6,10},{7,11},{8,12},{9,13},{1... | collective-permute-start | bytes 393224 | tf_op jit(solution)/shard_map/ppermute | solution.py:416
  67.9 11.9 %collective-permute-start.25 = (bf16[16,4096]{1,0:T(8,128)(2,1)S(1)}, bf16[16,4096]{1,0:T(8,128)(2,1)S(1)}, u32[]{:S(2)}, u32[]{:S(2)}) collective-permute-start(bf16[16,4096]{1,0:T(8,128)(2,1)S(1)} %add.7.refs_2_), channel_id=1, source_target_pairs={{0,8},{1,9},{2,10},{3,11},{4,12},{5,13},{6,14},{7,15},{8,0},{9,1},... | collective-permute-start | bytes 393224 | tf_op jit(solution)/shard_map/ppermute | solution.py:416
  70.8 10.3 %collective-permute-start.26 = (bf16[16,4096]{1,0:T(8,128)(2,1)S(1)}, bf16[16,4096]{1,0:T(8,128)(2,1)S(1)}, u32[]{:S(2)}, u32[]{:S(2)}) collective-permute-start(bf16[16,4096]{1,0:T(8,128)(2,1)S(1)} %add.7.refs_2_), channel_id=1, source_target_pairs={{0,12},{1,13},{2,14},{3,15},{4,0},{5,1},{6,2},{7,3},{8,4},{9,5},{1... | collective-permute-start | bytes 393224 | tf_op jit(solution)/shard_map/ppermute | solution.py:416
  71.2 10.2 %collective-permute-start.31 = (bf16[16,4096]{1,0:T(8,128)(2,1)S(1)}, bf16[16,4096]{1,0:T(8,128)(2,1)S(1)}, u32[]{:S(2)}, u32[]{:S(2)}) collective-permute-start(bf16[16,4096]{1,0:T(8,128)(2,1)S(1)} %add.7.refs_2_), channel_id=1, source_target_pairs={{0,2},{1,3},{2,0},{3,1},{4,6},{5,7},{6,4},{7,5},{8,10},{9,11},{10,... | collective-permute-start | bytes 393224 | tf_op jit(solution)/shard_map/ppermute | solution.py:416
  71.5 11.9 %collective-permute-start.27 = (bf16[16,4096]{1,0:T(8,128)(2,1)S(1)}, bf16[16,4096]{1,0:T(8,128)(2,1)S(1)}, u32[]{:S(2)}, u32[]{:S(2)}) collective-permute-start(bf16[16,4096]{1,0:T(8,128)(2,1)S(1)} %add.7.refs_2_), channel_id=1, source_target_pairs={{0,1},{1,0},{2,3},{3,2},{4,5},{5,4},{6,7},{7,6},{8,9},{9,8},{10,11... | collective-permute-start | bytes 393224 | tf_op jit(solution)/shard_map/ppermute | solution.py:416
  73.7 9.8 %collective-permute-start.32 = (bf16[16,4096]{1,0:T(8,128)(2,1)S(1)}, bf16[16,4096]{1,0:T(8,128)(2,1)S(1)}, u32[]{:S(2)}, u32[]{:S(2)}) collective-permute-start(bf16[16,4096]{1,0:T(8,128)(2,1)S(1)} %collective-permute-done.24.refs_3_), channel_id=1, source_target_pairs={{0,2},{1,3},{2,0},{3,1},{4,6},{5,7},{6,4},{7,5},{8,10},{9,11},{10,... | collective-permute-start | bytes 393224 | tf_op jit(solution)/shard_map/ppermute | solution.py:416
  81.0 6.2 %collective-permute-start.34 = (bf16[16,4096]{1,0:T(8,128)(2,1)S(1)}, bf16[16,4096]{1,0:T(8,128)(2,1)S(1)}, u32[]{:S(2)}, u32[]{:S(2)}) collective-permute-start(bf16[16,4096]{1,0:T(8,128)(2,1)S(1)} %collective-permute-done.26.refs_5_), channel_id=1, source_target_pairs={{0,2},{1,3},{2,0},{3,1},{4,6},{5,7},{6,4},{7,5},{8,10},{9,11},{10,... | collective-permute-start | bytes 393224 | tf_op jit(solution)/shard_map/ppermute | solution.py:416
  81.4 7.3 %collective-permute-start.28 = (bf16[16,4096]{1,0:T(8,128)(2,1)S(1)}, bf16[16,4096]{1,0:T(8,128)(2,1)S(1)}, u32[]{:S(2)}, u32[]{:S(2)}) collective-permute-start(bf16[16,4096]{1,0:T(8,128)(2,1)S(1)} %collective-permute-done.24.refs_3_), channel_id=1, source_target_pairs={{0,1},{1,0},{2,3},{3,2},{4,5},{5,4},{6,7},{7,6},{8,9},{9,8},{10,11... | collective-permute-start | bytes 393224 | tf_op jit(solution)/shard_map/ppermute | solution.py:416
  83.4 5.2 %collective-permute-start.29 = (bf16[16,4096]{1,0:T(8,128)(2,1)S(1)}, bf16[16,4096]{1,0:T(8,128)(2,1)S(1)}, u32[]{:S(2)}, u32[]{:S(2)}) collective-permute-start(bf16[16,4096]{1,0:T(8,128)(2,1)S(1)} %collective-permute-done.25.refs_4_), channel_id=1, source_target_pairs={{0,1},{1,0},{2,3},{3,2},{4,5},{5,4},{6,7},{7,6},{8,9},{9,8},{10,11... | collective-permute-start | bytes 393224 | tf_op jit(solution)/shard_map/ppermute | solution.py:416
  83.5 5.7 %collective-permute-start.30 = (bf16[16,4096]{1,0:T(8,128)(2,1)S(1)}, bf16[16,4096]{1,0:T(8,128)(2,1)S(1)}, u32[]{:S(2)}, u32[]{:S(2)}) collective-permute-start(bf16[16,4096]{1,0:T(8,128)(2,1)S(1)} %collective-permute-done.26.refs_5_), channel_id=1, source_target_pairs={{0,1},{1,0},{2,3},{3,2},{4,5},{5,4},{6,7},{7,6},{8,9},{9,8},{10,11... | collective-permute-start | bytes 393224 | tf_op jit(solution)/shard_map/ppermute | solution.py:416
  83.9 5.2 %collective-permute-start.35 = (bf16[16,4096]{1,0:T(8,128)(2,1)S(1)}, bf16[16,4096]{1,0:T(8,128)(2,1)S(1)}, u32[]{:S(2)}, u32[]{:S(2)}) collective-permute-start(bf16[16,4096]{1,0:T(8,128)(2,1)S(1)} %collective-permute-done.31.refs_10_), channel_id=1, source_target_pairs={{0,1},{1,0},{2,3},{3,2},{4,5},{5,4},{6,7},{7,6},{8,9},{9,8},{10,11... | collective-permute-start | bytes 393224 | tf_op jit(solution)/shard_map/ppermute | solution.py:416
  (12 other events, 58.3 us)

commit v3 on v2

--- a/solution.py
+++ b/solution.py
@@ -146,11 +146,23 @@
     )(after, pltpu.with_memory_space_constraint(weights, pltpu.HBM))
 
 
-def project(mm_ref, down_ref, keep_ref, send_ref):
-    total = jnp.dot(mm_ref[...], down_ref[...], preferred_element_type=F32)
-    own = keep_ref.shape[0]
-    keep_ref[...] = total[:own]
-    send_ref[...] = total[own:].astype(BF16)
+def column_parts(width):
+    return 2 if width % 256 == 0 else 1
+
+
+def project(mm_ref, down_ref, keeps, sends):
+    own, columns = keeps[0].shape
+    for k, (keep_ref, send_ref) in enumerate(zip(keeps, sends)):
+        down = down_ref[:, k * columns : (k + 1) * columns]
+        total = jnp.dot(mm_ref[...], down, preferred_element_type=F32)
+        keep_ref[...] = total[:own]
+        send_ref[...] = total[own:].astype(BF16)
+
+
+def project_shapes(rows, own, width):
+    parts = column_parts(width)
+    columns = width // parts
+    return [shaped((own, columns), F32)] * parts + [shaped((rows - own, columns), BF16)] * parts
 
 
 def first_kernel(count, *refs):
@@ -219,8 +231,8 @@
 def next_kernel(count, *refs):
     blocks, refs = refs[:count], refs[count:]
     flip_ref, table_ref, *gu_refs, qe_ref, down_ref, qc_hbm = refs[:7]
-    hq_ref, keep_ref, send_ref = refs[7:10]
-    tok_ref, rot_ref, mixed_ref, mm_ref, qc_ref, qc_sem = refs[10:]
+    hq_ref, *outs = refs[7:-6]
+    tok_ref, rot_ref, mixed_ref, mm_ref, qc_ref, qc_sem = refs[-6:]
     units = hq_ref.shape[1]
     step = min(256, units)
 
@@ -249,7 +261,7 @@
         def _():
             codes(block + slots).start()
 
-    project(mm_ref, down_ref, keep_ref, send_ref)
+    project(mm_ref, down_ref, outs[: len(outs) // 2], outs[len(outs) // 2 :])
 
 
 def next_hidden(cores, blocks, flip, table, gate_up, codes, exps, down):
@@ -261,12 +273,8 @@
     return pl.pallas_call(
         functools.partial(next_kernel, len(blocks)),
         in_specs=[spec(pltpu.VMEM)] * (len(blocks) + 6) + [spec(pltpu.HBM)],
-        out_specs=[spec(pltpu.VMEM)] * 3,
-        out_shape=[
-            shaped((rows, units), BF16),
-            shaped((own, width), F32),
-            shaped((rows - own, width), BF16),
-        ],
+        out_specs=[spec(pltpu.VMEM)] * (1 + 2 * column_parts(width)),
+        out_shape=[shaped((rows, units), BF16)] + project_shapes(rows, own, width),
         scratch_shapes=[
             pltpu.VMEM((rows, depth), BF16),
             pltpu.VMEM((rows, depth), BF16),
@@ -286,18 +294,17 @@
     )
 
 
-def last_kernel(mm_ref, down_ref, keep_ref, send_ref):
-    project(mm_ref, down_ref, keep_ref, send_ref)
+def last_kernel(mm_ref, down_ref, *outs):
+    project(mm_ref, down_ref, outs[: len(outs) // 2], outs[len(outs) // 2 :])
 
 
 def last_project(cores, mm, down):
     rows, (units, width) = mm.shape[0], down.shape
-    own = rows // cores
     return pl.pallas_call(
         last_kernel,
         in_specs=[spec(pltpu.VMEM)] * 2,
-        out_specs=[spec(pltpu.VMEM)] * 2,
-        out_shape=[shaped((own, width), F32), shaped((rows - own, width), BF16)],
+        out_specs=[spec(pltpu.VMEM)] * (2 * column_parts(width)),
+        out_shape=project_shapes(rows, rows // cores, width),
         compiler_params=params(4),
         name="last_project",
     )(mm, down)
@@ -346,43 +353,46 @@
     )(keep, *received, *blocks)
 
 
-def gram_kernel(scale, parts, *refs):
-    hqs, blocks = refs[:parts], refs[parts:-6]
+def gram_kernel(scale, parts, part, *refs):
+    hqs, blocks = refs[:parts], refs[parts : -6 - (part > 0)]
     o_hbm, hq_ref, turned_ref, proj_ref, o_ref, sem = refs[-6:]
     stack(hqs, hq_ref)
     stack(blocks, proj_ref)
     turned_ref[...] = hq_ref[...].T
-    units = turned_ref.shape[0]
+    units, columns = o_ref.shape
     step = min(256, units)
     copies = []
     for k in range(units // step):
         cut = pl.ds(k * step, step)
         gram = jnp.dot(turned_ref[cut, :], proj_ref[...], preferred_element_type=F32)
         o_ref[cut, :] = (gram * scale).astype(BF16)
-        copies.append(pltpu.make_async_copy(o_ref.at[cut], o_hbm.at[cut], sem.at[k]))
+        target = o_hbm.at[cut, pl.ds(part * columns, columns)]
+        copies.append(pltpu.make_async_copy(o_ref.at[cut], target, sem.at[k]))
         copies[-1].start()
     for copy in copies:
         copy.wait()
 
 
-def gram(hqs, blocks):
+def gram(hqs, blocks, width, part, made):
     rows = sum(hq.shape[0] for hq in hqs)
-    units, out = hqs[0].shape[1], blocks[0].shape[1]
-    return pl.pallas_call(
-        functools.partial(gram_kernel, 1.0 / rows**0.5, len(hqs)),
-        in_specs=[spec(pltpu.VMEM)] * (len(hqs) + len(blocks)),
+    units, columns = hqs[0].shape[1], blocks[0].shape[1]
+    count = len(hqs) + len(blocks)
+    return pl.pallas_call(
+        functools.partial(gram_kernel, 1.0 / rows**0.5, len(hqs), part),
+        in_specs=[spec(pltpu.VMEM)] * count + [spec(pltpu.HBM)] * len(made),
         out_specs=spec(pltpu.HBM),
-        out_shape=shaped((units, out), BF16),
+        out_shape=shaped((units, width), BF16),
+        input_output_aliases={count: 0} if made else {},
         scratch_shapes=[
             pltpu.VMEM((rows, units), BF16),
             pltpu.VMEM((units, rows), BF16),
-            pltpu.VMEM((rows, out), BF16),
-            pltpu.VMEM((units, out), BF16),
+            pltpu.VMEM((rows, columns), BF16),
+            pltpu.VMEM((units, columns), BF16),
             pltpu.SemaphoreType.DMA((units // min(256, units),)),
         ],
-        compiler_params=params(24),
+        compiler_params=params(20),
         name="gram",
-    )(*hqs, *blocks)
+    )(*hqs, *blocks, *made)
 
 
 def grid_of(mesh):
@@ -472,16 +482,25 @@
             chunk_blocks(blocks, chunks[0]), flip, table, gate_up, codes, quant_exps
         )
         gu = [held(value) for value in gu]
-        hqs, kept, sent = [hq], {chunks[0]: None}, {}
+        hqs, outs = [hq], {chunks[0]: None}
         for chunk in chunks[1:]:
-            hq, kept[chunk], sent[chunk] = next_hidden(
+            hq, *outs[chunk] = next_hidden(
                 grid[2], chunk_blocks(blocks, chunk), flip, table, gu, quant_codes, quant_exps, down_rows
             )
             hqs.append(hq)
-        kept[chunks[0]], sent[chunks[0]] = last_project(grid[2], mm, down_rows)
-        own = reduce_to_owner(grid, group, kept, sent)
-        projected, _ = gather(grid, own)
-        return gram(hqs, sum((chunk_blocks(projected, chunk) for chunk in chunks), []))
+        outs[chunks[0]] = last_project(grid[2], mm, down_rows)
+        out_width = down_rows.shape[1]
+        parts = column_parts(out_width)
+        owned, made = [], []
+        for part in range(parts):
+            kept = {chunk: outs[chunk][part] for chunk in chunks}
+            sent = {chunk: outs[chunk][parts + part] for chunk in chunks}
+            owned.append(reduce_to_owner(grid, group, kept, sent))
+        for part, own in enumerate(owned):
+            projected, _ = gather(grid, own)
+            pieces = sum((chunk_blocks(projected, chunk) for chunk in chunks), [])
+            made = [gram(hqs, pieces, out_width, part, made)]
+        return made[0]
 
     placed = (
         P(("dom", "tok"), None),

time: 94.9 us -> 102 us (1.075)
  starting transfers between devices: 40 us -> 60.7 us
  waiting for transfers between devices: 24.4 us -> 9.72 us
    ppermute x30 -> x45, starting transfers between devices: 34 us -> 48.5 us  [gather(): lax.ppermute(value, 'tok', shift(grid, axis, by))]
    ppermute x9 -> x18, waiting for transfers between devices: 14.7 us -> 6.45 us  [reduce_to_owner(): lax.ppermute(value, 'tok', shift(grid, axis, -by))]
    ppermute x30 -> x45, waiting for transfers between devices: 9.69 us -> 3.27 us  [gather(): lax.ppermute(value, 'tok', shift(grid, axis, by))]
    ppermute x9 -> x18, starting transfers between devices: 5.98 us -> 12.2 us  [reduce_to_owner(): lax.ppermute(value, 'tok', shift(grid, axis, -by))]
    pallas_call x1 -> x2, Pallas kernels: 4.11 us -> 5.02 us  [gram(): pl.pallas_call(functools.partial(gram_kernel, 1.0 / rows ** 0.5, len(hqs)...]
  transfers between devices with their start and end apart: 39 -> 63, of which waited for: 14 -> 10; matrix products, arithmetic and copies ran while one was open for 0% -> 0% of each run, Pallas kernels for 17% -> 18%
where the time goes in v3:
time: 102 us
  starting transfers between devices  60.7 us (60%)
  Pallas kernels  30.3 us (30%)
  waiting for transfers between devices  9.72 us (10%)
    ppermute x45, starting transfers between devices, gather(): lax.ppermute(value, 'tok', shift(grid, axis, by))  48.5 us
    ppermute x18, starting transfers between devices, reduce_to_owner(): lax.ppermute(value, 'tok', shift(grid, axis, -by))  12.2 us
    pallas_call x1, Pallas kernels, next_hidden(): pl.pallas_call(functools.partial(next_kernel, len(blocks)), in_specs=[spe...  9.26 us
    pallas_call x1, Pallas kernels, first_hidden(): pl.pallas_call(functools.partial(first_kernel, len(blocks)), in_specs=[sp...  8.46 us
    ppermute x18, waiting for transfers between devices, reduce_to_owner(): lax.ppermute(value, 'tok', shift(grid, axis, -by))  6.45 us
    pallas_call x1, Pallas kernels, fetch(): pl.pallas_call(fetch_kernel, in_specs=[spec(pltpu.VMEM), spec(pltpu.HBM)]...  5.96 us
    pallas_call x2, Pallas kernels, gram(): pl.pallas_call(functools.partial(gram_kernel, 1.0 / rows ** 0.5, len(hqs)...  5.02 us
    ppermute x45, waiting for transfers between devices, gather(): lax.ppermute(value, 'tok', shift(grid, axis, by))  3.27 us
  transfers between devices with their start and end apart: 63, of which 10 were waited for; matrix products, arithmetic and copies ran while one was open for 0% of the time, Pallas kernels for 18%

profile of v3, /device:TPU:1, one launch (start us, length us, event | category | flops | bytes accessed | tf_op | source)
XLA Modules:
  0.0 101.5 jit_solution(10014582369977532704)
XLA Ops:
  0.0 4.1 %collective-permute-start.2 = (bf16[16,4096]{1,0:T(8,128)(2,1)}, bf16[16,4096]{1,0:T(8,128)(2,1)S(1)}, u32[]{:S(2)}, u32[]{:S(2)}) collective-permute-start(bf16[16,4096]{1,0:T(8,128)(2,1)} %refs_0_.1), channel_id=1, source_target_pairs={{0,12},{1,13},{2,14},{3,15},{4,0},{5,1},{6,2},{7,3},{8,4},{9,5},{1... | collective-permute-start | bytes 393224 | tf_op jit(solution)/shard_map/ppermute | solution.py:426
  4.6 1.5 %collective-permute-start.3 = (bf16[16,4096]{1,0:T(8,128)(2,1)}, bf16[16,4096]{1,0:T(8,128)(2,1)S(1)}, u32[]{:S(2)}, u32[]{:S(2)}) collective-permute-start(bf16[16,4096]{1,0:T(8,128)(2,1)} %refs_0_.1), channel_id=1, source_target_pairs={{0,1},{1,0},{2,3},{3,2},{4,5},{5,4},{6,7},{7,6},{8,9},{9,8},{10,11... | collective-permute-start | bytes 393224 | tf_op jit(solution)/shard_map/ppermute | solution.py:426
  6.1 1.2 %collective-permute-start.7 = (bf16[16,4096]{1,0:T(8,128)(2,1)}, bf16[16,4096]{1,0:T(8,128)(2,1)S(1)}, u32[]{:S(2)}, u32[]{:S(2)}) collective-permute-start(bf16[16,4096]{1,0:T(8,128)(2,1)} %refs_0_.1), channel_id=1, source_target_pairs={{0,2},{1,3},{2,0},{3,1},{4,6},{5,7},{6,4},{7,5},{8,10},{9,11},{10,... | collective-permute-start | bytes 393224 | tf_op jit(solution)/shard_map/ppermute | solution.py:426
  7.4 1.9 %collective-permute-start.6 = (bf16[16,4096]{1,0:T(8,128)(2,1)S(1)}, bf16[16,4096]{1,0:T(8,128)(2,1)S(1)}, u32[]{:S(2)}, u32[]{:S(2)}) collective-permute-start(bf16[16,4096]{1,0:T(8,128)(2,1)S(1)} %collective-permute-done.2._.refs_3_), channel_id=1, source_target_pairs={{0,1},{1,0},{2,3},{3,2},{4,5},{5,4},{6,7},{7,6},{8,9},{9,8},{10,11... | collective-permute-start | bytes 393224 | tf_op jit(solution)/shard_map/ppermute | solution.py:426
  9.3 1.0 %collective-permute-done.refs_1_ = bf16[16,4096]{1,0:T(8,128)(2,1)S(1)} collective-permute-done((bf16[16,4096]{1,0:T(8,128)(2,1)}, bf16[16,4096]{1,0:T(8,128)(2,1)S(1)}, u32[]{:S(2)}, u32[]{:S(2)}) %collective-permute-start) | collective-permute-done | bytes 131104 | tf_op jit(solution)/shard_map/ppermute | solution.py:426
  10.3 3.2 %collective-permute-start.4 = (bf16[16,4096]{1,0:T(8,128)(2,1)S(1)}, bf16[16,4096]{1,0:T(8,128)(2,1)S(1)}, u32[]{:S(2)}, u32[]{:S(2)}) collective-permute-start(bf16[16,4096]{1,0:T(8,128)(2,1)S(1)} %collective-permute-done.refs_1_), channel_id=1, source_target_pairs={{0,1},{1,0},{2,3},{3,2},{4,5},{5,4},{6,7},{7,6},{8,9},{9,8},{10,11... | collective-permute-start | bytes 393224 | tf_op jit(solution)/shard_map/ppermute | solution.py:426
  13.5 1.9 %collective-permute-done.1.refs_2_ = bf16[16,4096]{1,0:T(8,128)(2,1)S(1)} collective-permute-done((bf16[16,4096]{1,0:T(8,128)(2,1)}, bf16[16,4096]{1,0:T(8,128)(2,1)S(1)}, u32[]{:S(2)}, u32[]{:S(2)}) %collective-permute-start.1) | collective-permute-done | bytes 131104 | tf_op jit(solution)/shard_map/ppermute | solution.py:426
  15.4 1.2 %collective-permute-start.10 = (bf16[16,4096]{1,0:T(8,128)(2,1)S(1)}, bf16[16,4096]{1,0:T(8,128)(2,1)S(1)}, u32[]{:S(2)}, u32[]{:S(2)}) collective-permute-start(bf16[16,4096]{1,0:T(8,128)(2,1)S(1)} %collective-permute-done.2._.refs_3_), channel_id=1, source_target_pairs={{0,2},{1,3},{2,0},{3,1},{4,6},{5,7},{6,4},{7,5},{8,10},{9,11},{10,... | collective-permute-start | bytes 393224 | tf_op jit(solution)/shard_map/ppermute | solution.py:426
  16.9 1.2 %collective-permute-start.9 = (bf16[16,4096]{1,0:T(8,128)(2,1)S(1)}, bf16[16,4096]{1,0:T(8,128)(2,1)S(1)}, u32[]{:S(2)}, u32[]{:S(2)}) collective-permute-start(bf16[16,4096]{1,0:T(8,128)(2,1)S(1)} %collective-permute-done.1.refs_2_), channel_id=1, source_target_pairs={{0,2},{1,3},{2,0},{3,1},{4,6},{5,7},{6,4},{7,5},{8,10},{9,11},{10,... | collective-permute-start | bytes 393224 | tf_op jit(solution)/shard_map/ppermute | solution.py:426
  18.1 2.2 %collective-permute-start.5 = (bf16[16,4096]{1,0:T(8,128)(2,1)S(1)}, bf16[16,4096]{1,0:T(8,128)(2,1)S(1)}, u32[]{:S(2)}, u32[]{:S(2)}) collective-permute-start(bf16[16,4096]{1,0:T(8,128)(2,1)S(1)} %collective-permute-done.1.refs_2_), channel_id=1, source_target_pairs={{0,1},{1,0},{2,3},{3,2},{4,5},{5,4},{6,7},{7,6},{8,9},{9,8},{10,11... | collective-permute-start | bytes 393224 | tf_op jit(solution)/shard_map/ppermute | solution.py:426
  20.6 6.0 %fetch.1 = (bf16[1024,1024]{1,0:T(8,128)(2,1)S(1)}, bf16[1024,1024]{1,0:T(8,128)(2,1)S(1)}, bf16[1024,1024]{1,0:T(8,128)(2,1)S(1)}, bf16[1024,1024]{1,0:T(8,128)...) custom-call(bf16[16,4096]{1,0:T(8,128)(2,1)S(1)} %collective-permute, ...), custom_call_target="tpu_custom_call" | custom-call | bytes 33554432 | tf_op jit(solution)/shard_map/fetch/pallas_call | solution.py:135
  27.7 8.5 %first_hidden.1 = (bf16[128,1024]{1,0:T(8,128)(2,1)S(1)}, bf16[128,1024]{1,0:T(8,128)(2,1)S(1)}, bf16[4096,1024]{1,0:T(8,128)(2,1)S(1)}, bf16[4096,1024]{1,0:T(8,128)(2,1)S(1)}) custom-call(bf16[16,4096]{1,0:T(8,128)(2,1)S(1)} %copy-done.1, bf16[16,4096]{1,0:T(8,128)(2,1)S(1)} %collective-permute-done.refs_1_, ...), custom_call_target="tpu_custom_call" | custom-call | flops 4294967296 | bytes 16777216 | tf_op jit(solution)/shard_map/first_hidden/pallas_call | solution.py:204
  36.3 9.3 %next_hidden.1 = (bf16[128,1024]{1,0:T(8,128)(2,1)S(1)}, f32[64,2048]{1,0:T(8,128)S(1)}, f32[64,2048]{1,0:T(8,128)S(1)}, bf16[64,2048]{1,0:T(8,128)(2,1)S(1)}, bf16[64,2048]{1,0:T(8,128)(2,1)S(1)}) custom-call(bf16[16,4096]{1,0:T(8,128)(2,1)S(1)} %collective-permute-done.7.refs_0_, bf16[16,4096]{1,0:T(8,128)(2,1)S(1)} %collective-permute-done.8.refs_1_, ...), custom_call_target="tpu_custom_call" | custom-call | flops 5368709120 | bytes 16777216 | tf_op jit(solution)/shard_map/next_hidden/pallas_call | solution.py:273
  46.1 1.3 %last_project.1 = (f32[64,2048]{1,0:T(8,128)S(1)}, f32[64,2048]{1,0:T(8,128)S(1)}, bf16[64,2048]{1,0:T(8,128)(2,1)S(1)}, bf16[64,2048]{1,0:T(8,128)(2,1)S(1)}) custom-call(bf16[128,1024]{1,0:T(8,128)(2,1)S(1)} %get-tuple-element.46.mm_ref, bf16[1024,4096]{1,0:T(8,128)(2,1)S(1)} %bitcast.2), custom_call_target="tpu_custom_call" | custom-call | tf_op jit(solution)/shard_map/last_project/pallas_call | solution.py:303
  50.1 1.1 %collective-permute-start.22 = (bf16[16,2048]{1,0:T(8,128)(2,1)S(1)}, bf16[16,2048]{1,0:T(8,128)(2,1)S(1)}, u32[]{:S(2)}, u32[]{:S(2)}) collective-permute-start(bf16[16,2048]{1,0:T(8,128)(2,1)S(1)} %get-tuple-element.54), channel_id=1, source_target_pairs={{0,2},{1,3},{2,0},{3,1},{4,6},{5,7},{6,4},{7,5},{8,10},{9,11},{10,... | collective-permute-start | bytes 196616 | tf_op jit(solution)/shard_map/ppermute | solution.py:441
  54.6 1.2 %collective-permute-done.22.refs_1_ = bf16[16,2048]{1,0:T(8,128)(2,1)S(1)} collective-permute-done((bf16[16,2048]{1,0:T(8,128)(2,1)S(1)}, bf16[16,2048]{1,0:T(8,128)(2,1)S(1)}, u32[]{:S(2)}, u32[]{:S(2)}) %collective-permute-start.22) | collective-permute-done | bytes 65568 | tf_op jit(solution)/shard_map/ppermute | solution.py:441
  55.9 2.0 %collective-permute-start.45 = (bf16[16,2048]{1,0:T(8,128)(2,1)S(1)}, bf16[16,2048]{1,0:T(8,128)(2,1)S(1)}, u32[]{:S(2)}, u32[]{:S(2)}) collective-permute-start(bf16[16,2048]{1,0:T(8,128)(2,1)S(1)} %add.13), channel_id=1, source_target_pairs={{0,12},{1,13},{2,14},{3,15},{4,0},{5,1},{6,2},{7,3},{8,4},{9,5},{1... | collective-permute-start | bytes 196616 | tf_op jit(solution)/shard_map/ppermute | solution.py:441
  60.5 2.9 %collective-permute-start.21 = (bf16[16,2048]{1,0:T(8,128)(2,1)S(1)}, bf16[16,2048]{1,0:T(8,128)(2,1)S(1)}, u32[]{:S(2)}, u32[]{:S(2)}) collective-permute-start(bf16[16,2048]{1,0:T(8,128)(2,1)S(1)} %add.9), channel_id=1, source_target_pairs={{0,12},{1,13},{2,14},{3,15},{4,0},{5,1},{6,2},{7,3},{8,4},{9,5},{1... | collective-permute-start | bytes 196616 | tf_op jit(solution)/shard_map/ppermute | solution.py:441
  64.0 1.9 %collective-permute-start.49 = (bf16[16,2048]{1,0:T(8,128)(2,1)S(1)}, bf16[16,2048]{1,0:T(8,128)(2,1)S(1)}, u32[]{:S(2)}, u32[]{:S(2)}) collective-permute-start(bf16[16,2048]{1,0:T(8,128)(2,1)S(1)} %add.15.refs_2_), channel_id=1, source_target_pairs={{0,8},{1,9},{2,10},{3,11},{4,12},{5,13},{6,14},{7,15},{8,0},{9,1},... | collective-permute-start | bytes 196616 | tf_op jit(solution)/shard_map/ppermute | solution.py:426
  65.9 2.3 %collective-permute-start.50 = (bf16[16,2048]{1,0:T(8,128)(2,1)S(1)}, bf16[16,2048]{1,0:T(8,128)(2,1)S(1)}, u32[]{:S(2)}, u32[]{:S(2)}) collective-permute-start(bf16[16,2048]{1,0:T(8,128)(2,1)S(1)} %add.15.refs_2_), channel_id=1, source_target_pairs={{0,12},{1,13},{2,14},{3,15},{4,0},{5,1},{6,2},{7,3},{8,4},{9,5},{1... | collective-permute-start | bytes 196616 | tf_op jit(solution)/shard_map/ppermute | solution.py:426
  68.8 1.9 %collective-permute-done.19.refs_2_ = bf16[16,2048]{1,0:T(8,128)(2,1)S(1)} collective-permute-done((bf16[16,2048]{1,0:T(8,128)(2,1)S(1)}, bf16[16,2048]{1,0:T(8,128)(2,1)S(1)}, u32[]{:S(2)}, u32[]{:S(2)}) %collective-permute-start.19) | collective-permute-done | bytes 65568 | tf_op jit(solution)/shard_map/ppermute | solution.py:441
  70.7 2.6 %collective-permute-start.51 = (bf16[16,2048]{1,0:T(8,128)(2,1)S(1)}, bf16[16,2048]{1,0:T(8,128)(2,1)S(1)}, u32[]{:S(2)}, u32[]{:S(2)}) collective-permute-start(bf16[16,2048]{1,0:T(8,128)(2,1)S(1)} %add.15.refs_2_), channel_id=1, source_target_pairs={{0,1},{1,0},{2,3},{3,2},{4,5},{5,4},{6,7},{7,6},{8,9},{9,8},{10,11... | collective-permute-start | bytes 196616 | tf_op jit(solution)/shard_map/ppermute | solution.py:426
  73.7 2.8 %collective-permute-start.25 = (bf16[16,2048]{1,0:T(8,128)(2,1)S(1)}, bf16[16,2048]{1,0:T(8,128)(2,1)S(1)}, u32[]{:S(2)}, u32[]{:S(2)}) collective-permute-start(bf16[16,2048]{1,0:T(8,128)(2,1)S(1)} %add.11.refs_2_), channel_id=1, source_target_pairs={{0,8},{1,9},{2,10},{3,11},{4,12},{5,13},{6,14},{7,15},{8,0},{9,1},... | collective-permute-start | bytes 196616 | tf_op jit(solution)/shard_map/ppermute | solution.py:426
  78.3 2.3 %collective-permute-start.27 = (bf16[16,2048]{1,0:T(8,128)(2,1)S(1)}, bf16[16,2048]{1,0:T(8,128)(2,1)S(1)}, u32[]{:S(2)}, u32[]{:S(2)}) collective-permute-start(bf16[16,2048]{1,0:T(8,128)(2,1)S(1)} %add.11.refs_2_), channel_id=1, source_target_pairs={{0,1},{1,0},{2,3},{3,2},{4,5},{5,4},{6,7},{7,6},{8,9},{9,8},{10,11... | collective-permute-start | bytes 196616 | tf_op jit(solution)/shard_map/ppermute | solution.py:426
  83.1 1.9 %collective-permute-start.52 = (bf16[16,2048]{1,0:T(8,128)(2,1)S(1)}, bf16[16,2048]{1,0:T(8,128)(2,1)S(1)}, u32[]{:S(2)}, u32[]{:S(2)}) collective-permute-start(bf16[16,2048]{1,0:T(8,128)(2,1)S(1)} %collective-permute-done.48.refs_3_), channel_id=1, source_target_pairs={{0,1},{1,0},{2,3},{3,2},{4,5},{5,4},{6,7},{7,6},{8,9},{9,8},{10,11... | collective-permute-start | bytes 196616 | tf_op jit(solution)/shard_map/ppermute | solution.py:426
  85.1 1.2 %collective-permute-start.54 = (bf16[16,2048]{1,0:T(8,128)(2,1)S(1)}, bf16[16,2048]{1,0:T(8,128)(2,1)S(1)}, u32[]{:S(2)}, u32[]{:S(2)}) collective-permute-start(bf16[16,2048]{1,0:T(8,128)(2,1)S(1)} %collective-permute-done.50.refs_5_), channel_id=1, source_target_pairs={{0,1},{1,0},{2,3},{3,2},{4,5},{5,4},{6,7},{7,6},{8,9},{9,8},{10,11... | collective-permute-start | bytes 196616 | tf_op jit(solution)/shard_map/ppermute | solution.py:426
  86.3 1.2 %collective-permute-start.59 = (bf16[16,2048]{1,0:T(8,128)(2,1)S(1)}, bf16[16,2048]{1,0:T(8,128)(2,1)S(1)}, u32[]{:S(2)}, u32[]{:S(2)}) collective-permute-start(bf16[16,2048]{1,0:T(8,128)(2,1)S(1)} %collective-permute-done.55.refs_10_), channel_id=1, source_target_pairs={{0,1},{1,0},{2,3},{3,2},{4,5},{5,4},{6,7},{7,6},{8,9},{9,8},{10,11... | collective-permute-start | bytes 196616 | tf_op jit(solution)/shard_map/ppermute | solution.py:426
  89.9 1.5 %collective-permute-start.28 = (bf16[16,2048]{1,0:T(8,128)(2,1)S(1)}, bf16[16,2048]{1,0:T(8,128)(2,1)S(1)}, u32[]{:S(2)}, u32[]{:S(2)}) collective-permute-start(bf16[16,2048]{1,0:T(8,128)(2,1)S(1)} %collective-permute-done.24.refs_3_), channel_id=1, source_target_pairs={{0,1},{1,0},{2,3},{3,2},{4,5},{5,4},{6,7},{7,6},{8,9},{9,8},{10,11... | collective-permute-start | bytes 196616 | tf_op jit(solution)/shard_map/ppermute | solution.py:426
  91.5 1.7 %collective-permute-start.60 = (bf16[16,2048]{1,0:T(8,128)(2,1)S(1)}, bf16[16,2048]{1,0:T(8,128)(2,1)S(1)}, u32[]{:S(2)}, u32[]{:S(2)}) collective-permute-start(bf16[16,2048]{1,0:T(8,128)(2,1)S(1)} %collective-permute-done.56.refs_11_), channel_id=1, source_target_pairs={{0,1},{1,0},{2,3},{3,2},{4,5},{5,4},{6,7},{7,6},{8,9},{9,8},{10,11... | collective-permute-start | bytes 196616 | tf_op jit(solution)/shard_map/ppermute | solution.py:426
  93.2 1.1 %collective-permute-start.61 = (bf16[16,2048]{1,0:T(8,128)(2,1)S(1)}, bf16[16,2048]{1,0:T(8,128)(2,1)S(1)}, u32[]{:S(2)}, u32[]{:S(2)}) collective-permute-start(bf16[16,2048]{1,0:T(8,128)(2,1)S(1)} %collective-permute-done.57.refs_12_), channel_id=1, source_target_pairs={{0,1},{1,0},{2,3},{3,2},{4,5},{5,4},{6,7},{7,6},{8,9},{9,8},{10,11... | collective-permute-start | bytes 196616 | tf_op jit(solution)/shard_map/ppermute | solution.py:426
  96.3 2.5 %gram.2.refs_18_ = bf16[1024,4096]{1,0:T(8,128)(2,1)} custom-call(bf16[128,1024]{1,0:T(8,128)(2,1)S(1)} %get-tuple-element.42.refs_0_, bf16[128,1024]{1,0:T(8,128)(2,1)S(1)} %get-tuple-element.45.refs_1_, bf16[16,2048]{1,0:T(8,128)(2,1)S(1)} %add.15.refs_2_, bf16[16,2048]{1,0:T(8,128)(2,1)S(1)} %collective-permute-done.48.refs_3_, ...), custom_call_target="tpu_custom_call" | custom-call | tf_op jit(solution)/shard_map/gram/pallas_call | solution.py:380
  98.8 2.5 %gram.3 = bf16[1024,4096]{1,0:T(8,128)(2,1)} custom-call(bf16[128,1024]{1,0:T(8,128)(2,1)S(1)} %get-tuple-element.42.refs_0_, bf16[128,1024]{1,0:T(8,128)(2,1)S(1)} %get-tuple-element.45.refs_1_, bf16[16,2048]{1,0:T(8,128)(2,1)S(1)} %add.11.refs_2_, bf16[16,2048]{1,0:T(8,128)(2,1)S(1)} %collective-permute-done.24.refs_3_, ...), custom_call_target="tpu_custom_call", output_to_operand_aliasing={{}: (18, {})} | custom-call | tf_op jit(solution)/shard_map/gram/pallas_call | solution.py:380
  (122 shorter events, 21.8 us)
Async XLA Ops:
  0.0 7.4 %collective-permute-start.2 = (bf16[16,4096]{1,0:T(8,128)(2,1)}, bf16[16,4096]{1,0:T(8,128)(2,1)S(1)}, u32[]{:S(2)}, u32[]{:S(2)}) collective-permute-start(bf16[16,4096]{1,0:T(8,128)(2,1)} %refs_0_.1), channel_id=1, source_target_pairs={{0,12},{1,13},{2,14},{3,15},{4,0},{5,1},{6,2},{7,3},{8,4},{9,5},{1... | collective-permute-start | bytes 393224 | tf_op jit(solution)/shard_map/ppermute | solution.py:426
  4.1 6.2 %collective-permute-start = (bf16[16,4096]{1,0:T(8,128)(2,1)}, bf16[16,4096]{1,0:T(8,128)(2,1)S(1)}, u32[]{:S(2)}, u32[]{:S(2)}) collective-permute-start(bf16[16,4096]{1,0:T(8,128)(2,1)} %refs_0_.1), channel_id=1, source_target_pairs={{0,4},{1,5},{2,6},{3,7},{4,8},{5,9},{6,10},{7,11},{8,12},{9,13},{1... | collective-permute-start | bytes 393224 | tf_op jit(solution)/shard_map/ppermute | solution.py:426
  4.1 11.2 %collective-permute-start.1 = (bf16[16,4096]{1,0:T(8,128)(2,1)}, bf16[16,4096]{1,0:T(8,128)(2,1)S(1)}, u32[]{:S(2)}, u32[]{:S(2)}) collective-permute-start(bf16[16,4096]{1,0:T(8,128)(2,1)} %refs_0_.1), channel_id=1, source_target_pairs={{0,8},{1,9},{2,10},{3,11},{4,12},{5,13},{6,14},{7,15},{8,0},{9,1},... | collective-permute-start | bytes 393224 | tf_op jit(solution)/shard_map/ppermute | solution.py:426
  4.6 12.0 %collective-permute-start.3 = (bf16[16,4096]{1,0:T(8,128)(2,1)}, bf16[16,4096]{1,0:T(8,128)(2,1)S(1)}, u32[]{:S(2)}, u32[]{:S(2)}) collective-permute-start(bf16[16,4096]{1,0:T(8,128)(2,1)} %refs_0_.1), channel_id=1, source_target_pairs={{0,1},{1,0},{2,3},{3,2},{4,5},{5,4},{6,7},{7,6},{8,9},{9,8},{10,11... | collective-permute-start | bytes 393224 | tf_op jit(solution)/shard_map/ppermute | solution.py:426
  6.1 10.8 %collective-permute-start.7 = (bf16[16,4096]{1,0:T(8,128)(2,1)}, bf16[16,4096]{1,0:T(8,128)(2,1)S(1)}, u32[]{:S(2)}, u32[]{:S(2)}) collective-permute-start(bf16[16,4096]{1,0:T(8,128)(2,1)} %refs_0_.1), channel_id=1, source_target_pairs={{0,2},{1,3},{2,0},{3,1},{4,6},{5,7},{6,4},{7,5},{8,10},{9,11},{10,... | collective-permute-start | bytes 393224 | tf_op jit(solution)/shard_map/ppermute | solution.py:426
  7.4 10.8 %collective-permute-start.6 = (bf16[16,4096]{1,0:T(8,128)(2,1)S(1)}, bf16[16,4096]{1,0:T(8,128)(2,1)S(1)}, u32[]{:S(2)}, u32[]{:S(2)}) collective-permute-start(bf16[16,4096]{1,0:T(8,128)(2,1)S(1)} %collective-permute-done.2._.refs_3_), channel_id=1, source_target_pairs={{0,1},{1,0},{2,3},{3,2},{4,5},{5,4},{6,7},{7,6},{8,9},{9,8},{10,11... | collective-permute-start | bytes 393224 | tf_op jit(solution)/shard_map/ppermute | solution.py:426
  10.3 16.3 %collective-permute-start.4 = (bf16[16,4096]{1,0:T(8,128)(2,1)S(1)}, bf16[16,4096]{1,0:T(8,128)(2,1)S(1)}, u32[]{:S(2)}, u32[]{:S(2)}) collective-permute-start(bf16[16,4096]{1,0:T(8,128)(2,1)S(1)} %collective-permute-done.refs_1_), channel_id=1, source_target_pairs={{0,1},{1,0},{2,3},{3,2},{4,5},{5,4},{6,7},{7,6},{8,9},{9,8},{10,11... | collective-permute-start | bytes 393224 | tf_op jit(solution)/shard_map/ppermute | solution.py:426
  15.4 11.3 %collective-permute-start.10 = (bf16[16,4096]{1,0:T(8,128)(2,1)S(1)}, bf16[16,4096]{1,0:T(8,128)(2,1)S(1)}, u32[]{:S(2)}, u32[]{:S(2)}) collective-permute-start(bf16[16,4096]{1,0:T(8,128)(2,1)S(1)} %collective-permute-done.2._.refs_3_), channel_id=1, source_target_pairs={{0,2},{1,3},{2,0},{3,1},{4,6},{5,7},{6,4},{7,5},{8,10},{9,11},{10,... | collective-permute-start | bytes 393224 | tf_op jit(solution)/shard_map/ppermute | solution.py:426
  16.6 10.6 %collective-permute-start.8 = (bf16[16,4096]{1,0:T(8,128)(2,1)S(1)}, bf16[16,4096]{1,0:T(8,128)(2,1)S(1)}, u32[]{:S(2)}, u32[]{:S(2)}) collective-permute-start(bf16[16,4096]{1,0:T(8,128)(2,1)S(1)} %collective-permute-done.refs_1_), channel_id=1, source_target_pairs={{0,2},{1,3},{2,0},{3,1},{4,6},{5,7},{6,4},{7,5},{8,10},{9,11},{10,... | collective-permute-start | bytes 393224 | tf_op jit(solution)/shard_map/ppermute | solution.py:426
  16.9 10.4 %collective-permute-start.9 = (bf16[16,4096]{1,0:T(8,128)(2,1)S(1)}, bf16[16,4096]{1,0:T(8,128)(2,1)S(1)}, u32[]{:S(2)}, u32[]{:S(2)}) collective-permute-start(bf16[16,4096]{1,0:T(8,128)(2,1)S(1)} %collective-permute-done.1.refs_2_), channel_id=1, source_target_pairs={{0,2},{1,3},{2,0},{3,1},{4,6},{5,7},{6,4},{7,5},{8,10},{9,11},{10,... | collective-permute-start | bytes 393224 | tf_op jit(solution)/shard_map/ppermute | solution.py:426
  18.1 9.6 %collective-permute-start.5 = (bf16[16,4096]{1,0:T(8,128)(2,1)S(1)}, bf16[16,4096]{1,0:T(8,128)(2,1)S(1)}, u32[]{:S(2)}, u32[]{:S(2)}) collective-permute-start(bf16[16,4096]{1,0:T(8,128)(2,1)S(1)} %collective-permute-done.1.refs_2_), channel_id=1, source_target_pairs={{0,1},{1,0},{2,3},{3,2},{4,5},{5,4},{6,7},{7,6},{8,9},{9,8},{10,11... | collective-permute-start | bytes 393224 | tf_op jit(solution)/shard_map/ppermute | solution.py:426
  26.6 9.6 %collective-permute-start.11 = (bf16[16,4096]{1,0:T(8,128)(2,1)S(1)}, bf16[16,4096]{1,0:T(8,128)(2,1)S(1)}, u32[]{:S(2)}, u32[]{:S(2)}) collective-permute-start(bf16[16,4096]{1,0:T(8,128)(2,1)S(1)} %collective-permute-done.7.refs_0_), channel_id=1, source_target_pairs={{0,1},{1,0},{2,3},{3,2},{4,5},{5,4},{6,7},{7,6},{8,9},{9,8},{10,11... | collective-permute-start | bytes 393224 | tf_op jit(solution)/shard_map/ppermute | solution.py:426
  26.7 9.5 %collective-permute-start.14 = (bf16[16,4096]{1,0:T(8,128)(2,1)S(1)}, bf16[16,4096]{1,0:T(8,128)(2,1)S(1)}, u32[]{:S(2)}, u32[]{:S(2)}) collective-permute-start(bf16[16,4096]{1,0:T(8,128)(2,1)S(1)} %collective-permute-done.10.refs_3_), channel_id=1, source_target_pairs={{0,1},{1,0},{2,3},{3,2},{4,5},{5,4},{6,7},{7,6},{8,9},{9,8},{10,11... | collective-permute-start | bytes 393224 | tf_op jit(solution)/shard_map/ppermute | solution.py:426
  27.2 9.0 %collective-permute-start.12 = (bf16[16,4096]{1,0:T(8,128)(2,1)S(1)}, bf16[16,4096]{1,0:T(8,128)(2,1)S(1)}, u32[]{:S(2)}, u32[]{:S(2)}) collective-permute-start(bf16[16,4096]{1,0:T(8,128)(2,1)S(1)} %collective-permute-done.8.refs_1_), channel_id=1, source_target_pairs={{0,1},{1,0},{2,3},{3,2},{4,5},{5,4},{6,7},{7,6},{8,9},{9,8},{10,11... | collective-permute-start | bytes 393224 | tf_op jit(solution)/shard_map/ppermute | solution.py:426
  27.3 9.0 %collective-permute-start.13 = (bf16[16,4096]{1,0:T(8,128)(2,1)S(1)}, bf16[16,4096]{1,0:T(8,128)(2,1)S(1)}, u32[]{:S(2)}, u32[]{:S(2)}) collective-permute-start(bf16[16,4096]{1,0:T(8,128)(2,1)S(1)} %collective-permute-done.9.refs_2_), channel_id=1, source_target_pairs={{0,1},{1,0},{2,3},{3,2},{4,5},{5,4},{6,7},{7,6},{8,9},{9,8},{10,11... | collective-permute-start | bytes 393224 | tf_op jit(solution)/shard_map/ppermute | solution.py:426
  47.5 6.1 %collective-permute-start.15 = (bf16[64,2048]{1,0:T(8,128)(2,1)S(1)}, bf16[64,2048]{1,0:T(8,128)(2,1)S(1)}, u32[]{:S(2)}, u32[]{:S(2)}) collective-permute-start(bf16[64,2048]{1,0:T(8,128)(2,1)S(1)} %get-tuple-element.48), channel_id=1, source_target_pairs={{0,1},{1,0},{2,3},{3,2},{4,5},{5,4},{6,7},{7,6},{8,9},{9,8},{10,11... | collective-permute-start | bytes 786440 | tf_op jit(solution)/shard_map/ppermute | solution.py:441
  51.6 6.3 %collective-permute-start.20 = (bf16[16,2048]{1,0:T(8,128)(2,1)S(1)}, bf16[16,2048]{1,0:T(8,128)(2,1)S(1)}, u32[]{:S(2)}, u32[]{:S(2)}) collective-permute-start(bf16[16,2048]{1,0:T(8,128)(2,1)S(1)} %get-tuple-element.53), channel_id=1, source_target_pairs={{0,2},{1,3},{2,0},{3,1},{4,6},{5,7},{6,4},{7,5},{8,10},{9,11},{10,... | collective-permute-start | bytes 196616 | tf_op jit(solution)/shard_map/ppermute | solution.py:441
  53.7 6.4 %collective-permute-start.41 = (bf16[16,2048]{1,0:T(8,128)(2,1)S(1)}, bf16[16,2048]{1,0:T(8,128)(2,1)S(1)}, u32[]{:S(2)}, u32[]{:S(2)}) collective-permute-start(bf16[16,2048]{1,0:T(8,128)(2,1)S(1)} %get-tuple-element.59), channel_id=1, source_target_pairs={{0,2},{1,3},{2,0},{3,1},{4,6},{5,7},{6,4},{7,5},{8,10},{9,11},{10,... | collective-permute-start | bytes 196616 | tf_op jit(solution)/shard_map/ppermute | solution.py:441
  54.6 5.9 %collective-permute-start.47 = (bf16[16,2048]{1,0:T(8,128)(2,1)S(1)}, bf16[16,2048]{1,0:T(8,128)(2,1)S(1)}, u32[]{:S(2)}, u32[]{:S(2)}) collective-permute-start(bf16[16,2048]{1,0:T(8,128)(2,1)S(1)} %add.14), channel_id=1, source_target_pairs={{0,4},{1,5},{2,6},{3,7},{4,8},{5,9},{6,10},{7,11},{8,12},{9,13},{1... | collective-permute-start | bytes 196616 | tf_op jit(solution)/shard_map/ppermute | solution.py:441
  55.9 7.5 %collective-permute-start.45 = (bf16[16,2048]{1,0:T(8,128)(2,1)S(1)}, bf16[16,2048]{1,0:T(8,128)(2,1)S(1)}, u32[]{:S(2)}, u32[]{:S(2)}) collective-permute-start(bf16[16,2048]{1,0:T(8,128)(2,1)S(1)} %add.13), channel_id=1, source_target_pairs={{0,12},{1,13},{2,14},{3,15},{4,0},{5,1},{6,2},{7,3},{8,4},{9,5},{1... | collective-permute-start | bytes 196616 | tf_op jit(solution)/shard_map/ppermute | solution.py:441
  58.0 5.9 %collective-permute-start.43 = (bf16[16,2048]{1,0:T(8,128)(2,1)S(1)}, bf16[16,2048]{1,0:T(8,128)(2,1)S(1)}, u32[]{:S(2)}, u32[]{:S(2)}) collective-permute-start(bf16[16,2048]{1,0:T(8,128)(2,1)S(1)} %add.12), channel_id=1, source_target_pairs={{0,8},{1,9},{2,10},{3,11},{4,12},{5,13},{6,14},{7,15},{8,0},{9,1},... | collective-permute-start | bytes 196616 | tf_op jit(solution)/shard_map/ppermute | solution.py:441
  60.5 7.7 %collective-permute-start.21 = (bf16[16,2048]{1,0:T(8,128)(2,1)S(1)}, bf16[16,2048]{1,0:T(8,128)(2,1)S(1)}, u32[]{:S(2)}, u32[]{:S(2)}) collective-permute-start(bf16[16,2048]{1,0:T(8,128)(2,1)S(1)} %add.9), channel_id=1, source_target_pairs={{0,12},{1,13},{2,14},{3,15},{4,0},{5,1},{6,2},{7,3},{8,4},{9,5},{1... | collective-permute-start | bytes 196616 | tf_op jit(solution)/shard_map/ppermute | solution.py:441
  63.3 7.4 %collective-permute-start.19 = (bf16[16,2048]{1,0:T(8,128)(2,1)S(1)}, bf16[16,2048]{1,0:T(8,128)(2,1)S(1)}, u32[]{:S(2)}, u32[]{:S(2)}) collective-permute-start(bf16[16,2048]{1,0:T(8,128)(2,1)S(1)} %add.8), channel_id=1, source_target_pairs={{0,8},{1,9},{2,10},{3,11},{4,12},{5,13},{6,14},{7,15},{8,0},{9,1},... | collective-permute-start | bytes 196616 | tf_op jit(solution)/shard_map/ppermute | solution.py:441
  63.9 9.4 %collective-permute-start.48 = (bf16[16,2048]{1,0:T(8,128)(2,1)S(1)}, bf16[16,2048]{1,0:T(8,128)(2,1)S(1)}, u32[]{:S(2)}, u32[]{:S(2)}) collective-permute-start(bf16[16,2048]{1,0:T(8,128)(2,1)S(1)} %add.15.refs_2_), channel_id=1, source_target_pairs={{0,4},{1,5},{2,6},{3,7},{4,8},{5,9},{6,10},{7,11},{8,12},{9,13},{1... | collective-permute-start | bytes 196616 | tf_op jit(solution)/shard_map/ppermute | solution.py:426
  64.0 9.7 %collective-permute-start.49 = (bf16[16,2048]{1,0:T(8,128)(2,1)S(1)}, bf16[16,2048]{1,0:T(8,128)(2,1)S(1)}, u32[]{:S(2)}, u32[]{:S(2)}) collective-permute-start(bf16[16,2048]{1,0:T(8,128)(2,1)S(1)} %add.15.refs_2_), channel_id=1, source_target_pairs={{0,8},{1,9},{2,10},{3,11},{4,12},{5,13},{6,14},{7,15},{8,0},{9,1},... | collective-permute-start | bytes 196616 | tf_op jit(solution)/shard_map/ppermute | solution.py:426
  65.9 10.7 %collective-permute-start.50 = (bf16[16,2048]{1,0:T(8,128)(2,1)S(1)}, bf16[16,2048]{1,0:T(8,128)(2,1)S(1)}, u32[]{:S(2)}, u32[]{:S(2)}) collective-permute-start(bf16[16,2048]{1,0:T(8,128)(2,1)S(1)} %add.15.refs_2_), channel_id=1, source_target_pairs={{0,12},{1,13},{2,14},{3,15},{4,0},{5,1},{6,2},{7,3},{8,4},{9,5},{1... | collective-permute-start | bytes 196616 | tf_op jit(solution)/shard_map/ppermute | solution.py:426
  68.2 9.3 %collective-permute-start.55 = (bf16[16,2048]{1,0:T(8,128)(2,1)S(1)}, bf16[16,2048]{1,0:T(8,128)(2,1)S(1)}, u32[]{:S(2)}, u32[]{:S(2)}) collective-permute-start(bf16[16,2048]{1,0:T(8,128)(2,1)S(1)} %add.15.refs_2_), channel_id=1, source_target_pairs={{0,2},{1,3},{2,0},{3,1},{4,6},{5,7},{6,4},{7,5},{8,10},{9,11},{10,... | collective-permute-start | bytes 196616 | tf_op jit(solution)/shard_map/ppermute | solution.py:426
  70.7 7.6 %collective-permute-start.51 = (bf16[16,2048]{1,0:T(8,128)(2,1)S(1)}, bf16[16,2048]{1,0:T(8,128)(2,1)S(1)}, u32[]{:S(2)}, u32[]{:S(2)}) collective-permute-start(bf16[16,2048]{1,0:T(8,128)(2,1)S(1)} %add.15.refs_2_), channel_id=1, source_target_pairs={{0,1},{1,0},{2,3},{3,2},{4,5},{5,4},{6,7},{7,6},{8,9},{9,8},{10,11... | collective-permute-start | bytes 196616 | tf_op jit(solution)/shard_map/ppermute | solution.py:426
  73.4 7.2 %collective-permute-start.24 = (bf16[16,2048]{1,0:T(8,128)(2,1)S(1)}, bf16[16,2048]{1,0:T(8,128)(2,1)S(1)}, u32[]{:S(2)}, u32[]{:S(2)}) collective-permute-start(bf16[16,2048]{1,0:T(8,128)(2,1)S(1)} %add.11.refs_2_), channel_id=1, source_target_pairs={{0,4},{1,5},{2,6},{3,7},{4,8},{5,9},{6,10},{7,11},{8,12},{9,13},{1... | collective-permute-start | bytes 196616 | tf_op jit(solution)/shard_map/ppermute | solution.py:426
  73.7 7.8 %collective-permute-start.25 = (bf16[16,2048]{1,0:T(8,128)(2,1)S(1)}, bf16[16,2048]{1,0:T(8,128)(2,1)S(1)}, u32[]{:S(2)}, u32[]{:S(2)}) collective-permute-start(bf16[16,2048]{1,0:T(8,128)(2,1)S(1)} %add.11.refs_2_), channel_id=1, source_target_pairs={{0,8},{1,9},{2,10},{3,11},{4,12},{5,13},{6,14},{7,15},{8,0},{9,1},... | collective-permute-start | bytes 196616 | tf_op jit(solution)/shard_map/ppermute | solution.py:426
  76.6 5.9 %collective-permute-start.26 = (bf16[16,2048]{1,0:T(8,128)(2,1)S(1)}, bf16[16,2048]{1,0:T(8,128)(2,1)S(1)}, u32[]{:S(2)}, u32[]{:S(2)}) collective-permute-start(bf16[16,2048]{1,0:T(8,128)(2,1)S(1)} %add.11.refs_2_), channel_id=1, source_target_pairs={{0,12},{1,13},{2,14},{3,15},{4,0},{5,1},{6,2},{7,3},{8,4},{9,5},{1... | collective-permute-start | bytes 196616 | tf_op jit(solution)/shard_map/ppermute | solution.py:426
  78.3 6.7 %collective-permute-start.27 = (bf16[16,2048]{1,0:T(8,128)(2,1)S(1)}, bf16[16,2048]{1,0:T(8,128)(2,1)S(1)}, u32[]{:S(2)}, u32[]{:S(2)}) collective-permute-start(bf16[16,2048]{1,0:T(8,128)(2,1)S(1)} %add.11.refs_2_), channel_id=1, source_target_pairs={{0,1},{1,0},{2,3},{3,2},{4,5},{5,4},{6,7},{7,6},{8,9},{9,8},{10,11... | collective-permute-start | bytes 196616 | tf_op jit(solution)/shard_map/ppermute | solution.py:426
  (36 other events, 170.0 us)

commit v4 on v2

--- a/solution.py
+++ b/solution.py
@@ -151,6 +151,10 @@
     own = keep_ref.shape[0]
     keep_ref[...] = total[:own]
     send_ref[...] = total[own:].astype(BF16)
+
+
+def project_shapes(rows, own, width):
+    return [shaped((own, width), F32), shaped((rows - own, width), BF16)]
 
 
 def first_kernel(count, *refs):
@@ -219,8 +223,8 @@
 def next_kernel(count, *refs):
     blocks, refs = refs[:count], refs[count:]
     flip_ref, table_ref, *gu_refs, qe_ref, down_ref, qc_hbm = refs[:7]
-    hq_ref, keep_ref, send_ref = refs[7:10]
-    tok_ref, rot_ref, mixed_ref, mm_ref, qc_ref, qc_sem = refs[10:]
+    hq_ref, *outs = refs[7:-6]
+    tok_ref, rot_ref, mixed_ref, mm_ref, qc_ref, qc_sem = refs[-6:]
     units = hq_ref.shape[1]
     step = min(256, units)
 
@@ -249,7 +253,7 @@
         def _():
             codes(block + slots).start()
 
-    project(mm_ref, down_ref, keep_ref, send_ref)
+    project(mm_ref, down_ref, *outs)
 
 
 def next_hidden(cores, blocks, flip, table, gate_up, codes, exps, down):
@@ -262,11 +266,7 @@
         functools.partial(next_kernel, len(blocks)),
         in_specs=[spec(pltpu.VMEM)] * (len(blocks) + 6) + [spec(pltpu.HBM)],
         out_specs=[spec(pltpu.VMEM)] * 3,
-        out_shape=[
-            shaped((rows, units), BF16),
-            shaped((own, width), F32),
-            shaped((rows - own, width), BF16),
-        ],
+        out_shape=[shaped((rows, units), BF16)] + project_shapes(rows, own, width),
         scratch_shapes=[
             pltpu.VMEM((rows, depth), BF16),
             pltpu.VMEM((rows, depth), BF16),
@@ -286,18 +286,17 @@
     )
 
 
-def last_kernel(mm_ref, down_ref, keep_ref, send_ref):
-    project(mm_ref, down_ref, keep_ref, send_ref)
+def last_kernel(mm_ref, down_ref, *outs):
+    project(mm_ref, down_ref, *outs)
 
 
 def last_project(cores, mm, down):
     rows, (units, width) = mm.shape[0], down.shape
-    own = rows // cores
     return pl.pallas_call(
         last_kernel,
         in_specs=[spec(pltpu.VMEM)] * 2,
         out_specs=[spec(pltpu.VMEM)] * 2,
-        out_shape=[shaped((own, width), F32), shaped((rows - own, width), BF16)],
+        out_shape=project_shapes(rows, rows // cores, width),
         compiler_params=params(4),
         name="last_project",
     )(mm, down)
@@ -346,14 +345,30 @@
     )(keep, *received, *blocks)
 
 
-def gram_kernel(scale, parts, *refs):
-    hqs, blocks = refs[:parts], refs[parts:-6]
-    o_hbm, hq_ref, turned_ref, proj_ref, o_ref, sem = refs[-6:]
-    stack(hqs, hq_ref)
+def turn_kernel(parts, *refs):
+    o_ref, hq_ref = refs[-2:]
+    stack(refs[:parts], hq_ref)
+    o_ref[...] = hq_ref[...].T
+
+
+def turn(hqs):
+    rows, units = sum(hq.shape[0] for hq in hqs), hqs[0].shape[1]
+    return pl.pallas_call(
+        functools.partial(turn_kernel, len(hqs)),
+        in_specs=[spec(pltpu.VMEM)] * len(hqs),
+        out_specs=spec(pltpu.VMEM),
+        out_shape=shaped((units, rows), BF16),
+        scratch_shapes=[pltpu.VMEM((rows, units), BF16)],
+        compiler_params=params(4),
+        name="turn",
+    )(*hqs)
+
+
+def gram_kernel(scale, turned_ref, *refs):
+    blocks, (o_hbm, proj_ref, o_ref, sem) = refs[:-4], refs[-4:]
     stack(blocks, proj_ref)
-    turned_ref[...] = hq_ref[...].T
     units = turned_ref.shape[0]
-    step = min(256, units)
+    step = min(128, units)
     copies = []
     for k in range(units // step):
         cut = pl.ds(k * step, step)
@@ -365,24 +380,22 @@
         copy.wait()
 
 
-def gram(hqs, blocks):
-    rows = sum(hq.shape[0] for hq in hqs)
-    units, out = hqs[0].shape[1], blocks[0].shape[1]
-    return pl.pallas_call(
-        functools.partial(gram_kernel, 1.0 / rows**0.5, len(hqs)),
-        in_specs=[spec(pltpu.VMEM)] * (len(hqs) + len(blocks)),
+def gram(turned, blocks):
+    units, rows = turned.shape
+    out = blocks[0].shape[1]
+    return pl.pallas_call(
+        functools.partial(gram_kernel, 1.0 / rows**0.5),
+        in_specs=[spec(pltpu.VMEM)] * (1 + len(blocks)),
         out_specs=spec(pltpu.HBM),
         out_shape=shaped((units, out), BF16),
         scratch_shapes=[
-            pltpu.VMEM((rows, units), BF16),
-            pltpu.VMEM((units, rows), BF16),
             pltpu.VMEM((rows, out), BF16),
             pltpu.VMEM((units, out), BF16),
-            pltpu.SemaphoreType.DMA((units // min(256, units),)),
+            pltpu.SemaphoreType.DMA((units // min(128, units),)),
         ],
         compiler_params=params(24),
         name="gram",
-    )(*hqs, *blocks)
+    )(turned, *blocks)
 
 
 def grid_of(mesh):
@@ -396,6 +409,10 @@
     return len(chips) // side, side, cores
 
 
+def mirrored(length):
+    return length & (length - 1) == 0
+
+
 def shift(grid, axis, by):
     pairs = []
     for line in range(grid[0]):
@@ -403,12 +420,17 @@
             for core in range(grid[2]):
                 spot = [line, side, core]
                 source = (spot[0] * grid[1] + spot[1]) * grid[2] + spot[2]
-                spot[axis] = (spot[axis] + by) % grid[axis]
+                if mirrored(grid[axis]):
+                    spot[axis] ^= abs(by)
+                else:
+                    spot[axis] = (spot[axis] + by) % grid[axis]
                 pairs.append((source, (spot[0] * grid[1] + spot[1]) * grid[2] + spot[2]))
     return pairs
 
 
 def far_first(lines):
+    if mirrored(lines):
+        return list(range(lines))[::-1]
     return sorted(range(lines), key=lambda s: -min(s, lines - s))
 
 
@@ -472,16 +494,19 @@
             chunk_blocks(blocks, chunks[0]), flip, table, gate_up, codes, quant_exps
         )
         gu = [held(value) for value in gu]
-        hqs, kept, sent = [hq], {chunks[0]: None}, {}
+        hqs, outs = [hq], {chunks[0]: None}
         for chunk in chunks[1:]:
-            hq, kept[chunk], sent[chunk] = next_hidden(
+            hq, *outs[chunk] = next_hidden(
                 grid[2], chunk_blocks(blocks, chunk), flip, table, gu, quant_codes, quant_exps, down_rows
             )
             hqs.append(hq)
-        kept[chunks[0]], sent[chunks[0]] = last_project(grid[2], mm, down_rows)
+        outs[chunks[0]] = last_project(grid[2], mm, down_rows)
+        kept = {chunk: outs[chunk][0] for chunk in chunks}
+        sent = {chunk: outs[chunk][1] for chunk in chunks}
         own = reduce_to_owner(grid, group, kept, sent)
+        turned = turn(hqs)
         projected, _ = gather(grid, own)
-        return gram(hqs, sum((chunk_blocks(projected, chunk) for chunk in chunks), []))
+        return gram(turned, sum((chunk_blocks(projected, chunk) for chunk in chunks), []))
 
     placed = (
         P(("dom", "tok"), None),

time: 94.9 us -> 96.1 us (1.013)
  starting transfers between devices: 40 us -> 53.7 us
  waiting for transfers between devices: 24.4 us -> 12.2 us
    ppermute x30, starting transfers between devices: 34 us -> 44.5 us  [gather(): lax.ppermute(value, 'tok', shift(grid, axis, by))]
    ppermute x30, waiting for transfers between devices: 9.69 us -> 3.36 us  [gather(): lax.ppermute(value, 'tok', shift(grid, axis, by))]
    ppermute x9, waiting for transfers between devices: 14.7 us -> 8.88 us  [reduce_to_owner(): lax.ppermute(value, 'tok', shift(grid, axis, -by))]
    ppermute x9, starting transfers between devices: 5.98 us -> 9.12 us  [reduce_to_owner(): lax.ppermute(value, 'tok', shift(grid, axis, -by))]
    pallas_call x1 -> x2, Pallas kernels: 4.11 us -> 4.02 us  [the longest x1 3.83 us: gram(): pl.pallas_call(functools.partial(gram_kernel, 1.0 / rows ** 0.5), in_spec...]
  transfers between devices with their start and end apart: 39 -> 39, of which waited for: 14 -> 12; matrix products, arithmetic and copies ran while one was open for 0% -> 0% of each run, Pallas kernels for 17% -> 17%
where the time goes in v4:
time: 96.1 us; the launch traced here: 95.7 us
  starting transfers between devices  53.7 us (56%)
  Pallas kernels  29.3 us (30%)
  waiting for transfers between devices  12.2 us (13%)
    ppermute x30, starting transfers between devices, gather(): lax.ppermute(value, 'tok', shift(grid, axis, by))  44.5 us
    pallas_call x1, Pallas kernels, next_hidden(): pl.pallas_call(functools.partial(next_kernel, len(blocks)), in_specs=[spe...  9.27 us
    ppermute x9, starting transfers between devices, reduce_to_owner(): lax.ppermute(value, 'tok', shift(grid, axis, -by))  9.12 us
    ppermute x9, waiting for transfers between devices, reduce_to_owner(): lax.ppermute(value, 'tok', shift(grid, axis, -by))  8.88 us
    pallas_call x1, Pallas kernels, first_hidden(): pl.pallas_call(functools.partial(first_kernel, len(blocks)), in_specs=[sp...  8.46 us
    pallas_call x1, Pallas kernels, fetch(): pl.pallas_call(fetch_kernel, in_specs=[spec(pltpu.VMEM), spec(pltpu.HBM)]...  5.96 us
    pallas_call x1, Pallas kernels, gram(): pl.pallas_call(functools.partial(gram_kernel, 1.0 / rows ** 0.5), in_spec...  3.83 us
    ppermute x30, waiting for transfers between devices, gather(): lax.ppermute(value, 'tok', shift(grid, axis, by))  3.36 us
  transfers between devices with their start and end apart: 39, of which 12 were waited for; matrix products, arithmetic and copies ran while one was open for 0% of the time, Pallas kernels for 17%

profile of v4, /device:TPU:1, one launch (start us, length us, event | category | flops | bytes accessed | tf_op | source)
XLA Modules:
  0.0 95.7 jit_solution(16703637310263822025)
XLA Ops:
  0.0 2.1 %collective-permute-start = (bf16[16,4096]{1,0:T(8,128)(2,1)}, bf16[16,4096]{1,0:T(8,128)(2,1)S(1)}, u32[]{:S(2)}, u32[]{:S(2)}) collective-permute-start(bf16[16,4096]{1,0:T(8,128)(2,1)} %refs_0_.1), channel_id=1, source_target_pairs={{0,4},{1,5},{2,6},{3,7},{4,0},{5,1},{6,2},{7,3},{8,12},{9,13},{10,... | collective-permute-start | bytes 393224 | tf_op jit(solution)/shard_map/ppermute | solution.py:438
  2.1 2.3 %collective-permute-start.1 = (bf16[16,4096]{1,0:T(8,128)(2,1)}, bf16[16,4096]{1,0:T(8,128)(2,1)S(1)}, u32[]{:S(2)}, u32[]{:S(2)}) collective-permute-start(bf16[16,4096]{1,0:T(8,128)(2,1)} %refs_0_.1), channel_id=1, source_target_pairs={{0,8},{1,9},{2,10},{3,11},{4,12},{5,13},{6,14},{7,15},{8,0},{9,1},... | collective-permute-start | bytes 393224 | tf_op jit(solution)/shard_map/ppermute | solution.py:438
  4.4 1.2 %collective-permute-start.3 = (bf16[16,4096]{1,0:T(8,128)(2,1)}, bf16[16,4096]{1,0:T(8,128)(2,1)S(1)}, u32[]{:S(2)}, u32[]{:S(2)}) collective-permute-start(bf16[16,4096]{1,0:T(8,128)(2,1)} %refs_0_.1), channel_id=1, source_target_pairs={{0,1},{1,0},{2,3},{3,2},{4,5},{5,4},{6,7},{7,6},{8,9},{9,8},{10,11... | collective-permute-start | bytes 393224 | tf_op jit(solution)/shard_map/ppermute | solution.py:438
  5.7 1.5 %collective-permute-start.7 = (bf16[16,4096]{1,0:T(8,128)(2,1)}, bf16[16,4096]{1,0:T(8,128)(2,1)S(1)}, u32[]{:S(2)}, u32[]{:S(2)}) collective-permute-start(bf16[16,4096]{1,0:T(8,128)(2,1)} %refs_0_.1), channel_id=1, source_target_pairs={{0,2},{1,3},{2,0},{3,1},{4,6},{5,7},{6,4},{7,5},{8,10},{9,11},{10,... | collective-permute-start | bytes 393224 | tf_op jit(solution)/shard_map/ppermute | solution.py:438
  7.1 1.2 %collective-permute-start.4 = (bf16[16,4096]{1,0:T(8,128)(2,1)S(1)}, bf16[16,4096]{1,0:T(8,128)(2,1)S(1)}, u32[]{:S(2)}, u32[]{:S(2)}) collective-permute-start(bf16[16,4096]{1,0:T(8,128)(2,1)S(1)} %collective-permute-done._.refs_1_), channel_id=1, source_target_pairs={{0,1},{1,0},{2,3},{3,2},{4,5},{5,4},{6,7},{7,6},{8,9},{9,8},{10,11... | collective-permute-start | bytes 393224 | tf_op jit(solution)/shard_map/ppermute | solution.py:438
  8.4 7.8 %collective-permute-start.5 = (bf16[16,4096]{1,0:T(8,128)(2,1)S(1)}, bf16[16,4096]{1,0:T(8,128)(2,1)S(1)}, u32[]{:S(2)}, u32[]{:S(2)}) collective-permute-start(bf16[16,4096]{1,0:T(8,128)(2,1)S(1)} %collective-permute-done.1.refs_2_), channel_id=1, source_target_pairs={{0,1},{1,0},{2,3},{3,2},{4,5},{5,4},{6,7},{7,6},{8,9},{9,8},{10,11... | collective-permute-start | bytes 393224 | tf_op jit(solution)/shard_map/ppermute | solution.py:438
  16.2 1.2 %collective-permute-start.8 = (bf16[16,4096]{1,0:T(8,128)(2,1)S(1)}, bf16[16,4096]{1,0:T(8,128)(2,1)S(1)}, u32[]{:S(2)}, u32[]{:S(2)}) collective-permute-start(bf16[16,4096]{1,0:T(8,128)(2,1)S(1)} %collective-permute-done._.refs_1_), channel_id=1, source_target_pairs={{0,2},{1,3},{2,0},{3,1},{4,6},{5,7},{6,4},{7,5},{8,10},{9,11},{10,... | collective-permute-start | bytes 393224 | tf_op jit(solution)/shard_map/ppermute | solution.py:438
  17.6 1.2 %collective-permute-start.10 = (bf16[16,4096]{1,0:T(8,128)(2,1)S(1)}, bf16[16,4096]{1,0:T(8,128)(2,1)S(1)}, u32[]{:S(2)}, u32[]{:S(2)}) collective-permute-start(bf16[16,4096]{1,0:T(8,128)(2,1)S(1)} %collective-permute-done.2.refs_3_), channel_id=1, source_target_pairs={{0,2},{1,3},{2,0},{3,1},{4,6},{5,7},{6,4},{7,5},{8,10},{9,11},{10,... | collective-permute-start | bytes 393224 | tf_op jit(solution)/shard_map/ppermute | solution.py:438
  20.0 6.0 %fetch.1 = (bf16[1024,1024]{1,0:T(8,128)(2,1)S(1)}, bf16[1024,1024]{1,0:T(8,128)(2,1)S(1)}, bf16[1024,1024]{1,0:T(8,128)(2,1)S(1)}, bf16[1024,1024]{1,0:T(8,128)...) custom-call(bf16[16,4096]{1,0:T(8,128)(2,1)S(1)} %collective-permute, ...), custom_call_target="tpu_custom_call" | custom-call | bytes 33554432 | tf_op jit(solution)/shard_map/fetch/pallas_call | solution.py:135
  27.7 8.5 %first_hidden.1 = (bf16[128,1024]{1,0:T(8,128)(2,1)S(1)}, bf16[128,1024]{1,0:T(8,128)(2,1)S(1)}, bf16[4096,1024]{1,0:T(8,128)(2,1)S(1)}, bf16[4096,1024]{1,0:T(8,128)(2,1)S(1)}) custom-call(bf16[16,4096]{1,0:T(8,128)(2,1)S(1)} %copy-done.1, bf16[16,4096]{1,0:T(8,128)(2,1)S(1)} %collective-permute-done._.refs_1_, ...), custom_call_target="tpu_custom_call" | custom-call | flops 4294967296 | bytes 16777216 | tf_op jit(solution)/shard_map/first_hidden/pallas_call | solution.py:196
  36.3 9.3 %next_hidden.1 = (bf16[128,1024]{1,0:T(8,128)(2,1)S(1)}, f32[64,4096]{1,0:T(8,128)S(1)}, bf16[64,4096]{1,0:T(8,128)(2,1)S(1)}) custom-call(bf16[16,4096]{1,0:T(8,128)(2,1)S(1)} %collective-permute-done.7.refs_0_, bf16[16,4096]{1,0:T(8,128)(2,1)S(1)} %collective-permute-done.8.refs_1_, bf16[16,4096]{1,0:T(8,128)(2,1)S(1)} %collective-permute-done.9.refs_2_, ...), custom_call_target="tpu_custom_call" | custom-call | flops 5368709120 | bytes 16777216 | tf_op jit(solution)/shard_map/next_hidden/pallas_call | solution.py:265
  45.6 1.3 %last_project.1 = (f32[64,4096]{1,0:T(8,128)S(1)}, bf16[64,4096]{1,0:T(8,128)(2,1)S(1)}) custom-call(bf16[128,1024]{1,0:T(8,128)(2,1)S(1)} %get-tuple-element.38.mm_ref, bf16[1024,4096]{1,0:T(8,128)(2,1)S(1)} %bitcast.2), custom_call_target="tpu_custom_call" | custom-call | tf_op jit(solution)/shard_map/last_project/pallas_call | solution.py:295
  47.6 1.3 %collective-permute-start.22 = (bf16[16,4096]{1,0:T(8,128)(2,1)S(1)}, bf16[16,4096]{1,0:T(8,128)(2,1)S(1)}, u32[]{:S(2)}, u32[]{:S(2)}) collective-permute-start(bf16[16,4096]{1,0:T(8,128)(2,1)S(1)} %get-tuple-element.46), channel_id=1, source_target_pairs={{0,2},{1,3},{2,0},{3,1},{4,6},{5,7},{6,4},{7,5},{8,10},{9,11},{10,... | collective-permute-start | bytes 393224 | tf_op jit(solution)/shard_map/ppermute | solution.py:453
  49.1 1.3 %collective-permute-start.18 = (bf16[16,4096]{1,0:T(8,128)(2,1)S(1)}, bf16[16,4096]{1,0:T(8,128)(2,1)S(1)}, u32[]{:S(2)}, u32[]{:S(2)}) collective-permute-start(bf16[16,4096]{1,0:T(8,128)(2,1)S(1)} %get-tuple-element.44), channel_id=1, source_target_pairs={{0,2},{1,3},{2,0},{3,1},{4,6},{5,7},{6,4},{7,5},{8,10},{9,11},{10,... | collective-permute-start | bytes 393224 | tf_op jit(solution)/shard_map/ppermute | solution.py:453
  50.6 2.0 %collective-permute-done.22.refs_1_ = bf16[16,4096]{1,0:T(8,128)(2,1)S(1)} collective-permute-done((bf16[16,4096]{1,0:T(8,128)(2,1)S(1)}, bf16[16,4096]{1,0:T(8,128)(2,1)S(1)}, u32[]{:S(2)}, u32[]{:S(2)}) %collective-permute-start.22) | collective-permute-done | bytes 131104 | tf_op jit(solution)/shard_map/ppermute | solution.py:453
  52.6 1.2 %collective-permute-start.23 = (bf16[16,4096]{1,0:T(8,128)(2,1)S(1)}, bf16[16,4096]{1,0:T(8,128)(2,1)S(1)}, u32[]{:S(2)}, u32[]{:S(2)}) collective-permute-start(bf16[16,4096]{1,0:T(8,128)(2,1)S(1)} %add.6), channel_id=1, source_target_pairs={{0,4},{1,5},{2,6},{3,7},{4,0},{5,1},{6,2},{7,3},{8,12},{9,13},{10,... | collective-permute-start | bytes 393224 | tf_op jit(solution)/shard_map/ppermute | solution.py:453
  53.9 1.5 %collective-permute-done.20.refs_1_ = bf16[16,4096]{1,0:T(8,128)(2,1)S(1)} collective-permute-done((bf16[16,4096]{1,0:T(8,128)(2,1)S(1)}, bf16[16,4096]{1,0:T(8,128)(2,1)S(1)}, u32[]{:S(2)}, u32[]{:S(2)}) %collective-permute-start.20) | collective-permute-done | bytes 131104 | tf_op jit(solution)/shard_map/ppermute | solution.py:453
  55.5 2.2 %collective-permute-start.21 = (bf16[16,4096]{1,0:T(8,128)(2,1)S(1)}, bf16[16,4096]{1,0:T(8,128)(2,1)S(1)}, u32[]{:S(2)}, u32[]{:S(2)}) collective-permute-start(bf16[16,4096]{1,0:T(8,128)(2,1)S(1)} %add.5), channel_id=1, source_target_pairs={{0,8},{1,9},{2,10},{3,11},{4,12},{5,13},{6,14},{7,15},{8,0},{9,1},... | collective-permute-start | bytes 393224 | tf_op jit(solution)/shard_map/ppermute | solution.py:453
  58.3 2.1 %collective-permute-start.19 = (bf16[16,4096]{1,0:T(8,128)(2,1)S(1)}, bf16[16,4096]{1,0:T(8,128)(2,1)S(1)}, u32[]{:S(2)}, u32[]{:S(2)}) collective-permute-start(bf16[16,4096]{1,0:T(8,128)(2,1)S(1)} %add.4), channel_id=1, source_target_pairs={{0,12},{1,13},{2,14},{3,15},{4,8},{5,9},{6,10},{7,11},{8,4},{9,5},... | collective-permute-start | bytes 393224 | tf_op jit(solution)/shard_map/ppermute | solution.py:453
  61.0 4.0 %collective-permute-done.19.refs_2_ = bf16[16,4096]{1,0:T(8,128)(2,1)S(1)} collective-permute-done((bf16[16,4096]{1,0:T(8,128)(2,1)S(1)}, bf16[16,4096]{1,0:T(8,128)(2,1)S(1)}, u32[]{:S(2)}, u32[]{:S(2)}) %collective-permute-start.19) | collective-permute-done | bytes 131104 | tf_op jit(solution)/shard_map/ppermute | solution.py:453
  65.2 4.5 %collective-permute-start.24 = (bf16[16,4096]{1,0:T(8,128)(2,1)S(1)}, bf16[16,4096]{1,0:T(8,128)(2,1)S(1)}, u32[]{:S(2)}, u32[]{:S(2)}) collective-permute-start(bf16[16,4096]{1,0:T(8,128)(2,1)S(1)} %add.7.refs_0_), channel_id=1, source_target_pairs={{0,4},{1,5},{2,6},{3,7},{4,0},{5,1},{6,2},{7,3},{8,12},{9,13},{10,... | collective-permute-start | bytes 393224 | tf_op jit(solution)/shard_map/ppermute | solution.py:438
  69.7 0.9 collective-permute-start.25
  70.6 1.2 %collective-permute-start.26 = (bf16[16,4096]{1,0:T(8,128)(2,1)S(1)}, bf16[16,4096]{1,0:T(8,128)(2,1)S(1)}, u32[]{:S(2)}, u32[]{:S(2)}) collective-permute-start(bf16[16,4096]{1,0:T(8,128)(2,1)S(1)} %add.7.refs_0_), channel_id=1, source_target_pairs={{0,12},{1,13},{2,14},{3,15},{4,8},{5,9},{6,10},{7,11},{8,4},{9,5},... | collective-permute-start | bytes 393224 | tf_op jit(solution)/shard_map/ppermute | solution.py:438
  71.8 1.6 %collective-permute-start.31 = (bf16[16,4096]{1,0:T(8,128)(2,1)S(1)}, bf16[16,4096]{1,0:T(8,128)(2,1)S(1)}, u32[]{:S(2)}, u32[]{:S(2)}) collective-permute-start(bf16[16,4096]{1,0:T(8,128)(2,1)S(1)} %add.7.refs_0_), channel_id=1, source_target_pairs={{0,2},{1,3},{2,0},{3,1},{4,6},{5,7},{6,4},{7,5},{8,10},{9,11},{10,... | collective-permute-start | bytes 393224 | tf_op jit(solution)/shard_map/ppermute | solution.py:438
  73.4 2.0 %collective-permute-start.27 = (bf16[16,4096]{1,0:T(8,128)(2,1)S(1)}, bf16[16,4096]{1,0:T(8,128)(2,1)S(1)}, u32[]{:S(2)}, u32[]{:S(2)}) collective-permute-start(bf16[16,4096]{1,0:T(8,128)(2,1)S(1)} %add.7.refs_0_), channel_id=1, source_target_pairs={{0,1},{1,0},{2,3},{3,2},{4,5},{5,4},{6,7},{7,6},{8,9},{9,8},{10,11... | collective-permute-start | bytes 393224 | tf_op jit(solution)/shard_map/ppermute | solution.py:438
  75.8 1.1 %collective-permute-start.33 = (bf16[16,4096]{1,0:T(8,128)(2,1)S(1)}, bf16[16,4096]{1,0:T(8,128)(2,1)S(1)}, u32[]{:S(2)}, u32[]{:S(2)}) collective-permute-start(bf16[16,4096]{1,0:T(8,128)(2,1)S(1)} %collective-permute-done.25.refs_2_), channel_id=1, source_target_pairs={{0,2},{1,3},{2,0},{3,1},{4,6},{5,7},{6,4},{7,5},{8,10},{9,11},{10,... | collective-permute-start | bytes 393224 | tf_op jit(solution)/shard_map/ppermute | solution.py:438
  76.9 2.2 %collective-permute-done.26.refs_3_ = bf16[16,4096]{1,0:T(8,128)(2,1)S(1)} collective-permute-done((bf16[16,4096]{1,0:T(8,128)(2,1)S(1)}, bf16[16,4096]{1,0:T(8,128)(2,1)S(1)}, u32[]{:S(2)}, u32[]{:S(2)}) %collective-permute-start.26) | collective-permute-done | bytes 131104 | tf_op jit(solution)/shard_map/ppermute | solution.py:438
  79.1 2.2 %collective-permute-start.34 = (bf16[16,4096]{1,0:T(8,128)(2,1)S(1)}, bf16[16,4096]{1,0:T(8,128)(2,1)S(1)}, u32[]{:S(2)}, u32[]{:S(2)}) collective-permute-start(bf16[16,4096]{1,0:T(8,128)(2,1)S(1)} %collective-permute-done.26.refs_3_), channel_id=1, source_target_pairs={{0,2},{1,3},{2,0},{3,1},{4,6},{5,7},{6,4},{7,5},{8,10},{9,11},{10,... | collective-permute-start | bytes 393224 | tf_op jit(solution)/shard_map/ppermute | solution.py:438
  81.3 4.3 %collective-permute-start.28 = (bf16[16,4096]{1,0:T(8,128)(2,1)S(1)}, bf16[16,4096]{1,0:T(8,128)(2,1)S(1)}, u32[]{:S(2)}, u32[]{:S(2)}) collective-permute-start(bf16[16,4096]{1,0:T(8,128)(2,1)S(1)} %collective-permute-done.24.refs_1_), channel_id=1, source_target_pairs={{0,1},{1,0},{2,3},{3,2},{4,5},{5,4},{6,7},{7,6},{8,9},{9,8},{10,11... | collective-permute-start | bytes 393224 | tf_op jit(solution)/shard_map/ppermute | solution.py:438
  86.1 2.4 %collective-permute-start.35 = (bf16[16,4096]{1,0:T(8,128)(2,1)S(1)}, bf16[16,4096]{1,0:T(8,128)(2,1)S(1)}, u32[]{:S(2)}, u32[]{:S(2)}) collective-permute-start(bf16[16,4096]{1,0:T(8,128)(2,1)S(1)} %collective-permute-done.31.refs_8_), channel_id=1, source_target_pairs={{0,1},{1,0},{2,3},{3,2},{4,5},{5,4},{6,7},{7,6},{8,9},{9,8},{10,11... | collective-permute-start | bytes 393224 | tf_op jit(solution)/shard_map/ppermute | solution.py:438
  88.5 1.8 %collective-permute-start.36 = (bf16[16,4096]{1,0:T(8,128)(2,1)S(1)}, bf16[16,4096]{1,0:T(8,128)(2,1)S(1)}, u32[]{:S(2)}, u32[]{:S(2)}) collective-permute-start(bf16[16,4096]{1,0:T(8,128)(2,1)S(1)} %collective-permute-done.32.refs_9_), channel_id=1, source_target_pairs={{0,1},{1,0},{2,3},{3,2},{4,5},{5,4},{6,7},{7,6},{8,9},{9,8},{10,11... | collective-permute-start | bytes 393224 | tf_op jit(solution)/shard_map/ppermute | solution.py:438
  91.9 3.8 %gram.1 = bf16[1024,4096]{1,0:T(8,128)(2,1)} custom-call(bf16[1024,256]{1,0:T(8,128)(2,1)S(1)} %turn.1.turned_ref, bf16[16,4096]{1,0:T(8,128)(2,1)S(1)} %add.7.refs_0_, bf16[16,4096]{1,0:T(8,128)(2,1)S(1)} %collective-permute-done.24.refs_1_, bf16[16,4096]{1,0:T(8,128)(2,1)S(1)} %collective-permute-done.25.refs_2_, ...), custom_call_target="tpu_custom_call" | custom-call | tf_op jit(solution)/shard_map/gram/pallas_call | solution.py:386
  (69 shorter events, 8.2 us)
Async XLA Ops:
  0.0 7.1 %collective-permute-start = (bf16[16,4096]{1,0:T(8,128)(2,1)}, bf16[16,4096]{1,0:T(8,128)(2,1)S(1)}, u32[]{:S(2)}, u32[]{:S(2)}) collective-permute-start(bf16[16,4096]{1,0:T(8,128)(2,1)} %refs_0_.1), channel_id=1, source_target_pairs={{0,4},{1,5},{2,6},{3,7},{4,0},{5,1},{6,2},{7,3},{8,12},{9,13},{10,... | collective-permute-start | bytes 393224 | tf_op jit(solution)/shard_map/ppermute | solution.py:438
  2.1 6.2 %collective-permute-start.1 = (bf16[16,4096]{1,0:T(8,128)(2,1)}, bf16[16,4096]{1,0:T(8,128)(2,1)S(1)}, u32[]{:S(2)}, u32[]{:S(2)}) collective-permute-start(bf16[16,4096]{1,0:T(8,128)(2,1)} %refs_0_.1), channel_id=1, source_target_pairs={{0,8},{1,9},{2,10},{3,11},{4,12},{5,13},{6,14},{7,15},{8,0},{9,1},... | collective-permute-start | bytes 393224 | tf_op jit(solution)/shard_map/ppermute | solution.py:438
  4.4 11.7 %collective-permute-start.2 = (bf16[16,4096]{1,0:T(8,128)(2,1)}, bf16[16,4096]{1,0:T(8,128)(2,1)S(1)}, u32[]{:S(2)}, u32[]{:S(2)}) collective-permute-start(bf16[16,4096]{1,0:T(8,128)(2,1)} %refs_0_.1), channel_id=1, source_target_pairs={{0,12},{1,13},{2,14},{3,15},{4,8},{5,9},{6,10},{7,11},{8,4},{9,5},... | collective-permute-start | bytes 393224 | tf_op jit(solution)/shard_map/ppermute | solution.py:438
  4.4 13.0 %collective-permute-start.3 = (bf16[16,4096]{1,0:T(8,128)(2,1)}, bf16[16,4096]{1,0:T(8,128)(2,1)S(1)}, u32[]{:S(2)}, u32[]{:S(2)}) collective-permute-start(bf16[16,4096]{1,0:T(8,128)(2,1)} %refs_0_.1), channel_id=1, source_target_pairs={{0,1},{1,0},{2,3},{3,2},{4,5},{5,4},{6,7},{7,6},{8,9},{9,8},{10,11... | collective-permute-start | bytes 393224 | tf_op jit(solution)/shard_map/ppermute | solution.py:438
  5.7 12.0 %collective-permute-start.7 = (bf16[16,4096]{1,0:T(8,128)(2,1)}, bf16[16,4096]{1,0:T(8,128)(2,1)S(1)}, u32[]{:S(2)}, u32[]{:S(2)}) collective-permute-start(bf16[16,4096]{1,0:T(8,128)(2,1)} %refs_0_.1), channel_id=1, source_target_pairs={{0,2},{1,3},{2,0},{3,1},{4,6},{5,7},{6,4},{7,5},{8,10},{9,11},{10,... | collective-permute-start | bytes 393224 | tf_op jit(solution)/shard_map/ppermute | solution.py:438
  7.1 11.8 %collective-permute-start.4 = (bf16[16,4096]{1,0:T(8,128)(2,1)S(1)}, bf16[16,4096]{1,0:T(8,128)(2,1)S(1)}, u32[]{:S(2)}, u32[]{:S(2)}) collective-permute-start(bf16[16,4096]{1,0:T(8,128)(2,1)S(1)} %collective-permute-done._.refs_1_), channel_id=1, source_target_pairs={{0,1},{1,0},{2,3},{3,2},{4,5},{5,4},{6,7},{7,6},{8,9},{9,8},{10,11... | collective-permute-start | bytes 393224 | tf_op jit(solution)/shard_map/ppermute | solution.py:438
  8.4 17.6 %collective-permute-start.5 = (bf16[16,4096]{1,0:T(8,128)(2,1)S(1)}, bf16[16,4096]{1,0:T(8,128)(2,1)S(1)}, u32[]{:S(2)}, u32[]{:S(2)}) collective-permute-start(bf16[16,4096]{1,0:T(8,128)(2,1)S(1)} %collective-permute-done.1.refs_2_), channel_id=1, source_target_pairs={{0,1},{1,0},{2,3},{3,2},{4,5},{5,4},{6,7},{7,6},{8,9},{9,8},{10,11... | collective-permute-start | bytes 393224 | tf_op jit(solution)/shard_map/ppermute | solution.py:438
  16.2 9.9 %collective-permute-start.8 = (bf16[16,4096]{1,0:T(8,128)(2,1)S(1)}, bf16[16,4096]{1,0:T(8,128)(2,1)S(1)}, u32[]{:S(2)}, u32[]{:S(2)}) collective-permute-start(bf16[16,4096]{1,0:T(8,128)(2,1)S(1)} %collective-permute-done._.refs_1_), channel_id=1, source_target_pairs={{0,2},{1,3},{2,0},{3,1},{4,6},{5,7},{6,4},{7,5},{8,10},{9,11},{10,... | collective-permute-start | bytes 393224 | tf_op jit(solution)/shard_map/ppermute | solution.py:438
  17.4 9.2 %collective-permute-start.9 = (bf16[16,4096]{1,0:T(8,128)(2,1)S(1)}, bf16[16,4096]{1,0:T(8,128)(2,1)S(1)}, u32[]{:S(2)}, u32[]{:S(2)}) collective-permute-start(bf16[16,4096]{1,0:T(8,128)(2,1)S(1)} %collective-permute-done.1.refs_2_), channel_id=1, source_target_pairs={{0,2},{1,3},{2,0},{3,1},{4,6},{5,7},{6,4},{7,5},{8,10},{9,11},{10,... | collective-permute-start | bytes 393224 | tf_op jit(solution)/shard_map/ppermute | solution.py:438
  17.6 9.2 %collective-permute-start.10 = (bf16[16,4096]{1,0:T(8,128)(2,1)S(1)}, bf16[16,4096]{1,0:T(8,128)(2,1)S(1)}, u32[]{:S(2)}, u32[]{:S(2)}) collective-permute-start(bf16[16,4096]{1,0:T(8,128)(2,1)S(1)} %collective-permute-done.2.refs_3_), channel_id=1, source_target_pairs={{0,2},{1,3},{2,0},{3,1},{4,6},{5,7},{6,4},{7,5},{8,10},{9,11},{10,... | collective-permute-start | bytes 393224 | tf_op jit(solution)/shard_map/ppermute | solution.py:438
  18.9 8.8 %collective-permute-start.6 = (bf16[16,4096]{1,0:T(8,128)(2,1)S(1)}, bf16[16,4096]{1,0:T(8,128)(2,1)S(1)}, u32[]{:S(2)}, u32[]{:S(2)}) collective-permute-start(bf16[16,4096]{1,0:T(8,128)(2,1)S(1)} %collective-permute-done.2.refs_3_), channel_id=1, source_target_pairs={{0,1},{1,0},{2,3},{3,2},{4,5},{5,4},{6,7},{7,6},{8,9},{9,8},{10,11... | collective-permute-start | bytes 393224 | tf_op jit(solution)/shard_map/ppermute | solution.py:438
  26.0 10.2 %collective-permute-start.11 = (bf16[16,4096]{1,0:T(8,128)(2,1)S(1)}, bf16[16,4096]{1,0:T(8,128)(2,1)S(1)}, u32[]{:S(2)}, u32[]{:S(2)}) collective-permute-start(bf16[16,4096]{1,0:T(8,128)(2,1)S(1)} %collective-permute-done.7.refs_0_), channel_id=1, source_target_pairs={{0,1},{1,0},{2,3},{3,2},{4,5},{5,4},{6,7},{7,6},{8,9},{9,8},{10,11... | collective-permute-start | bytes 393224 | tf_op jit(solution)/shard_map/ppermute | solution.py:438
  26.1 10.1 %collective-permute-start.12 = (bf16[16,4096]{1,0:T(8,128)(2,1)S(1)}, bf16[16,4096]{1,0:T(8,128)(2,1)S(1)}, u32[]{:S(2)}, u32[]{:S(2)}) collective-permute-start(bf16[16,4096]{1,0:T(8,128)(2,1)S(1)} %collective-permute-done.8.refs_1_), channel_id=1, source_target_pairs={{0,1},{1,0},{2,3},{3,2},{4,5},{5,4},{6,7},{7,6},{8,9},{9,8},{10,11... | collective-permute-start | bytes 393224 | tf_op jit(solution)/shard_map/ppermute | solution.py:438
  26.6 9.6 %collective-permute-start.13 = (bf16[16,4096]{1,0:T(8,128)(2,1)S(1)}, bf16[16,4096]{1,0:T(8,128)(2,1)S(1)}, u32[]{:S(2)}, u32[]{:S(2)}) collective-permute-start(bf16[16,4096]{1,0:T(8,128)(2,1)S(1)} %collective-permute-done.9.refs_2_), channel_id=1, source_target_pairs={{0,1},{1,0},{2,3},{3,2},{4,5},{5,4},{6,7},{7,6},{8,9},{9,8},{10,11... | collective-permute-start | bytes 393224 | tf_op jit(solution)/shard_map/ppermute | solution.py:438
  26.8 9.4 %collective-permute-start.14 = (bf16[16,4096]{1,0:T(8,128)(2,1)S(1)}, bf16[16,4096]{1,0:T(8,128)(2,1)S(1)}, u32[]{:S(2)}, u32[]{:S(2)}) collective-permute-start(bf16[16,4096]{1,0:T(8,128)(2,1)S(1)} %collective-permute-done.10.refs_3_), channel_id=1, source_target_pairs={{0,1},{1,0},{2,3},{3,2},{4,5},{5,4},{6,7},{7,6},{8,9},{9,8},{10,11... | collective-permute-start | bytes 393224 | tf_op jit(solution)/shard_map/ppermute | solution.py:438
  47.6 5.0 %collective-permute-start.22 = (bf16[16,4096]{1,0:T(8,128)(2,1)S(1)}, bf16[16,4096]{1,0:T(8,128)(2,1)S(1)}, u32[]{:S(2)}, u32[]{:S(2)}) collective-permute-start(bf16[16,4096]{1,0:T(8,128)(2,1)S(1)} %get-tuple-element.46), channel_id=1, source_target_pairs={{0,2},{1,3},{2,0},{3,1},{4,6},{5,7},{6,4},{7,5},{8,10},{9,11},{10,... | collective-permute-start | bytes 393224 | tf_op jit(solution)/shard_map/ppermute | solution.py:453
  49.0 6.5 %collective-permute-start.20 = (bf16[16,4096]{1,0:T(8,128)(2,1)S(1)}, bf16[16,4096]{1,0:T(8,128)(2,1)S(1)}, u32[]{:S(2)}, u32[]{:S(2)}) collective-permute-start(bf16[16,4096]{1,0:T(8,128)(2,1)S(1)} %get-tuple-element.45), channel_id=1, source_target_pairs={{0,2},{1,3},{2,0},{3,1},{4,6},{5,7},{6,4},{7,5},{8,10},{9,11},{10,... | collective-permute-start | bytes 393224 | tf_op jit(solution)/shard_map/ppermute | solution.py:453
  49.1 9.1 %collective-permute-start.18 = (bf16[16,4096]{1,0:T(8,128)(2,1)S(1)}, bf16[16,4096]{1,0:T(8,128)(2,1)S(1)}, u32[]{:S(2)}, u32[]{:S(2)}) collective-permute-start(bf16[16,4096]{1,0:T(8,128)(2,1)S(1)} %get-tuple-element.44), channel_id=1, source_target_pairs={{0,2},{1,3},{2,0},{3,1},{4,6},{5,7},{6,4},{7,5},{8,10},{9,11},{10,... | collective-permute-start | bytes 393224 | tf_op jit(solution)/shard_map/ppermute | solution.py:453
  50.4 10.6 %collective-permute-start.17 = (bf16[16,4096]{1,0:T(8,128)(2,1)S(1)}, bf16[16,4096]{1,0:T(8,128)(2,1)S(1)}, u32[]{:S(2)}, u32[]{:S(2)}) collective-permute-start(bf16[16,4096]{1,0:T(8,128)(2,1)S(1)} %get-tuple-element.43), channel_id=1, source_target_pairs={{0,2},{1,3},{2,0},{3,1},{4,6},{5,7},{6,4},{7,5},{8,10},{9,11},{10,... | collective-permute-start | bytes 393224 | tf_op jit(solution)/shard_map/ppermute | solution.py:453
  52.6 8.4 %collective-permute-start.23 = (bf16[16,4096]{1,0:T(8,128)(2,1)S(1)}, bf16[16,4096]{1,0:T(8,128)(2,1)S(1)}, u32[]{:S(2)}, u32[]{:S(2)}) collective-permute-start(bf16[16,4096]{1,0:T(8,128)(2,1)S(1)} %add.6), channel_id=1, source_target_pairs={{0,4},{1,5},{2,6},{3,7},{4,0},{5,1},{6,2},{7,3},{8,12},{9,13},{10,... | collective-permute-start | bytes 393224 | tf_op jit(solution)/shard_map/ppermute | solution.py:453
  55.5 5.6 %collective-permute-start.21 = (bf16[16,4096]{1,0:T(8,128)(2,1)S(1)}, bf16[16,4096]{1,0:T(8,128)(2,1)S(1)}, u32[]{:S(2)}, u32[]{:S(2)}) collective-permute-start(bf16[16,4096]{1,0:T(8,128)(2,1)S(1)} %add.5), channel_id=1, source_target_pairs={{0,8},{1,9},{2,10},{3,11},{4,12},{5,13},{6,14},{7,15},{8,0},{9,1},... | collective-permute-start | bytes 393224 | tf_op jit(solution)/shard_map/ppermute | solution.py:453
  58.3 6.8 %collective-permute-start.19 = (bf16[16,4096]{1,0:T(8,128)(2,1)S(1)}, bf16[16,4096]{1,0:T(8,128)(2,1)S(1)}, u32[]{:S(2)}, u32[]{:S(2)}) collective-permute-start(bf16[16,4096]{1,0:T(8,128)(2,1)S(1)} %add.4), channel_id=1, source_target_pairs={{0,12},{1,13},{2,14},{3,15},{4,8},{5,9},{6,10},{7,11},{8,4},{9,5},... | collective-permute-start | bytes 393224 | tf_op jit(solution)/shard_map/ppermute | solution.py:453
  65.2 10.2 %collective-permute-start.24 = (bf16[16,4096]{1,0:T(8,128)(2,1)S(1)}, bf16[16,4096]{1,0:T(8,128)(2,1)S(1)}, u32[]{:S(2)}, u32[]{:S(2)}) collective-permute-start(bf16[16,4096]{1,0:T(8,128)(2,1)S(1)} %add.7.refs_0_), channel_id=1, source_target_pairs={{0,4},{1,5},{2,6},{3,7},{4,0},{5,1},{6,2},{7,3},{8,12},{9,13},{10,... | collective-permute-start | bytes 393224 | tf_op jit(solution)/shard_map/ppermute | solution.py:438
  69.7 6.1 %collective-permute-start.25 = (bf16[16,4096]{1,0:T(8,128)(2,1)S(1)}, bf16[16,4096]{1,0:T(8,128)(2,1)S(1)}, u32[]{:S(2)}, u32[]{:S(2)}) collective-permute-start(bf16[16,4096]{1,0:T(8,128)(2,1)S(1)} %add.7.refs_0_), channel_id=1, source_target_pairs={{0,8},{1,9},{2,10},{3,11},{4,12},{5,13},{6,14},{7,15},{8,0},{9,1},... | collective-permute-start | bytes 393224 | tf_op jit(solution)/shard_map/ppermute | solution.py:438
  70.6 8.5 %collective-permute-start.26 = (bf16[16,4096]{1,0:T(8,128)(2,1)S(1)}, bf16[16,4096]{1,0:T(8,128)(2,1)S(1)}, u32[]{:S(2)}, u32[]{:S(2)}) collective-permute-start(bf16[16,4096]{1,0:T(8,128)(2,1)S(1)} %add.7.refs_0_), channel_id=1, source_target_pairs={{0,12},{1,13},{2,14},{3,15},{4,8},{5,9},{6,10},{7,11},{8,4},{9,5},... | collective-permute-start | bytes 393224 | tf_op jit(solution)/shard_map/ppermute | solution.py:438
  71.8 9.4 %collective-permute-start.31 = (bf16[16,4096]{1,0:T(8,128)(2,1)S(1)}, bf16[16,4096]{1,0:T(8,128)(2,1)S(1)}, u32[]{:S(2)}, u32[]{:S(2)}) collective-permute-start(bf16[16,4096]{1,0:T(8,128)(2,1)S(1)} %add.7.refs_0_), channel_id=1, source_target_pairs={{0,2},{1,3},{2,0},{3,1},{4,6},{5,7},{6,4},{7,5},{8,10},{9,11},{10,... | collective-permute-start | bytes 393224 | tf_op jit(solution)/shard_map/ppermute | solution.py:438
  73.4 12.1 %collective-permute-start.27 = (bf16[16,4096]{1,0:T(8,128)(2,1)S(1)}, bf16[16,4096]{1,0:T(8,128)(2,1)S(1)}, u32[]{:S(2)}, u32[]{:S(2)}) collective-permute-start(bf16[16,4096]{1,0:T(8,128)(2,1)S(1)} %add.7.refs_0_), channel_id=1, source_target_pairs={{0,1},{1,0},{2,3},{3,2},{4,5},{5,4},{6,7},{7,6},{8,9},{9,8},{10,11... | collective-permute-start | bytes 393224 | tf_op jit(solution)/shard_map/ppermute | solution.py:438
  75.4 10.2 %collective-permute-start.32 = (bf16[16,4096]{1,0:T(8,128)(2,1)S(1)}, bf16[16,4096]{1,0:T(8,128)(2,1)S(1)}, u32[]{:S(2)}, u32[]{:S(2)}) collective-permute-start(bf16[16,4096]{1,0:T(8,128)(2,1)S(1)} %collective-permute-done.24.refs_1_), channel_id=1, source_target_pairs={{0,2},{1,3},{2,0},{3,1},{4,6},{5,7},{6,4},{7,5},{8,10},{9,11},{10,... | collective-permute-start | bytes 393224 | tf_op jit(solution)/shard_map/ppermute | solution.py:438
  75.8 10.3 %collective-permute-start.33 = (bf16[16,4096]{1,0:T(8,128)(2,1)S(1)}, bf16[16,4096]{1,0:T(8,128)(2,1)S(1)}, u32[]{:S(2)}, u32[]{:S(2)}) collective-permute-start(bf16[16,4096]{1,0:T(8,128)(2,1)S(1)} %collective-permute-done.25.refs_2_), channel_id=1, source_target_pairs={{0,2},{1,3},{2,0},{3,1},{4,6},{5,7},{6,4},{7,5},{8,10},{9,11},{10,... | collective-permute-start | bytes 393224 | tf_op jit(solution)/shard_map/ppermute | solution.py:438
  79.1 9.4 %collective-permute-start.34 = (bf16[16,4096]{1,0:T(8,128)(2,1)S(1)}, bf16[16,4096]{1,0:T(8,128)(2,1)S(1)}, u32[]{:S(2)}, u32[]{:S(2)}) collective-permute-start(bf16[16,4096]{1,0:T(8,128)(2,1)S(1)} %collective-permute-done.26.refs_3_), channel_id=1, source_target_pairs={{0,2},{1,3},{2,0},{3,1},{4,6},{5,7},{6,4},{7,5},{8,10},{9,11},{10,... | collective-permute-start | bytes 393224 | tf_op jit(solution)/shard_map/ppermute | solution.py:438
  81.3 9.0 %collective-permute-start.28 = (bf16[16,4096]{1,0:T(8,128)(2,1)S(1)}, bf16[16,4096]{1,0:T(8,128)(2,1)S(1)}, u32[]{:S(2)}, u32[]{:S(2)}) collective-permute-start(bf16[16,4096]{1,0:T(8,128)(2,1)S(1)} %collective-permute-done.24.refs_1_), channel_id=1, source_target_pairs={{0,1},{1,0},{2,3},{3,2},{4,5},{5,4},{6,7},{7,6},{8,9},{9,8},{10,11... | collective-permute-start | bytes 393224 | tf_op jit(solution)/shard_map/ppermute | solution.py:438
  85.6 5.4 %collective-permute-start.30 = (bf16[16,4096]{1,0:T(8,128)(2,1)S(1)}, bf16[16,4096]{1,0:T(8,128)(2,1)S(1)}, u32[]{:S(2)}, u32[]{:S(2)}) collective-permute-start(bf16[16,4096]{1,0:T(8,128)(2,1)S(1)} %collective-permute-done.26.refs_3_), channel_id=1, source_target_pairs={{0,1},{1,0},{2,3},{3,2},{4,5},{5,4},{6,7},{7,6},{8,9},{9,8},{10,11... | collective-permute-start | bytes 393224 | tf_op jit(solution)/shard_map/ppermute | solution.py:438
  (12 other events, 61.4 us)

commit v5 on v4

--- a/solution.py
+++ b/solution.py
@@ -83,7 +83,7 @@
 
 
 def hidden_columns(
-    block, width, tok_ref, rot_ref, gu_refs, codes_of, qe_ref, hq_ref, mm_ref, full_first, arrived
+    block, width, tok_ref, rot_ref, gu_refs, codes_of, qe_ref, hq_ref, mm_ref, only, arrived
 ):
     depth = tok_ref.shape[1]
     groups = qe_ref.shape[1]
@@ -102,14 +102,19 @@
 
         return piece
 
-    if full_first:
+    if only != "quant":
+        if only:
+            arrived(block)
         full = swiglu(pieces, tok_ref, full_weight(0), full_weight(1))
-        arrived(block)
-    quant = swiglu(pieces, rot_ref, quant_weight(0), quant_weight(1))
-    if not full_first:
-        arrived(block)
-        full = swiglu(pieces, tok_ref, full_weight(0), full_weight(1))
-    hq_ref[:, cut] = quant
+    if only == "full":
+        quant = hq_ref[:, cut]
+    else:
+        if not only:
+            arrived(block)
+        quant = swiglu(pieces, rot_ref, quant_weight(0), quant_weight(1))
+        hq_ref[:, cut] = quant
+    if only == "quant":
+        return
     mm_ref[:, cut] = (full.astype(F32) - quant.astype(F32)).astype(BF16)
 
 
@@ -181,13 +186,15 @@
     sign = (1 - 2 * flip_ref[...]).astype(F32).astype(BF16)
     rotate_rows(blocks, sign, table_ref[...], tok_ref, mixed_ref, rot_ref)
 
-    @pl.loop(0, units // step)
-    def _(block):
-        hidden_columns(
-            block, step, tok_ref, rot_ref, gu_refs,
-            lambda i, k, rows, cut: qc_refs[i * len(qc_refs) // 2 + k][:, cut],
-            qe_ref, hq_ref, mm_ref, full_first=False, arrived=full_arrived,
-        )
+    for only in ("quant", "full"):
+
+        @pl.loop(0, units // step)
+        def _(block):
+            hidden_columns(
+                block, step, tok_ref, rot_ref, gu_refs,
+                lambda i, k, rows, cut: qc_refs[i * len(qc_refs) // 2 + k][:, cut],
+                qe_ref, hq_ref, mm_ref, only=only, arrived=full_arrived,
+            )
 
 
 def first_hidden(blocks, flip, table, gate_up, codes, exps):
@@ -235,10 +242,11 @@
         slot = lax.rem(block, slots)
         return pltpu.make_async_copy(qc_hbm.at[:, :, cut], qc_ref.at[slot], qc_sem.at[slot])
 
-    for block in range(slots):
-        codes(block).start()
+    codes(0).start()
     sign = (1 - 2 * flip_ref[...]).astype(F32).astype(BF16)
     rotate_rows(blocks, sign, table_ref[...], tok_ref, mixed_ref, rot_ref)
+    for block in range(1, slots):
+        codes(block).start()
 
     @pl.loop(0, units // step)
     def _(block):
@@ -246,7 +254,7 @@
         hidden_columns(
             block, step, tok_ref, rot_ref, gu_refs,
             lambda i, k, rows, cut: qc_ref[slot, i, rows, :],
-            qe_ref, hq_ref, mm_ref, full_first=True, arrived=lambda k: codes(k).wait(),
+            qe_ref, hq_ref, mm_ref, only=None, arrived=lambda k: codes(k).wait(),
         )
 
         @pl.when(block + slots < units // step)

time: 96.1 us -> 96 us (level)
  transfers between devices with their start and end apart: 39 -> 39, of which waited for: 12 -> 12; matrix products, arithmetic and copies ran while one was open for 0% -> 0% of each run, Pallas kernels for 17% -> 16%
where the time goes in v5:
time: 96 us; the launch traced here: 95.5 us
  starting transfers between devices  53.6 us (56%)
  Pallas kernels  28.4 us (30%)
  waiting for transfers between devices  12.3 us (13%)
    ppermute x30, starting transfers between devices, gather(): lax.ppermute(value, 'tok', shift(grid, axis, by))  44.5 us
    pallas_call x1, Pallas kernels, next_hidden(): pl.pallas_call(functools.partial(next_kernel, len(blocks)), in_specs=[spe...  9.25 us
    ppermute x9, starting transfers between devices, reduce_to_owner(): lax.ppermute(value, 'tok', shift(grid, axis, -by))  9.11 us
    ppermute x9, waiting for transfers between devices, reduce_to_owner(): lax.ppermute(value, 'tok', shift(grid, axis, -by))  8.89 us
    pallas_call x1, Pallas kernels, first_hidden(): pl.pallas_call(functools.partial(first_kernel, len(blocks)), in_specs=[sp...  7.55 us
    pallas_call x1, Pallas kernels, fetch(): pl.pallas_call(fetch_kernel, in_specs=[spec(pltpu.VMEM), spec(pltpu.HBM)]...  5.96 us
    pallas_call x1, Pallas kernels, gram(): pl.pallas_call(functools.partial(gram_kernel, 1.0 / rows ** 0.5), in_spec...  3.83 us
    ppermute x30, waiting for transfers between devices, gather(): lax.ppermute(value, 'tok', shift(grid, axis, by))  3.39 us
  transfers between devices with their start and end apart: 39, of which 12 were waited for; matrix products, arithmetic and copies ran while one was open for 0% of the time, Pallas kernels for 16%

profile of v5, /device:TPU:1, one launch (start us, length us, event | category | flops | bytes accessed | tf_op | source)
XLA Modules:
  0.0 95.5 jit_solution(9124407649964303748)
XLA Ops:
  0.0 2.1 %collective-permute-start = (bf16[16,4096]{1,0:T(8,128)(2,1)}, bf16[16,4096]{1,0:T(8,128)(2,1)S(1)}, u32[]{:S(2)}, u32[]{:S(2)}) collective-permute-start(bf16[16,4096]{1,0:T(8,128)(2,1)} %refs_0_.1), channel_id=1, source_target_pairs={{0,4},{1,5},{2,6},{3,7},{4,0},{5,1},{6,2},{7,3},{8,12},{9,13},{10,... | collective-permute-start | bytes 393224 | tf_op jit(solution)/shard_map/ppermute | solution.py:446
  2.1 2.3 %collective-permute-start.1 = (bf16[16,4096]{1,0:T(8,128)(2,1)}, bf16[16,4096]{1,0:T(8,128)(2,1)S(1)}, u32[]{:S(2)}, u32[]{:S(2)}) collective-permute-start(bf16[16,4096]{1,0:T(8,128)(2,1)} %refs_0_.1), channel_id=1, source_target_pairs={{0,8},{1,9},{2,10},{3,11},{4,12},{5,13},{6,14},{7,15},{8,0},{9,1},... | collective-permute-start | bytes 393224 | tf_op jit(solution)/shard_map/ppermute | solution.py:446
  4.4 1.2 %collective-permute-start.3 = (bf16[16,4096]{1,0:T(8,128)(2,1)}, bf16[16,4096]{1,0:T(8,128)(2,1)S(1)}, u32[]{:S(2)}, u32[]{:S(2)}) collective-permute-start(bf16[16,4096]{1,0:T(8,128)(2,1)} %refs_0_.1), channel_id=1, source_target_pairs={{0,1},{1,0},{2,3},{3,2},{4,5},{5,4},{6,7},{7,6},{8,9},{9,8},{10,11... | collective-permute-start | bytes 393224 | tf_op jit(solution)/shard_map/ppermute | solution.py:446
  5.7 1.5 %collective-permute-start.7 = (bf16[16,4096]{1,0:T(8,128)(2,1)}, bf16[16,4096]{1,0:T(8,128)(2,1)S(1)}, u32[]{:S(2)}, u32[]{:S(2)}) collective-permute-start(bf16[16,4096]{1,0:T(8,128)(2,1)} %refs_0_.1), channel_id=1, source_target_pairs={{0,2},{1,3},{2,0},{3,1},{4,6},{5,7},{6,4},{7,5},{8,10},{9,11},{10,... | collective-permute-start | bytes 393224 | tf_op jit(solution)/shard_map/ppermute | solution.py:446
  7.1 1.2 %collective-permute-start.4 = (bf16[16,4096]{1,0:T(8,128)(2,1)S(1)}, bf16[16,4096]{1,0:T(8,128)(2,1)S(1)}, u32[]{:S(2)}, u32[]{:S(2)}) collective-permute-start(bf16[16,4096]{1,0:T(8,128)(2,1)S(1)} %collective-permute-done._.refs_1_), channel_id=1, source_target_pairs={{0,1},{1,0},{2,3},{3,2},{4,5},{5,4},{6,7},{7,6},{8,9},{9,8},{10,11... | collective-permute-start | bytes 393224 | tf_op jit(solution)/shard_map/ppermute | solution.py:446
  8.4 7.8 %collective-permute-start.5 = (bf16[16,4096]{1,0:T(8,128)(2,1)S(1)}, bf16[16,4096]{1,0:T(8,128)(2,1)S(1)}, u32[]{:S(2)}, u32[]{:S(2)}) collective-permute-start(bf16[16,4096]{1,0:T(8,128)(2,1)S(1)} %collective-permute-done.1.refs_2_), channel_id=1, source_target_pairs={{0,1},{1,0},{2,3},{3,2},{4,5},{5,4},{6,7},{7,6},{8,9},{9,8},{10,11... | collective-permute-start | bytes 393224 | tf_op jit(solution)/shard_map/ppermute | solution.py:446
  16.2 1.2 %collective-permute-start.8 = (bf16[16,4096]{1,0:T(8,128)(2,1)S(1)}, bf16[16,4096]{1,0:T(8,128)(2,1)S(1)}, u32[]{:S(2)}, u32[]{:S(2)}) collective-permute-start(bf16[16,4096]{1,0:T(8,128)(2,1)S(1)} %collective-permute-done._.refs_1_), channel_id=1, source_target_pairs={{0,2},{1,3},{2,0},{3,1},{4,6},{5,7},{6,4},{7,5},{8,10},{9,11},{10,... | collective-permute-start | bytes 393224 | tf_op jit(solution)/shard_map/ppermute | solution.py:446
  17.6 1.2 %collective-permute-start.10 = (bf16[16,4096]{1,0:T(8,128)(2,1)S(1)}, bf16[16,4096]{1,0:T(8,128)(2,1)S(1)}, u32[]{:S(2)}, u32[]{:S(2)}) collective-permute-start(bf16[16,4096]{1,0:T(8,128)(2,1)S(1)} %collective-permute-done.2.refs_3_), channel_id=1, source_target_pairs={{0,2},{1,3},{2,0},{3,1},{4,6},{5,7},{6,4},{7,5},{8,10},{9,11},{10,... | collective-permute-start | bytes 393224 | tf_op jit(solution)/shard_map/ppermute | solution.py:446
  20.0 6.0 %fetch.1 = (bf16[1024,1024]{1,0:T(8,128)(2,1)S(1)}, bf16[1024,1024]{1,0:T(8,128)(2,1)S(1)}, bf16[1024,1024]{1,0:T(8,128)(2,1)S(1)}, bf16[1024,1024]{1,0:T(8,128)...) custom-call(bf16[16,4096]{1,0:T(8,128)(2,1)S(1)} %collective-permute, ...), custom_call_target="tpu_custom_call" | custom-call | bytes 33554432 | tf_op jit(solution)/shard_map/fetch/pallas_call | solution.py:140
  27.7 7.5 %first_hidden.1 = (bf16[128,1024]{1,0:T(8,128)(2,1)S(1)}, bf16[128,1024]{1,0:T(8,128)(2,1)S(1)}, bf16[4096,1024]{1,0:T(8,128)(2,1)S(1)}, bf16[4096,1024]{1,0:T(8,128)(2,1)S(1)}) custom-call(bf16[16,4096]{1,0:T(8,128)(2,1)S(1)} %copy-done.1, bf16[16,4096]{1,0:T(8,128)(2,1)S(1)} %collective-permute-done._.refs_1_, ...), custom_call_target="tpu_custom_call" | custom-call | flops 4294967296 | bytes 16777216 | tf_op jit(solution)/shard_map/first_hidden/pallas_call | solution.py:203
  36.2 9.3 %next_hidden.1 = (bf16[128,1024]{1,0:T(8,128)(2,1)S(1)}, f32[64,4096]{1,0:T(8,128)S(1)}, bf16[64,4096]{1,0:T(8,128)(2,1)S(1)}) custom-call(bf16[16,4096]{1,0:T(8,128)(2,1)S(1)} %collective-permute-done.7.refs_0_, bf16[16,4096]{1,0:T(8,128)(2,1)S(1)} %collective-permute-done.8.refs_1_, bf16[16,4096]{1,0:T(8,128)(2,1)S(1)} %collective-permute-done.9.refs_2_, ...), custom_call_target="tpu_custom_call" | custom-call | flops 5368709120 | bytes 16777216 | tf_op jit(solution)/shard_map/next_hidden/pallas_call | solution.py:273
  45.5 1.3 %last_project.1 = (f32[64,4096]{1,0:T(8,128)S(1)}, bf16[64,4096]{1,0:T(8,128)(2,1)S(1)}) custom-call(bf16[128,1024]{1,0:T(8,128)(2,1)S(1)} %get-tuple-element.38.mm_ref, bf16[1024,4096]{1,0:T(8,128)(2,1)S(1)} %bitcast.2), custom_call_target="tpu_custom_call" | custom-call | tf_op jit(solution)/shard_map/last_project/pallas_call | solution.py:303
  47.5 1.3 %collective-permute-start.22 = (bf16[16,4096]{1,0:T(8,128)(2,1)S(1)}, bf16[16,4096]{1,0:T(8,128)(2,1)S(1)}, u32[]{:S(2)}, u32[]{:S(2)}) collective-permute-start(bf16[16,4096]{1,0:T(8,128)(2,1)S(1)} %get-tuple-element.46), channel_id=1, source_target_pairs={{0,2},{1,3},{2,0},{3,1},{4,6},{5,7},{6,4},{7,5},{8,10},{9,11},{10,... | collective-permute-start | bytes 393224 | tf_op jit(solution)/shard_map/ppermute | solution.py:461
  49.0 1.3 %collective-permute-start.18 = (bf16[16,4096]{1,0:T(8,128)(2,1)S(1)}, bf16[16,4096]{1,0:T(8,128)(2,1)S(1)}, u32[]{:S(2)}, u32[]{:S(2)}) collective-permute-start(bf16[16,4096]{1,0:T(8,128)(2,1)S(1)} %get-tuple-element.44), channel_id=1, source_target_pairs={{0,2},{1,3},{2,0},{3,1},{4,6},{5,7},{6,4},{7,5},{8,10},{9,11},{10,... | collective-permute-start | bytes 393224 | tf_op jit(solution)/shard_map/ppermute | solution.py:461
  50.5 2.0 %collective-permute-done.22.refs_1_ = bf16[16,4096]{1,0:T(8,128)(2,1)S(1)} collective-permute-done((bf16[16,4096]{1,0:T(8,128)(2,1)S(1)}, bf16[16,4096]{1,0:T(8,128)(2,1)S(1)}, u32[]{:S(2)}, u32[]{:S(2)}) %collective-permute-start.22) | collective-permute-done | bytes 131104 | tf_op jit(solution)/shard_map/ppermute | solution.py:461
  52.5 1.2 %collective-permute-start.23 = (bf16[16,4096]{1,0:T(8,128)(2,1)S(1)}, bf16[16,4096]{1,0:T(8,128)(2,1)S(1)}, u32[]{:S(2)}, u32[]{:S(2)}) collective-permute-start(bf16[16,4096]{1,0:T(8,128)(2,1)S(1)} %add.6), channel_id=1, source_target_pairs={{0,4},{1,5},{2,6},{3,7},{4,0},{5,1},{6,2},{7,3},{8,12},{9,13},{10,... | collective-permute-start | bytes 393224 | tf_op jit(solution)/shard_map/ppermute | solution.py:461
  53.7 1.6 %collective-permute-done.20.refs_1_ = bf16[16,4096]{1,0:T(8,128)(2,1)S(1)} collective-permute-done((bf16[16,4096]{1,0:T(8,128)(2,1)S(1)}, bf16[16,4096]{1,0:T(8,128)(2,1)S(1)}, u32[]{:S(2)}, u32[]{:S(2)}) %collective-permute-start.20) | collective-permute-done | bytes 131104 | tf_op jit(solution)/shard_map/ppermute | solution.py:461
  55.3 2.2 %collective-permute-start.21 = (bf16[16,4096]{1,0:T(8,128)(2,1)S(1)}, bf16[16,4096]{1,0:T(8,128)(2,1)S(1)}, u32[]{:S(2)}, u32[]{:S(2)}) collective-permute-start(bf16[16,4096]{1,0:T(8,128)(2,1)S(1)} %add.5), channel_id=1, source_target_pairs={{0,8},{1,9},{2,10},{3,11},{4,12},{5,13},{6,14},{7,15},{8,0},{9,1},... | collective-permute-start | bytes 393224 | tf_op jit(solution)/shard_map/ppermute | solution.py:461
  58.1 2.1 %collective-permute-start.19 = (bf16[16,4096]{1,0:T(8,128)(2,1)S(1)}, bf16[16,4096]{1,0:T(8,128)(2,1)S(1)}, u32[]{:S(2)}, u32[]{:S(2)}) collective-permute-start(bf16[16,4096]{1,0:T(8,128)(2,1)S(1)} %add.4), channel_id=1, source_target_pairs={{0,12},{1,13},{2,14},{3,15},{4,8},{5,9},{6,10},{7,11},{8,4},{9,5},... | collective-permute-start | bytes 393224 | tf_op jit(solution)/shard_map/ppermute | solution.py:461
  60.9 4.0 %collective-permute-done.19.refs_2_ = bf16[16,4096]{1,0:T(8,128)(2,1)S(1)} collective-permute-done((bf16[16,4096]{1,0:T(8,128)(2,1)S(1)}, bf16[16,4096]{1,0:T(8,128)(2,1)S(1)}, u32[]{:S(2)}, u32[]{:S(2)}) %collective-permute-start.19) | collective-permute-done | bytes 131104 | tf_op jit(solution)/shard_map/ppermute | solution.py:461
  65.0 4.5 %collective-permute-start.24 = (bf16[16,4096]{1,0:T(8,128)(2,1)S(1)}, bf16[16,4096]{1,0:T(8,128)(2,1)S(1)}, u32[]{:S(2)}, u32[]{:S(2)}) collective-permute-start(bf16[16,4096]{1,0:T(8,128)(2,1)S(1)} %add.7.refs_0_), channel_id=1, source_target_pairs={{0,4},{1,5},{2,6},{3,7},{4,0},{5,1},{6,2},{7,3},{8,12},{9,13},{10,... | collective-permute-start | bytes 393224 | tf_op jit(solution)/shard_map/ppermute | solution.py:446
  69.6 0.9 collective-permute-start.25
  70.5 1.3 %collective-permute-start.26 = (bf16[16,4096]{1,0:T(8,128)(2,1)S(1)}, bf16[16,4096]{1,0:T(8,128)(2,1)S(1)}, u32[]{:S(2)}, u32[]{:S(2)}) collective-permute-start(bf16[16,4096]{1,0:T(8,128)(2,1)S(1)} %add.7.refs_0_), channel_id=1, source_target_pairs={{0,12},{1,13},{2,14},{3,15},{4,8},{5,9},{6,10},{7,11},{8,4},{9,5},... | collective-permute-start | bytes 393224 | tf_op jit(solution)/shard_map/ppermute | solution.py:446
  71.7 1.6 %collective-permute-start.31 = (bf16[16,4096]{1,0:T(8,128)(2,1)S(1)}, bf16[16,4096]{1,0:T(8,128)(2,1)S(1)}, u32[]{:S(2)}, u32[]{:S(2)}) collective-permute-start(bf16[16,4096]{1,0:T(8,128)(2,1)S(1)} %add.7.refs_0_), channel_id=1, source_target_pairs={{0,2},{1,3},{2,0},{3,1},{4,6},{5,7},{6,4},{7,5},{8,10},{9,11},{10,... | collective-permute-start | bytes 393224 | tf_op jit(solution)/shard_map/ppermute | solution.py:446
  73.3 1.9 %collective-permute-start.27 = (bf16[16,4096]{1,0:T(8,128)(2,1)S(1)}, bf16[16,4096]{1,0:T(8,128)(2,1)S(1)}, u32[]{:S(2)}, u32[]{:S(2)}) collective-permute-start(bf16[16,4096]{1,0:T(8,128)(2,1)S(1)} %add.7.refs_0_), channel_id=1, source_target_pairs={{0,1},{1,0},{2,3},{3,2},{4,5},{5,4},{6,7},{7,6},{8,9},{9,8},{10,11... | collective-permute-start | bytes 393224 | tf_op jit(solution)/shard_map/ppermute | solution.py:446
  75.7 1.0 %collective-permute-start.33 = (bf16[16,4096]{1,0:T(8,128)(2,1)S(1)}, bf16[16,4096]{1,0:T(8,128)(2,1)S(1)}, u32[]{:S(2)}, u32[]{:S(2)}) collective-permute-start(bf16[16,4096]{1,0:T(8,128)(2,1)S(1)} %collective-permute-done.25.refs_2_), channel_id=1, source_target_pairs={{0,2},{1,3},{2,0},{3,1},{4,6},{5,7},{6,4},{7,5},{8,10},{9,11},{10,... | collective-permute-start | bytes 393224 | tf_op jit(solution)/shard_map/ppermute | solution.py:446
  76.7 2.2 %collective-permute-done.26.refs_3_ = bf16[16,4096]{1,0:T(8,128)(2,1)S(1)} collective-permute-done((bf16[16,4096]{1,0:T(8,128)(2,1)S(1)}, bf16[16,4096]{1,0:T(8,128)(2,1)S(1)}, u32[]{:S(2)}, u32[]{:S(2)}) %collective-permute-start.26) | collective-permute-done | bytes 131104 | tf_op jit(solution)/shard_map/ppermute | solution.py:446
  79.0 2.2 %collective-permute-start.34 = (bf16[16,4096]{1,0:T(8,128)(2,1)S(1)}, bf16[16,4096]{1,0:T(8,128)(2,1)S(1)}, u32[]{:S(2)}, u32[]{:S(2)}) collective-permute-start(bf16[16,4096]{1,0:T(8,128)(2,1)S(1)} %collective-permute-done.26.refs_3_), channel_id=1, source_target_pairs={{0,2},{1,3},{2,0},{3,1},{4,6},{5,7},{6,4},{7,5},{8,10},{9,11},{10,... | collective-permute-start | bytes 393224 | tf_op jit(solution)/shard_map/ppermute | solution.py:446
  81.2 4.2 %collective-permute-start.28 = (bf16[16,4096]{1,0:T(8,128)(2,1)S(1)}, bf16[16,4096]{1,0:T(8,128)(2,1)S(1)}, u32[]{:S(2)}, u32[]{:S(2)}) collective-permute-start(bf16[16,4096]{1,0:T(8,128)(2,1)S(1)} %collective-permute-done.24.refs_1_), channel_id=1, source_target_pairs={{0,1},{1,0},{2,3},{3,2},{4,5},{5,4},{6,7},{7,6},{8,9},{9,8},{10,11... | collective-permute-start | bytes 393224 | tf_op jit(solution)/shard_map/ppermute | solution.py:446
  85.9 2.4 %collective-permute-start.35 = (bf16[16,4096]{1,0:T(8,128)(2,1)S(1)}, bf16[16,4096]{1,0:T(8,128)(2,1)S(1)}, u32[]{:S(2)}, u32[]{:S(2)}) collective-permute-start(bf16[16,4096]{1,0:T(8,128)(2,1)S(1)} %collective-permute-done.31.refs_8_), channel_id=1, source_target_pairs={{0,1},{1,0},{2,3},{3,2},{4,5},{5,4},{6,7},{7,6},{8,9},{9,8},{10,11... | collective-permute-start | bytes 393224 | tf_op jit(solution)/shard_map/ppermute | solution.py:446
  88.4 1.8 %collective-permute-start.36 = (bf16[16,4096]{1,0:T(8,128)(2,1)S(1)}, bf16[16,4096]{1,0:T(8,128)(2,1)S(1)}, u32[]{:S(2)}, u32[]{:S(2)}) collective-permute-start(bf16[16,4096]{1,0:T(8,128)(2,1)S(1)} %collective-permute-done.32.refs_9_), channel_id=1, source_target_pairs={{0,1},{1,0},{2,3},{3,2},{4,5},{5,4},{6,7},{7,6},{8,9},{9,8},{10,11... | collective-permute-start | bytes 393224 | tf_op jit(solution)/shard_map/ppermute | solution.py:446
  91.7 3.8 %gram.1 = bf16[1024,4096]{1,0:T(8,128)(2,1)} custom-call(bf16[1024,256]{1,0:T(8,128)(2,1)S(1)} %turn.1.turned_ref, bf16[16,4096]{1,0:T(8,128)(2,1)S(1)} %add.7.refs_0_, bf16[16,4096]{1,0:T(8,128)(2,1)S(1)} %collective-permute-done.24.refs_1_, bf16[16,4096]{1,0:T(8,128)(2,1)S(1)} %collective-permute-done.25.refs_2_, ...), custom_call_target="tpu_custom_call" | custom-call | tf_op jit(solution)/shard_map/gram/pallas_call | solution.py:394
  (69 shorter events, 9.1 us)
Async XLA Ops:
  0.0 7.1 %collective-permute-start = (bf16[16,4096]{1,0:T(8,128)(2,1)}, bf16[16,4096]{1,0:T(8,128)(2,1)S(1)}, u32[]{:S(2)}, u32[]{:S(2)}) collective-permute-start(bf16[16,4096]{1,0:T(8,128)(2,1)} %refs_0_.1), channel_id=1, source_target_pairs={{0,4},{1,5},{2,6},{3,7},{4,0},{5,1},{6,2},{7,3},{8,12},{9,13},{10,... | collective-permute-start | bytes 393224 | tf_op jit(solution)/shard_map/ppermute | solution.py:446
  2.1 6.2 %collective-permute-start.1 = (bf16[16,4096]{1,0:T(8,128)(2,1)}, bf16[16,4096]{1,0:T(8,128)(2,1)S(1)}, u32[]{:S(2)}, u32[]{:S(2)}) collective-permute-start(bf16[16,4096]{1,0:T(8,128)(2,1)} %refs_0_.1), channel_id=1, source_target_pairs={{0,8},{1,9},{2,10},{3,11},{4,12},{5,13},{6,14},{7,15},{8,0},{9,1},... | collective-permute-start | bytes 393224 | tf_op jit(solution)/shard_map/ppermute | solution.py:446
  4.4 11.7 %collective-permute-start.2 = (bf16[16,4096]{1,0:T(8,128)(2,1)}, bf16[16,4096]{1,0:T(8,128)(2,1)S(1)}, u32[]{:S(2)}, u32[]{:S(2)}) collective-permute-start(bf16[16,4096]{1,0:T(8,128)(2,1)} %refs_0_.1), channel_id=1, source_target_pairs={{0,12},{1,13},{2,14},{3,15},{4,8},{5,9},{6,10},{7,11},{8,4},{9,5},... | collective-permute-start | bytes 393224 | tf_op jit(solution)/shard_map/ppermute | solution.py:446
  4.4 13.0 %collective-permute-start.3 = (bf16[16,4096]{1,0:T(8,128)(2,1)}, bf16[16,4096]{1,0:T(8,128)(2,1)S(1)}, u32[]{:S(2)}, u32[]{:S(2)}) collective-permute-start(bf16[16,4096]{1,0:T(8,128)(2,1)} %refs_0_.1), channel_id=1, source_target_pairs={{0,1},{1,0},{2,3},{3,2},{4,5},{5,4},{6,7},{7,6},{8,9},{9,8},{10,11... | collective-permute-start | bytes 393224 | tf_op jit(solution)/shard_map/ppermute | solution.py:446
  5.7 12.0 %collective-permute-start.7 = (bf16[16,4096]{1,0:T(8,128)(2,1)}, bf16[16,4096]{1,0:T(8,128)(2,1)S(1)}, u32[]{:S(2)}, u32[]{:S(2)}) collective-permute-start(bf16[16,4096]{1,0:T(8,128)(2,1)} %refs_0_.1), channel_id=1, source_target_pairs={{0,2},{1,3},{2,0},{3,1},{4,6},{5,7},{6,4},{7,5},{8,10},{9,11},{10,... | collective-permute-start | bytes 393224 | tf_op jit(solution)/shard_map/ppermute | solution.py:446
  7.1 11.8 %collective-permute-start.4 = (bf16[16,4096]{1,0:T(8,128)(2,1)S(1)}, bf16[16,4096]{1,0:T(8,128)(2,1)S(1)}, u32[]{:S(2)}, u32[]{:S(2)}) collective-permute-start(bf16[16,4096]{1,0:T(8,128)(2,1)S(1)} %collective-permute-done._.refs_1_), channel_id=1, source_target_pairs={{0,1},{1,0},{2,3},{3,2},{4,5},{5,4},{6,7},{7,6},{8,9},{9,8},{10,11... | collective-permute-start | bytes 393224 | tf_op jit(solution)/shard_map/ppermute | solution.py:446
  8.4 17.6 %collective-permute-start.5 = (bf16[16,4096]{1,0:T(8,128)(2,1)S(1)}, bf16[16,4096]{1,0:T(8,128)(2,1)S(1)}, u32[]{:S(2)}, u32[]{:S(2)}) collective-permute-start(bf16[16,4096]{1,0:T(8,128)(2,1)S(1)} %collective-permute-done.1.refs_2_), channel_id=1, source_target_pairs={{0,1},{1,0},{2,3},{3,2},{4,5},{5,4},{6,7},{7,6},{8,9},{9,8},{10,11... | collective-permute-start | bytes 393224 | tf_op jit(solution)/shard_map/ppermute | solution.py:446
  16.2 9.9 %collective-permute-start.8 = (bf16[16,4096]{1,0:T(8,128)(2,1)S(1)}, bf16[16,4096]{1,0:T(8,128)(2,1)S(1)}, u32[]{:S(2)}, u32[]{:S(2)}) collective-permute-start(bf16[16,4096]{1,0:T(8,128)(2,1)S(1)} %collective-permute-done._.refs_1_), channel_id=1, source_target_pairs={{0,2},{1,3},{2,0},{3,1},{4,6},{5,7},{6,4},{7,5},{8,10},{9,11},{10,... | collective-permute-start | bytes 393224 | tf_op jit(solution)/shard_map/ppermute | solution.py:446
  17.4 9.2 %collective-permute-start.9 = (bf16[16,4096]{1,0:T(8,128)(2,1)S(1)}, bf16[16,4096]{1,0:T(8,128)(2,1)S(1)}, u32[]{:S(2)}, u32[]{:S(2)}) collective-permute-start(bf16[16,4096]{1,0:T(8,128)(2,1)S(1)} %collective-permute-done.1.refs_2_), channel_id=1, source_target_pairs={{0,2},{1,3},{2,0},{3,1},{4,6},{5,7},{6,4},{7,5},{8,10},{9,11},{10,... | collective-permute-start | bytes 393224 | tf_op jit(solution)/shard_map/ppermute | solution.py:446
  17.6 9.2 %collective-permute-start.10 = (bf16[16,4096]{1,0:T(8,128)(2,1)S(1)}, bf16[16,4096]{1,0:T(8,128)(2,1)S(1)}, u32[]{:S(2)}, u32[]{:S(2)}) collective-permute-start(bf16[16,4096]{1,0:T(8,128)(2,1)S(1)} %collective-permute-done.2.refs_3_), channel_id=1, source_target_pairs={{0,2},{1,3},{2,0},{3,1},{4,6},{5,7},{6,4},{7,5},{8,10},{9,11},{10,... | collective-permute-start | bytes 393224 | tf_op jit(solution)/shard_map/ppermute | solution.py:446
  18.9 8.8 %collective-permute-start.6 = (bf16[16,4096]{1,0:T(8,128)(2,1)S(1)}, bf16[16,4096]{1,0:T(8,128)(2,1)S(1)}, u32[]{:S(2)}, u32[]{:S(2)}) collective-permute-start(bf16[16,4096]{1,0:T(8,128)(2,1)S(1)} %collective-permute-done.2.refs_3_), channel_id=1, source_target_pairs={{0,1},{1,0},{2,3},{3,2},{4,5},{5,4},{6,7},{7,6},{8,9},{9,8},{10,11... | collective-permute-start | bytes 393224 | tf_op jit(solution)/shard_map/ppermute | solution.py:446
  26.0 9.3 %collective-permute-start.11 = (bf16[16,4096]{1,0:T(8,128)(2,1)S(1)}, bf16[16,4096]{1,0:T(8,128)(2,1)S(1)}, u32[]{:S(2)}, u32[]{:S(2)}) collective-permute-start(bf16[16,4096]{1,0:T(8,128)(2,1)S(1)} %collective-permute-done.7.refs_0_), channel_id=1, source_target_pairs={{0,1},{1,0},{2,3},{3,2},{4,5},{5,4},{6,7},{7,6},{8,9},{9,8},{10,11... | collective-permute-start | bytes 393224 | tf_op jit(solution)/shard_map/ppermute | solution.py:446
  26.1 9.2 %collective-permute-start.12 = (bf16[16,4096]{1,0:T(8,128)(2,1)S(1)}, bf16[16,4096]{1,0:T(8,128)(2,1)S(1)}, u32[]{:S(2)}, u32[]{:S(2)}) collective-permute-start(bf16[16,4096]{1,0:T(8,128)(2,1)S(1)} %collective-permute-done.8.refs_1_), channel_id=1, source_target_pairs={{0,1},{1,0},{2,3},{3,2},{4,5},{5,4},{6,7},{7,6},{8,9},{9,8},{10,11... | collective-permute-start | bytes 393224 | tf_op jit(solution)/shard_map/ppermute | solution.py:446
  26.6 8.7 %collective-permute-start.13 = (bf16[16,4096]{1,0:T(8,128)(2,1)S(1)}, bf16[16,4096]{1,0:T(8,128)(2,1)S(1)}, u32[]{:S(2)}, u32[]{:S(2)}) collective-permute-start(bf16[16,4096]{1,0:T(8,128)(2,1)S(1)} %collective-permute-done.9.refs_2_), channel_id=1, source_target_pairs={{0,1},{1,0},{2,3},{3,2},{4,5},{5,4},{6,7},{7,6},{8,9},{9,8},{10,11... | collective-permute-start | bytes 393224 | tf_op jit(solution)/shard_map/ppermute | solution.py:446
  26.8 8.5 %collective-permute-start.14 = (bf16[16,4096]{1,0:T(8,128)(2,1)S(1)}, bf16[16,4096]{1,0:T(8,128)(2,1)S(1)}, u32[]{:S(2)}, u32[]{:S(2)}) collective-permute-start(bf16[16,4096]{1,0:T(8,128)(2,1)S(1)} %collective-permute-done.10.refs_3_), channel_id=1, source_target_pairs={{0,1},{1,0},{2,3},{3,2},{4,5},{5,4},{6,7},{7,6},{8,9},{9,8},{10,11... | collective-permute-start | bytes 393224 | tf_op jit(solution)/shard_map/ppermute | solution.py:446
  47.5 5.0 %collective-permute-start.22 = (bf16[16,4096]{1,0:T(8,128)(2,1)S(1)}, bf16[16,4096]{1,0:T(8,128)(2,1)S(1)}, u32[]{:S(2)}, u32[]{:S(2)}) collective-permute-start(bf16[16,4096]{1,0:T(8,128)(2,1)S(1)} %get-tuple-element.46), channel_id=1, source_target_pairs={{0,2},{1,3},{2,0},{3,1},{4,6},{5,7},{6,4},{7,5},{8,10},{9,11},{10,... | collective-permute-start | bytes 393224 | tf_op jit(solution)/shard_map/ppermute | solution.py:461
  48.8 6.5 %collective-permute-start.20 = (bf16[16,4096]{1,0:T(8,128)(2,1)S(1)}, bf16[16,4096]{1,0:T(8,128)(2,1)S(1)}, u32[]{:S(2)}, u32[]{:S(2)}) collective-permute-start(bf16[16,4096]{1,0:T(8,128)(2,1)S(1)} %get-tuple-element.45), channel_id=1, source_target_pairs={{0,2},{1,3},{2,0},{3,1},{4,6},{5,7},{6,4},{7,5},{8,10},{9,11},{10,... | collective-permute-start | bytes 393224 | tf_op jit(solution)/shard_map/ppermute | solution.py:461
  49.0 9.1 %collective-permute-start.18 = (bf16[16,4096]{1,0:T(8,128)(2,1)S(1)}, bf16[16,4096]{1,0:T(8,128)(2,1)S(1)}, u32[]{:S(2)}, u32[]{:S(2)}) collective-permute-start(bf16[16,4096]{1,0:T(8,128)(2,1)S(1)} %get-tuple-element.44), channel_id=1, source_target_pairs={{0,2},{1,3},{2,0},{3,1},{4,6},{5,7},{6,4},{7,5},{8,10},{9,11},{10,... | collective-permute-start | bytes 393224 | tf_op jit(solution)/shard_map/ppermute | solution.py:461
  50.3 10.6 %collective-permute-start.17 = (bf16[16,4096]{1,0:T(8,128)(2,1)S(1)}, bf16[16,4096]{1,0:T(8,128)(2,1)S(1)}, u32[]{:S(2)}, u32[]{:S(2)}) collective-permute-start(bf16[16,4096]{1,0:T(8,128)(2,1)S(1)} %get-tuple-element.43), channel_id=1, source_target_pairs={{0,2},{1,3},{2,0},{3,1},{4,6},{5,7},{6,4},{7,5},{8,10},{9,11},{10,... | collective-permute-start | bytes 393224 | tf_op jit(solution)/shard_map/ppermute | solution.py:461
  52.5 8.4 %collective-permute-start.23 = (bf16[16,4096]{1,0:T(8,128)(2,1)S(1)}, bf16[16,4096]{1,0:T(8,128)(2,1)S(1)}, u32[]{:S(2)}, u32[]{:S(2)}) collective-permute-start(bf16[16,4096]{1,0:T(8,128)(2,1)S(1)} %add.6), channel_id=1, source_target_pairs={{0,4},{1,5},{2,6},{3,7},{4,0},{5,1},{6,2},{7,3},{8,12},{9,13},{10,... | collective-permute-start | bytes 393224 | tf_op jit(solution)/shard_map/ppermute | solution.py:461
  55.3 5.6 %collective-permute-start.21 = (bf16[16,4096]{1,0:T(8,128)(2,1)S(1)}, bf16[16,4096]{1,0:T(8,128)(2,1)S(1)}, u32[]{:S(2)}, u32[]{:S(2)}) collective-permute-start(bf16[16,4096]{1,0:T(8,128)(2,1)S(1)} %add.5), channel_id=1, source_target_pairs={{0,8},{1,9},{2,10},{3,11},{4,12},{5,13},{6,14},{7,15},{8,0},{9,1},... | collective-permute-start | bytes 393224 | tf_op jit(solution)/shard_map/ppermute | solution.py:461
  58.1 6.8 %collective-permute-start.19 = (bf16[16,4096]{1,0:T(8,128)(2,1)S(1)}, bf16[16,4096]{1,0:T(8,128)(2,1)S(1)}, u32[]{:S(2)}, u32[]{:S(2)}) collective-permute-start(bf16[16,4096]{1,0:T(8,128)(2,1)S(1)} %add.4), channel_id=1, source_target_pairs={{0,12},{1,13},{2,14},{3,15},{4,8},{5,9},{6,10},{7,11},{8,4},{9,5},... | collective-permute-start | bytes 393224 | tf_op jit(solution)/shard_map/ppermute | solution.py:461
  65.0 10.2 %collective-permute-start.24 = (bf16[16,4096]{1,0:T(8,128)(2,1)S(1)}, bf16[16,4096]{1,0:T(8,128)(2,1)S(1)}, u32[]{:S(2)}, u32[]{:S(2)}) collective-permute-start(bf16[16,4096]{1,0:T(8,128)(2,1)S(1)} %add.7.refs_0_), channel_id=1, source_target_pairs={{0,4},{1,5},{2,6},{3,7},{4,0},{5,1},{6,2},{7,3},{8,12},{9,13},{10,... | collective-permute-start | bytes 393224 | tf_op jit(solution)/shard_map/ppermute | solution.py:446
  69.6 6.1 %collective-permute-start.25 = (bf16[16,4096]{1,0:T(8,128)(2,1)S(1)}, bf16[16,4096]{1,0:T(8,128)(2,1)S(1)}, u32[]{:S(2)}, u32[]{:S(2)}) collective-permute-start(bf16[16,4096]{1,0:T(8,128)(2,1)S(1)} %add.7.refs_0_), channel_id=1, source_target_pairs={{0,8},{1,9},{2,10},{3,11},{4,12},{5,13},{6,14},{7,15},{8,0},{9,1},... | collective-permute-start | bytes 393224 | tf_op jit(solution)/shard_map/ppermute | solution.py:446
  70.5 8.5 %collective-permute-start.26 = (bf16[16,4096]{1,0:T(8,128)(2,1)S(1)}, bf16[16,4096]{1,0:T(8,128)(2,1)S(1)}, u32[]{:S(2)}, u32[]{:S(2)}) collective-permute-start(bf16[16,4096]{1,0:T(8,128)(2,1)S(1)} %add.7.refs_0_), channel_id=1, source_target_pairs={{0,12},{1,13},{2,14},{3,15},{4,8},{5,9},{6,10},{7,11},{8,4},{9,5},... | collective-permute-start | bytes 393224 | tf_op jit(solution)/shard_map/ppermute | solution.py:446
  71.7 9.5 %collective-permute-start.31 = (bf16[16,4096]{1,0:T(8,128)(2,1)S(1)}, bf16[16,4096]{1,0:T(8,128)(2,1)S(1)}, u32[]{:S(2)}, u32[]{:S(2)}) collective-permute-start(bf16[16,4096]{1,0:T(8,128)(2,1)S(1)} %add.7.refs_0_), channel_id=1, source_target_pairs={{0,2},{1,3},{2,0},{3,1},{4,6},{5,7},{6,4},{7,5},{8,10},{9,11},{10,... | collective-permute-start | bytes 393224 | tf_op jit(solution)/shard_map/ppermute | solution.py:446
  73.3 12.1 %collective-permute-start.27 = (bf16[16,4096]{1,0:T(8,128)(2,1)S(1)}, bf16[16,4096]{1,0:T(8,128)(2,1)S(1)}, u32[]{:S(2)}, u32[]{:S(2)}) collective-permute-start(bf16[16,4096]{1,0:T(8,128)(2,1)S(1)} %add.7.refs_0_), channel_id=1, source_target_pairs={{0,1},{1,0},{2,3},{3,2},{4,5},{5,4},{6,7},{7,6},{8,9},{9,8},{10,11... | collective-permute-start | bytes 393224 | tf_op jit(solution)/shard_map/ppermute | solution.py:446
  75.2 10.2 %collective-permute-start.32 = (bf16[16,4096]{1,0:T(8,128)(2,1)S(1)}, bf16[16,4096]{1,0:T(8,128)(2,1)S(1)}, u32[]{:S(2)}, u32[]{:S(2)}) collective-permute-start(bf16[16,4096]{1,0:T(8,128)(2,1)S(1)} %collective-permute-done.24.refs_1_), channel_id=1, source_target_pairs={{0,2},{1,3},{2,0},{3,1},{4,6},{5,7},{6,4},{7,5},{8,10},{9,11},{10,... | collective-permute-start | bytes 393224 | tf_op jit(solution)/shard_map/ppermute | solution.py:446
  75.7 10.2 %collective-permute-start.33 = (bf16[16,4096]{1,0:T(8,128)(2,1)S(1)}, bf16[16,4096]{1,0:T(8,128)(2,1)S(1)}, u32[]{:S(2)}, u32[]{:S(2)}) collective-permute-start(bf16[16,4096]{1,0:T(8,128)(2,1)S(1)} %collective-permute-done.25.refs_2_), channel_id=1, source_target_pairs={{0,2},{1,3},{2,0},{3,1},{4,6},{5,7},{6,4},{7,5},{8,10},{9,11},{10,... | collective-permute-start | bytes 393224 | tf_op jit(solution)/shard_map/ppermute | solution.py:446
  79.0 9.4 %collective-permute-start.34 = (bf16[16,4096]{1,0:T(8,128)(2,1)S(1)}, bf16[16,4096]{1,0:T(8,128)(2,1)S(1)}, u32[]{:S(2)}, u32[]{:S(2)}) collective-permute-start(bf16[16,4096]{1,0:T(8,128)(2,1)S(1)} %collective-permute-done.26.refs_3_), channel_id=1, source_target_pairs={{0,2},{1,3},{2,0},{3,1},{4,6},{5,7},{6,4},{7,5},{8,10},{9,11},{10,... | collective-permute-start | bytes 393224 | tf_op jit(solution)/shard_map/ppermute | solution.py:446
  81.2 9.0 %collective-permute-start.28 = (bf16[16,4096]{1,0:T(8,128)(2,1)S(1)}, bf16[16,4096]{1,0:T(8,128)(2,1)S(1)}, u32[]{:S(2)}, u32[]{:S(2)}) collective-permute-start(bf16[16,4096]{1,0:T(8,128)(2,1)S(1)} %collective-permute-done.24.refs_1_), channel_id=1, source_target_pairs={{0,1},{1,0},{2,3},{3,2},{4,5},{5,4},{6,7},{7,6},{8,9},{9,8},{10,11... | collective-permute-start | bytes 393224 | tf_op jit(solution)/shard_map/ppermute | solution.py:446
  85.5 5.4 %collective-permute-start.30 = (bf16[16,4096]{1,0:T(8,128)(2,1)S(1)}, bf16[16,4096]{1,0:T(8,128)(2,1)S(1)}, u32[]{:S(2)}, u32[]{:S(2)}) collective-permute-start(bf16[16,4096]{1,0:T(8,128)(2,1)S(1)} %collective-permute-done.26.refs_3_), channel_id=1, source_target_pairs={{0,1},{1,0},{2,3},{3,2},{4,5},{5,4},{6,7},{7,6},{8,9},{9,8},{10,11... | collective-permute-start | bytes 393224 | tf_op jit(solution)/shard_map/ppermute | solution.py:446
  (12 other events, 60.3 us)
